TPU v7x, 32 devices: a whole 2x2x4 slice. The times are simulated.
32 devices in a mesh: dp: 8 (over z, x), fsdp: 4 (over y, core).
Axes of the slice: x: 2, y: 2, z: 4, core: 2. Of those that a mesh axis runs over, the one named last changes fastest.
Arguments:
- hidden: bfloat16 [16, 1024, 896], P('dp', 'fsdp'), may hold values from -20 to 20
- neighbours: bfloat16 [16, 16, 256, 896], P('dp', 'fsdp'), may hold values from -5 to 5
- piece_starts: int32 [16, 2], P('dp'), may hold values from 0 to 768, as said below
- out_grad: bfloat16 [16, 1024, 896], P('dp', 'fsdp'), may hold values from -5 to 5
- attn_weights: bfloat16 [7168, 896], P(('dp', 'fsdp')), may hold values from -2 to 2
- ffw_weights: bfloat16 [7168, 896], P(('dp', 'fsdp')), may hold values from -0.1875 to 0.1875
- vectors: bfloat16 [7168], P(('dp', 'fsdp')), may hold values from -2 to 2
- rel_table: float32 [32, 14], replicated, may hold values from -4 to 4
Outputs:
- out: bfloat16 [16, 1024, 896], P('dp', 'fsdp')
- hidden_grad: float32 [16, 1024, 896], P('dp', 'fsdp')
- neighbour_grad: float32 [16, 16, 256, 896], P('dp', 'fsdp')
- attn_grad: float32 [7168, 896], P(('dp', 'fsdp'))
- ffw_grad: float32 [7168, 896], P(('dp', 'fsdp'))
- vectors_grad: float32 [7168], P(('dp', 'fsdp'))
- table_grad: float32 [32, 14], replicated
Inputs may be any that keep to these rules, and one draw needn't show every extreme that they name: `piece_starts`: piece j of a sequence starts between j * 512 and (j + 1) * 512 - 256, so pieces do not intersect.
All inputs are finite; a program needn't handle non-finite values.
Results may differ from a plain program's by a relative error of at most 0.02.
Values may be sent and summed in bfloat16 or wider, within the bound.
A program may use at most 512 MiB of HBM per device.

v0:
```python
import jax
import jax.numpy as jnp
from jax import lax
from jax.sharding import PartitionSpec as P

FF = 3584
SPAN = 64
PIECE = 256


relative_bucket_limits = (1, 2, 3, 4, 5, 6, 7, 8, 12, 16, 24, 32, 64, 128, 256)
norm_eps = 1e-06
gelu_scale = 0.7978845608028654
gelu_cubic = 0.044715
masked_score = -1e30


def from_behind(array, axis, by):
    length = lax.axis_size(axis)
    pairs = [(i, i + by) for i in range(length) if 0 <= i + by < length]
    return lax.ppermute(array, axis, pairs)


def product(left_side, right_side):
    return jnp.dot(left_side, right_side, preferred_element_type=jnp.float32)


def times_transposed(left_side, right_side):
    return lax.dot_general(
        left_side, right_side, (((1,), (1,)), ((), ())), preferred_element_type=jnp.float32
    )


def transposed_times(left_side, right_side):
    return lax.dot_general(
        left_side, right_side, (((0,), (0,)), ((), ())), preferred_element_type=jnp.float32
    )


def inverse_rms(residual):
    return lax.rsqrt(jnp.mean(residual * residual, axis=-1, keepdims=True) + norm_eps)


def norm_back(residual, scale, gain, incoming):
    weighted = gain * incoming
    return scale * weighted - residual * scale * scale * scale * jnp.mean(
        residual * weighted, axis=-1, keepdims=True
    )


def gelu_parts(values):
    tangent = jnp.tanh(gelu_scale * (values + gelu_cubic * values * values * values))
    result = 0.5 * values * (1.0 + tangent)
    slope = 0.5 * (1.0 + tangent) + 0.5 * values * (1.0 - tangent * tangent) * gelu_scale * (
        1.0 + 3.0 * gelu_cubic * values * values
    )
    return (result, slope)


def split_three(values):
    upper = values.astype(jnp.bfloat16)
    remainder = values - upper.astype(jnp.float32)
    middle = remainder.astype(jnp.bfloat16)
    least = (remainder - middle.astype(jnp.float32)).astype(jnp.bfloat16)
    return (upper, middle, least)


def rel_buckets(query_pos, key_pos):
    offset = key_pos[None, :] - query_pos[:, None]
    magnitude = jnp.abs(offset)
    counted = jnp.zeros(offset.shape, jnp.int32)
    for threshold in relative_bucket_limits:
        counted = counted + (magnitude >= threshold).astype(jnp.int32)
    return counted + (offset > 0).astype(jnp.int32) * (len(relative_bucket_limits) + 1)


def piece_labels(positions, starts_row):
    inside = (positions[:, None] >= starts_row[None, :]) & (
        positions[:, None] < starts_row[None, :] + PIECE
    )
    labels = jnp.arange(1, starts_row.shape[0] + 1, dtype=jnp.int32)
    return jnp.sum(jnp.where(inside, labels[None, :], 0), axis=1)


def visible(query_pos, key_pos, query_piece, key_piece):
    causal = key_pos[None, :] <= query_pos[:, None]
    shared = (query_piece[:, None] == key_piece[None, :]) & (query_piece[:, None] > 0)
    return causal | shared


def fetch_weights(attn_part, ffw_part, vector_part):
    return (
        lax.all_gather(attn_part, ("dp", "fsdp"), axis=0, tiled=True),
        lax.all_gather(ffw_part, ("dp", "fsdp"), axis=0, tiled=True),
        lax.all_gather(vector_part, ("dp", "fsdp"), axis=0, tiled=True),
    )


def unpack(gathered, model_width):
    attn_full, ffw_full, vector_full = gathered
    matrices = attn_full.reshape(8, model_width, model_width)
    units = ffw_full.shape[0] // 2
    vector_float = vector_full.astype(jnp.float32)
    gain_rows = vector_float[units : units + 3 * model_width].reshape(3, model_width)
    return (
        matrices,
        ffw_full[:units],
        ffw_full[units:],
        vector_float[:units],
        gain_rows,
        vector_float[units + 3 * model_width :],
    )


def per_device(
    hidden, neighbours, piece_starts, out_grad, attn_weights, ffw_weights, vectors, rel_table
):
    micro_count, local_rows, model_width = hidden.shape
    group_size = lax.axis_size("fsdp")
    seq_length = local_rows * group_size
    head_count = rel_table.shape[1]
    head_size = model_width // head_count
    bucket_count = rel_table.shape[0]
    local_spans = neighbours.shape[1]
    span_keys = neighbours.shape[2]
    carried_rows = SPAN - 1
    kept_rows = local_rows - carried_rows
    query_pos = lax.axis_index("fsdp") * local_rows + jnp.arange(local_rows, dtype=jnp.int32)
    key_pos = jnp.arange(seq_length, dtype=jnp.int32)
    bucket_ids = rel_buckets(query_pos, key_pos)
    bucket_indicator = (
        bucket_ids[None, :, :] == jnp.arange(bucket_count, dtype=jnp.int32)[:, None, None]
    ).astype(jnp.bfloat16)
    rel_bias = jnp.zeros((head_count, local_rows, seq_length), jnp.float32)
    for partial_bias_table in split_three(rel_table):
        rel_bias = rel_bias + jnp.einsum(
            "jap,jv->vap", bucket_indicator, partial_bias_table, preferred_element_type=jnp.float32
        )

    def micro_step(totals, batch_item):
        tokens_low, near_tokens, starts_row, cotangent = batch_item
        weights_ahead = fetch_weights(attn_weights, ffw_weights, vectors)
        matrices, w_input, w_output, bias_input, gain_rows, bias_output = unpack(
            weights_ahead, model_width
        )
        residual = tokens_low.astype(jnp.float32)
        scale_one = inverse_rms(residual)
        normed_one = (residual * scale_one * gain_rows[0]).astype(jnp.bfloat16)
        queries = product(normed_one, matrices[0]).astype(jnp.bfloat16)
        keys_here = product(normed_one, matrices[1]).astype(jnp.bfloat16)
        values_here = product(normed_one, matrices[2]).astype(jnp.bfloat16)
        keys_all, values_all = (
            lax.all_gather(keys_here, "fsdp", axis=0, tiled=True),
            lax.all_gather(values_here, "fsdp", axis=0, tiled=True),
        )
        query_heads = queries.reshape(local_rows, head_count, head_size)
        key_heads = keys_all.reshape(seq_length, head_count, head_size)
        value_heads = values_all.reshape(seq_length, head_count, head_size)
        allowed = visible(
            query_pos,
            key_pos,
            piece_labels(query_pos, starts_row),
            piece_labels(key_pos, starts_row),
        )

        def self_scores():
            raw_scores = jnp.einsum(
                "qhd,khd->hqk", query_heads, key_heads, preferred_element_type=jnp.float32
            )
            return jnp.where(allowed[None], raw_scores * 0.125 + rel_bias, masked_score)

        scores_fwd = self_scores()
        row_top = jnp.max(scores_fwd, axis=-1, keepdims=True)
        exp_scores = jnp.exp(scores_fwd - row_top)
        row_total = jnp.sum(exp_scores, axis=-1, keepdims=True)
        self_weights = (exp_scores / row_total).astype(jnp.bfloat16)
        self_lse = row_top + jnp.log(row_total)
        context = (
            jnp.einsum(
                "hqk,khd->qhd", self_weights, value_heads, preferred_element_type=jnp.float32
            )
            .reshape(local_rows, model_width)
            .astype(jnp.bfloat16)
        )
        first_sum = residual + product(context, matrices[3])
        scale_two = inverse_rms(first_sum)
        normed_two = (first_sum * scale_two * gain_rows[1]).astype(jnp.bfloat16)
        cross_queries = product(normed_two, matrices[4]).astype(jnp.bfloat16)
        near_flat = near_tokens.reshape(local_spans * span_keys, model_width)
        cross_keys = product(near_flat, matrices[5]).astype(jnp.bfloat16)
        cross_values = product(near_flat, matrices[6]).astype(jnp.bfloat16)
        incoming = from_behind(cross_queries[:carried_rows], "fsdp", -1)
        block_queries = jnp.concatenate([cross_queries[carried_rows:], incoming], axis=0).reshape(
            local_spans, SPAN, head_count, head_size
        )
        block_keys = cross_keys.reshape(local_spans, span_keys, head_count, head_size)
        block_values = cross_values.reshape(local_spans, span_keys, head_count, head_size)

        def cross_scores():
            return (
                jnp.einsum(
                    "cqhd,ckhd->chqk", block_queries, block_keys, preferred_element_type=jnp.float32
                )
                * 0.125
            )

        cross_fwd = cross_scores()
        cross_top = jnp.max(cross_fwd, axis=-1, keepdims=True)
        cross_exp = jnp.exp(cross_fwd - cross_top)
        cross_total = jnp.sum(cross_exp, axis=-1, keepdims=True)
        cross_weights = (cross_exp / cross_total).astype(jnp.bfloat16)
        cross_lse = cross_top + jnp.log(cross_total)
        block_context = (
            jnp.einsum(
                "chqk,ckhd->cqhd", cross_weights, block_values, preferred_element_type=jnp.float32
            )
            .reshape(local_rows, model_width)
            .astype(jnp.bfloat16)
        )
        arriving = from_behind(block_context[kept_rows:], "fsdp", 1)
        placed = jnp.concatenate([arriving, block_context[:kept_rows]], axis=0)
        second_sum = first_sum + product(placed, matrices[7])
        scale_three = inverse_rms(second_sum)
        third_normalized = (second_sum * scale_three * gain_rows[2]).astype(jnp.bfloat16)
        pre_act = times_transposed(third_normalized, w_input) + bias_input
        act_value, act_slope = gelu_parts(pre_act)
        activated = act_value.astype(jnp.bfloat16)
        output_sum = second_sum + product(activated, w_output) + bias_output
        refreshed = lax.optimization_barrier((attn_weights, ffw_weights, vectors, output_sum))
        weights_behind = unpack(
            fetch_weights(refreshed[0], refreshed[1], refreshed[2]), model_width
        )
        back_mats, back_w_input, back_w_output, unused_bias, back_gains, unused_out = weights_behind
        grad_out = cotangent.astype(jnp.float32)
        grad_bias_output = jnp.sum(grad_out, axis=0)
        grad_out_low = grad_out.astype(jnp.bfloat16)
        grad_w_output = transposed_times(activated, grad_out_low)
        grad_act = times_transposed(grad_out_low, back_w_output)
        grad_pre = grad_act * act_slope
        grad_bias_input = jnp.sum(grad_pre, axis=0)
        grad_pre_low = grad_pre.astype(jnp.bfloat16)
        grad_w_input = transposed_times(grad_pre_low, third_normalized)
        grad_norm_three = product(grad_pre_low, back_w_input)
        grad_gain_three = jnp.sum(grad_norm_three * second_sum * scale_three, axis=0)
        grad_second = grad_out + norm_back(second_sum, scale_three, back_gains[2], grad_norm_three)
        grad_second_low = grad_second.astype(jnp.bfloat16)
        grad_cross_out = transposed_times(placed, grad_second_low)
        grad_placed = times_transposed(grad_second_low, back_mats[7]).astype(jnp.bfloat16)
        returning = from_behind(grad_placed[:carried_rows], "fsdp", -1)
        grad_block_context = jnp.concatenate(
            [grad_placed[carried_rows:], returning], axis=0
        ).reshape(local_spans, SPAN, head_count, head_size)
        cross_attention_probabilities = jnp.exp(cross_scores() - cross_lse)
        cross_probs_low = cross_attention_probabilities.astype(jnp.bfloat16)
        grad_cross_w = jnp.einsum(
            "cqhd,ckhd->chqk", grad_block_context, block_values, preferred_element_type=jnp.float32
        )
        grad_cross_values = (
            jnp.einsum(
                "chqk,cqhd->ckhd",
                cross_probs_low,
                grad_block_context,
                preferred_element_type=jnp.float32,
            )
            .reshape(local_spans * span_keys, model_width)
            .astype(jnp.bfloat16)
        )
        grad_cross_scores = cross_attention_probabilities * (
            grad_cross_w
            - jnp.sum(cross_attention_probabilities * grad_cross_w, axis=-1, keepdims=True)
        )
        grad_cross_low = (grad_cross_scores * 0.125).astype(jnp.bfloat16)
        grad_block_queries = (
            jnp.einsum(
                "chqk,ckhd->cqhd", grad_cross_low, block_keys, preferred_element_type=jnp.float32
            )
            .reshape(local_rows, model_width)
            .astype(jnp.bfloat16)
        )
        grad_cross_keys = (
            jnp.einsum(
                "chqk,cqhd->ckhd", grad_cross_low, block_queries, preferred_element_type=jnp.float32
            )
            .reshape(local_spans * span_keys, model_width)
            .astype(jnp.bfloat16)
        )
        handed_back = from_behind(grad_block_queries[kept_rows:], "fsdp", 1)
        grad_cross_queries = jnp.concatenate([handed_back, grad_block_queries[:kept_rows]], axis=0)
        grad_cross_query_mat = transposed_times(normed_two, grad_cross_queries)
        grad_cross_key_mat = transposed_times(near_flat, grad_cross_keys)
        grad_cross_value_mat = transposed_times(near_flat, grad_cross_values)
        near_grad = times_transposed(grad_cross_keys, back_mats[5]) + times_transposed(
            grad_cross_values, back_mats[6]
        )
        grad_norm_two = times_transposed(grad_cross_queries, back_mats[4])
        grad_gain_two = jnp.sum(grad_norm_two * first_sum * scale_two, axis=0)
        grad_first = grad_second + norm_back(first_sum, scale_two, back_gains[1], grad_norm_two)
        grad_first_low = grad_first.astype(jnp.bfloat16)
        grad_self_out = transposed_times(context, grad_first_low)
        grad_context = (
            times_transposed(grad_first_low, back_mats[3])
            .astype(jnp.bfloat16)
            .reshape(local_rows, head_count, head_size)
        )
        self_probs = jnp.exp(self_scores() - self_lse)
        self_probs_low = self_probs.astype(jnp.bfloat16)
        grad_self_w = jnp.einsum(
            "qhd,khd->hqk", grad_context, value_heads, preferred_element_type=jnp.float32
        )
        grad_values_all = jnp.einsum(
            "hqk,qhd->khd", self_probs_low, grad_context, preferred_element_type=jnp.float32
        ).reshape(seq_length, model_width)
        grad_self_scores = self_probs * (
            grad_self_w - jnp.sum(self_probs * grad_self_w, axis=-1, keepdims=True)
        )
        table_step = jnp.zeros((bucket_count, head_count), jnp.float32)
        for partial_scores in split_three(grad_self_scores):
            table_step = table_step + jnp.einsum(
                "tfw,efw->et", partial_scores, bucket_indicator, preferred_element_type=jnp.float32
            )
        grad_self_low = (grad_self_scores * 0.125).astype(jnp.bfloat16)
        grad_queries = (
            jnp.einsum("hqk,khd->qhd", grad_self_low, key_heads, preferred_element_type=jnp.float32)
            .reshape(local_rows, model_width)
            .astype(jnp.bfloat16)
        )
        grad_keys_all = jnp.einsum(
            "hqk,qhd->khd", grad_self_low, query_heads, preferred_element_type=jnp.float32
        ).reshape(seq_length, model_width)
        grad_keys_sum, grad_values_sum = (
            lax.psum_scatter(grad_keys_all, "fsdp", scatter_dimension=0, tiled=True),
            lax.psum_scatter(grad_values_all, "fsdp", scatter_dimension=0, tiled=True),
        )
        grad_keys_low = grad_keys_sum.astype(jnp.bfloat16)
        grad_values_low = grad_values_sum.astype(jnp.bfloat16)
        grad_query_mat = transposed_times(normed_one, grad_queries)
        grad_key_mat = transposed_times(normed_one, grad_keys_low)
        value_matrix_gradient = transposed_times(normed_one, grad_values_low)
        grad_norm_one = (
            times_transposed(grad_queries, back_mats[0])
            + times_transposed(grad_keys_low, back_mats[1])
            + times_transposed(grad_values_low, back_mats[2])
        )
        grad_gain_one = jnp.sum(grad_norm_one * residual * scale_one, axis=0)
        hidden_step = grad_first + norm_back(residual, scale_one, back_gains[0], grad_norm_one)
        matrix_step = jnp.stack(
            [
                grad_query_mat,
                grad_key_mat,
                value_matrix_gradient,
                grad_self_out,
                grad_cross_query_mat,
                grad_cross_key_mat,
                grad_cross_value_mat,
                grad_cross_out,
            ]
        )
        ffw_step = jnp.stack([grad_w_input, grad_w_output])
        vector_step = jnp.concatenate(
            [grad_bias_input, grad_gain_one, grad_gain_two, grad_gain_three, grad_bias_output]
        )
        new_totals = (
            totals[0] + matrix_step,
            totals[1] + ffw_step,
            totals[2] + vector_step,
            totals[3] + table_step,
        )
        return (
            new_totals,
            (
                output_sum.astype(jnp.bfloat16),
                hidden_step,
                near_grad.reshape(local_spans, span_keys, model_width),
            ),
        )

    zero_totals = (
        jnp.zeros((8, model_width, model_width), jnp.float32),
        jnp.zeros((2, FF, model_width), jnp.float32),
        jnp.zeros((FF + 4 * model_width,), jnp.float32),
        jnp.zeros((bucket_count, head_count), jnp.float32),
    )
    totals, stacked = lax.scan(
        micro_step, zero_totals, (hidden, neighbours, piece_starts, out_grad)
    )
    attn_sum, ffw_sum, vector_sum = (
        lax.psum_scatter(
            totals[0].reshape(8 * model_width, model_width),
            ("dp", "fsdp"),
            scatter_dimension=0,
            tiled=True,
        ),
        lax.psum_scatter(
            totals[1].reshape(2 * FF, model_width), ("dp", "fsdp"), scatter_dimension=0, tiled=True
        ),
        lax.psum_scatter(totals[2], ("dp", "fsdp"), scatter_dimension=0, tiled=True),
    )
    table_sum = lax.psum(totals[3], ("dp", "fsdp"))
    return (stacked[0], stacked[1], stacked[2], attn_sum, ffw_sum, vector_sum, table_sum)


def solution(mesh):
    placed = (
        P("dp", "fsdp", None),
        P("dp", "fsdp", None, None),
        P("dp", None),
        P("dp", "fsdp", None),
        P(("dp", "fsdp"), None),
        P(("dp", "fsdp"), None),
        P(("dp", "fsdp")),
        P(),
    )
    return jax.shard_map(
        per_device,
        mesh=mesh,
        in_specs=placed,
        out_specs=(
            P("dp", "fsdp", None),
            P("dp", "fsdp", None),
            P("dp", "fsdp", None, None),
            P(("dp", "fsdp"), None),
            P(("dp", "fsdp"), None),
            P(("dp", "fsdp")),
            P(),
        ),
        check_vma=False,
    )
```

profile of v0, /device:TPU:0, one launch (start us, length us, event | category | flops | bytes accessed | tf_op | source)
XLA Modules:
  0.0 2070.9 jit_solution(12714397518656481928)
XLA Ops:
  27.5 20.4 fusion.258
  47.9 19.5 copy.106
  67.4 1437.2 %while.24 = (s32[]{:T(128)}, f32[8,896,896]{2,1,0:T(8,128)}, f32[2,3584,896]{2,1,0:T(8,128)}, f32[7168]{0:T(1024)}, f32[32,14]{0,1:T(8,128)}, /*index=5*/bf16[2,...) while((s32[]{:T(128)}, f32[8,896,896]{2,1,0:T(8,128)}, ...), condition=%wide.region_22.23_spmd.clone.clone, body=%wide.region_0.22_spmd.clone.clone.sunk | while | flops 32108781568 | bytes 1149200640 | solution.py:383
  68.5 42.7 %all-reduce.8 = bf16[7168]{0:T(1024)(128)(2,1)S(1)} all-reduce(bf16[7168]{0:T(1024)(128)(2,1)S(1)} %dynamic-update-slice.58), channel_id=1, replica_groups=mesh['dp'=8,'fsdp'=4] {'dp','fsdp'}, use_global_device_ids=true, to_apply=%add | all-reduce | flops 7168 | bytes 28672 | tf_op jit(solution)/shard_map/while
  111.5 60.9 %all-gather.7.cloned.1.call-done = bf16[7168,896]{1,0:T(8,128)(2,1)} async-done(((bf16[224,896]{1,0:T(8,128)(2,1)}), bf16[7168,896]{1,0:T(8,128)(2,1)}) %all-gather.7.cloned.1.call-update) | async-done | bytes 12845072 | tf_op jit(solution)/shard_map/while/body/eval_jaxpr/all_gather | solution.py:93
  331.7 40.1 %all-reduce.9 = bf16[7168]{0:T(1024)(128)(2,1)S(1)} all-reduce(bf16[7168]{0:T(1024)(128)(2,1)S(1)} %dynamic-update-slice.59), channel_id=1, replica_groups=mesh['dp'=8,'fsdp'=4] {'dp','fsdp'}, use_global_device_ids=true, to_apply=%add.1 | all-reduce | flops 7168 | bytes 28672 | tf_op jit(solution)/shard_map/while
  372.4 55.2 %all-gather.17.cloned.1.call-done = bf16[7168,896]{1,0:T(8,128)(2,1)} async-done(((bf16[224,896]{1,0:T(8,128)(2,1)}), bf16[7168,896]{1,0:T(8,128)(2,1)}) %all-gather.17.cloned.1.call-update) | async-done | bytes 12845072 | tf_op jit(solution)/shard_map/while/body/eval_jaxpr/all_gather | solution.py:94
  440.4 85.5 %all-gather.15.cloned.1.call-done = bf16[7168,896]{1,0:T(8,128)(2,1)} async-done(((bf16[224,896]{1,0:T(8,128)(2,1)}), bf16[7168,896]{1,0:T(8,128)(2,1)}) %all-gather.15.cloned.1.call-update) | async-done | bytes 12845072 | tf_op jit(solution)/shard_map/while/body/eval_jaxpr/all_gather | solution.py:93
  540.3 27.1 %fusion.514 = bf16[4,64,14,64]{1,3,2,0:T(8,128)(2,1)} fusion(bf16[4,256,14,64]{1,3,2,0:T(8,128)(2,1)} %copy.162, f32[4,14,64,256]{3,2,1,0:T(8,128)} %fusion.513, f32[4,14,64,256]{3,2,1,0:T(8,128)} %copy-done, f32[4,14,64]{2,1,0:T(8,128)S(1)} %log_add_fusion.5), kind=kOutput, calls=%fused_computation.122.clone.1 | convolution fusion | flops 125931264 | bytes 9648128 | tf_op jit(solution)/shard_map/while/body/eval_jaxpr/chqk,ckhd->cqhd/dot_general | solution.py:274
  587.6 23.4 %subtract_convert_fusion.3 = (bf16[14,256,1024]{2,1,0:T(8,128)(2,1)}, bf16[14,256,1024]{2,1,0:T(8,128)(2,1)}, bf16[14,256,1024]{2,1,0:T(8,128)(2,1)}, f32[14,256,1024]{2,1,0:T(8,128)}) fusion(f32[14,256,1024]{2,1,0:T(8,128)} %get-tuple-element.539, f32[14,256]{1,0:T(8,128)S(1)} %log_add_fusion.4, bf16[256,14,64]{0,2,1:T(8,128)(2,1)S(1)} %bitcast.366, ...), kind=kOutput, calls=%fused_computation.15.clone.1 | convolution fusion | flops 983568896 | bytes 53688320 | tf_op jit(solution)/shard_map/while/body/eval_jaxpr/sub | solution.py:314
  637.2 26.0 %convert_bitcast_fusion.7 = bf16[4,256,14,64]{1,3,2,0:T(8,128)(2,1)} fusion(bf16[4,64,14,64]{1,3,2,0:T(8,128)(2,1)S(1)} %copy-done.11, f32[4,14,64,256]{3,2,1,0:T(8,128)} %fusion.513, f32[4,14,64,256]{3,2,1,0:T(8,128)} %copy-done, f32[4,14,64]{2,1,0:T(8,128)S(1)} %log_add_fusion.5), kind=kOutput, calls=%fused_computation.78.clone.1 | convolution fusion | flops 126619392 | bytes 9648128 | tf_op jit(solution)/shard_map/while/body/eval_jaxpr/chqk,cqhd->ckhd/dot_general | solution.py:281
  756.2 20.2 select_add_fusion.5
  779.2 42.2 %all-reduce.8 = bf16[7168]{0:T(1024)(128)(2,1)S(1)} all-reduce(bf16[7168]{0:T(1024)(128)(2,1)S(1)} %dynamic-update-slice.58), channel_id=1, replica_groups=mesh['dp'=8,'fsdp'=4] {'dp','fsdp'}, use_global_device_ids=true, to_apply=%add | all-reduce | flops 7168 | bytes 28672 | tf_op jit(solution)/shard_map/while
  821.6 60.1 %all-gather.7.cloned.1.call-done = bf16[7168,896]{1,0:T(8,128)(2,1)} async-done(((bf16[224,896]{1,0:T(8,128)(2,1)}), bf16[7168,896]{1,0:T(8,128)(2,1)}) %all-gather.7.cloned.1.call-update) | async-done | bytes 12845072 | tf_op jit(solution)/shard_map/while/body/eval_jaxpr/all_gather | solution.py:93
  1041.0 40.1 %all-reduce.9 = bf16[7168]{0:T(1024)(128)(2,1)S(1)} all-reduce(bf16[7168]{0:T(1024)(128)(2,1)S(1)} %dynamic-update-slice.59), channel_id=1, replica_groups=mesh['dp'=8,'fsdp'=4] {'dp','fsdp'}, use_global_device_ids=true, to_apply=%add.1 | all-reduce | flops 7168 | bytes 28672 | tf_op jit(solution)/shard_map/while
  1081.6 55.2 %all-gather.17.cloned.1.call-done = bf16[7168,896]{1,0:T(8,128)(2,1)} async-done(((bf16[224,896]{1,0:T(8,128)(2,1)}), bf16[7168,896]{1,0:T(8,128)(2,1)}) %all-gather.17.cloned.1.call-update) | async-done | bytes 12845072 | tf_op jit(solution)/shard_map/while/body/eval_jaxpr/all_gather | solution.py:94
  1149.7 85.5 %all-gather.15.cloned.1.call-done = bf16[7168,896]{1,0:T(8,128)(2,1)} async-done(((bf16[224,896]{1,0:T(8,128)(2,1)}), bf16[7168,896]{1,0:T(8,128)(2,1)}) %all-gather.15.cloned.1.call-update) | async-done | bytes 12845072 | tf_op jit(solution)/shard_map/while/body/eval_jaxpr/all_gather | solution.py:93
  1249.5 27.1 %fusion.514 = bf16[4,64,14,64]{1,3,2,0:T(8,128)(2,1)} fusion(bf16[4,256,14,64]{1,3,2,0:T(8,128)(2,1)} %copy.162, f32[4,14,64,256]{3,2,1,0:T(8,128)} %fusion.513, f32[4,14,64,256]{3,2,1,0:T(8,128)} %copy-done, f32[4,14,64]{2,1,0:T(8,128)S(1)} %log_add_fusion.5), kind=kOutput, calls=%fused_computation.122.clone.1 | convolution fusion | flops 125931264 | bytes 9648128 | tf_op jit(solution)/shard_map/while/body/eval_jaxpr/chqk,ckhd->cqhd/dot_general | solution.py:274
  1296.9 23.4 %subtract_convert_fusion.3 = (bf16[14,256,1024]{2,1,0:T(8,128)(2,1)}, bf16[14,256,1024]{2,1,0:T(8,128)(2,1)}, bf16[14,256,1024]{2,1,0:T(8,128)(2,1)}, f32[14,256,1024]{2,1,0:T(8,128)}) fusion(f32[14,256,1024]{2,1,0:T(8,128)} %get-tuple-element.539, f32[14,256]{1,0:T(8,128)S(1)} %log_add_fusion.4, bf16[256,14,64]{0,2,1:T(8,128)(2,1)S(1)} %bitcast.366, ...), kind=kOutput, calls=%fused_computation.15.clone.1 | convolution fusion | flops 983568896 | bytes 53688320 | tf_op jit(solution)/shard_map/while/body/eval_jaxpr/sub | solution.py:314
  1355.5 26.0 %convert_bitcast_fusion.7 = bf16[4,256,14,64]{1,3,2,0:T(8,128)(2,1)} fusion(bf16[4,64,14,64]{1,3,2,0:T(8,128)(2,1)S(1)} %copy-done.11, f32[4,14,64,256]{3,2,1,0:T(8,128)} %fusion.513, f32[4,14,64,256]{3,2,1,0:T(8,128)} %copy-done, f32[4,14,64]{2,1,0:T(8,128)S(1)} %log_add_fusion.5), kind=kOutput, calls=%fused_computation.78.clone.1 | convolution fusion | flops 126619392 | bytes 9648128 | tf_op jit(solution)/shard_map/while/body/eval_jaxpr/chqk,cqhd->ckhd/dot_general | solution.py:281
  1474.6 26.6 %select_add_fusion.5 = f32[8,896,896]{2,1,0:T(8,128)} fusion(f32[8,896,896]{2,1,0:T(8,128)} %bitcast_dynamic-update-slice_fusion.26, f32[8,896,896]{2,1,0:T(8,128)} %get-tuple-element.599, pred[]{:T(512)S(6)} %compare.3), kind=kLoop, calls=%fused_computation.11.clone.1 | loop fusion | flops 12845056 | bytes 77070336 | tf_op jit(solution)/shard_map/while/body/eval_jaxpr/add | solution.py:363
  1506.0 55.1 %all-reduce.5 = (f32[7168]{0:T(1024)S(1)}, f32[32,14]{0,1:T(8,128)}) all-reduce(f32[7168]{0:T(1024)S(1)} %copy-done.44, f32[32,14]{0,1:T(8,128)S(1)} %copy-done.58), channel_id=6, replica_groups=mesh['dp'=8,'fsdp'=4] {'dp','fsdp'}, use_global_device_ids=true, to_apply=%region_25.26.clone | all-reduce | flops 7616 | bytes 60928
  1561.7 222.1 %reduce-scatter.5.cloned.1.call-done = f32[224,896]{1,0:T(8,128)} async-done(((f32[7168,896]{1,0:T(8,128)}), f32[224,896]{1,0:T(8,128)}) %reduce-scatter.5.cloned.1.call-update) | async-done | bytes 802832 | tf_op jit(solution)/shard_map/reduce_scatter | solution.py:387
  1783.9 279.6 %reduce-scatter.7.cloned.1.call-done = f32[224,896]{1,0:T(8,128)} async-done(((f32[7168,896]{1,0:T(8,128)}), f32[224,896]{1,0:T(8,128)}) %reduce-scatter.7.cloned.1.call-update) | async-done | bytes 802832 | tf_op jit(solution)/shard_map/reduce_scatter | solution.py:393
  (552 shorter events, 687.2 us)
Async XLA Ops:
  67.4 104.9 %all-gather.7.cloned.1.call-start = ((), (), s32[]{:S(2)}) async-start(), calls=%async_computation.6 | async-start | bytes 13246464 | tf_op jit(solution)/shard_map/while/body/eval_jaxpr/all_gather | solution.py:93
  68.2 126.7 %all-gather.9.cloned.1.call-start = ((), (), s32[]{:S(2)}) async-start(), calls=%async_computation.7 | async-start | bytes 2293760 | tf_op jit(solution)/shard_map/while/body/eval_jaxpr/all_gather | solution.py:153
  175.3 42.2 %all-gather.11.cloned.1.call-start = ((), (), s32[]{:S(2)}) async-start(), calls=%async_computation.8 | async-start | bytes 2293760 | tf_op jit(solution)/shard_map/while/body/eval_jaxpr/all_gather | solution.py:154
  178.3 139.4 %all-gather.13.cloned.1.call-start = ((), (), s32[]{:S(2)}) async-start(), calls=%async_computation.9 | async-start | bytes 13246464 | tf_op jit(solution)/shard_map/while/body/eval_jaxpr/all_gather | solution.py:94
  178.9 248.6 %all-gather.17.cloned.1.call-start = ((), (), s32[]{:S(2)}) async-start(), calls=%async_computation.11 | async-start | bytes 13246464 | tf_op jit(solution)/shard_map/while/body/eval_jaxpr/all_gather | solution.py:94
  251.2 30.6 %collective-permute-start = (bf16[63,896]{1,0:T(8,128)(2,1)S(1)}, bf16[63,896]{1,0:T(8,128)(2,1)S(1)}, u32[]{:S(2)}, u32[]{:S(2)}) collective-permute-start(bf16[63,896]{1,0:T(8,128)(2,1)S(1)} %slice.396), channel_id=1, source_target_pairs={{1,0},{2,1},{3,2},{5,4},{6,5},{7,6},{9,8},{10,9},{11,10},{13,12},{... | collective-permute-start | bytes 338696 | tf_op jit(solution)/shard_map/while/body/eval_jaxpr/ppermute | solution.py:21
  295.7 4.0 collective-permute-start.1
  330.8 195.1 %all-gather.15.cloned.1.call-start = ((), (), s32[]{:S(2)}) async-start(), calls=%async_computation.10 | async-start | bytes 13246464 | tf_op jit(solution)/shard_map/while/body/eval_jaxpr/all_gather | solution.py:93
  331.4 395.4 %reduce-scatter.9.cloned.1.call-start = ((), (), s32[]{:S(2)}) async-start(), calls=%async_computation.12 | async-start | bytes 4587520 | tf_op jit(solution)/shard_map/while/body/eval_jaxpr/reduce_scatter | solution.py:331
  572.5 6.3 collective-permute-start.3
  619.5 110.7 %reduce-scatter.11.cloned.1.call-start = ((), (), s32[]{:S(2)}) async-start(), calls=%async_computation.13 | async-start | bytes 4587520 | tf_op jit(solution)/shard_map/while/body/eval_jaxpr/reduce_scatter | solution.py:332
  778.1 103.5 %all-gather.7.cloned.1.call-start = ((), (), s32[]{:S(2)}) async-start(), calls=%async_computation.6 | async-start | bytes 13246464 | tf_op jit(solution)/shard_map/while/body/eval_jaxpr/all_gather | solution.py:93
  778.8 125.3 %all-gather.9.cloned.1.call-start = ((), (), s32[]{:S(2)}) async-start(), calls=%async_computation.7 | async-start | bytes 2293760 | tf_op jit(solution)/shard_map/while/body/eval_jaxpr/all_gather | solution.py:153
  884.6 42.3 %all-gather.11.cloned.1.call-start = ((), (), s32[]{:S(2)}) async-start(), calls=%async_computation.8 | async-start | bytes 2293760 | tf_op jit(solution)/shard_map/while/body/eval_jaxpr/all_gather | solution.py:154
  887.6 139.4 %all-gather.13.cloned.1.call-start = ((), (), s32[]{:S(2)}) async-start(), calls=%async_computation.9 | async-start | bytes 13246464 | tf_op jit(solution)/shard_map/while/body/eval_jaxpr/all_gather | solution.py:94
  888.2 248.6 %all-gather.17.cloned.1.call-start = ((), (), s32[]{:S(2)}) async-start(), calls=%async_computation.11 | async-start | bytes 13246464 | tf_op jit(solution)/shard_map/while/body/eval_jaxpr/all_gather | solution.py:94
  960.5 30.6 %collective-permute-start = (bf16[63,896]{1,0:T(8,128)(2,1)S(1)}, bf16[63,896]{1,0:T(8,128)(2,1)S(1)}, u32[]{:S(2)}, u32[]{:S(2)}) collective-permute-start(bf16[63,896]{1,0:T(8,128)(2,1)S(1)} %slice.396), channel_id=1, source_target_pairs={{1,0},{2,1},{3,2},{5,4},{6,5},{7,6},{9,8},{10,9},{11,10},{13,12},{... | collective-permute-start | bytes 338696 | tf_op jit(solution)/shard_map/while/body/eval_jaxpr/ppermute | solution.py:21
  1004.9 4.0 collective-permute-start.1
  1040.1 195.1 %all-gather.15.cloned.1.call-start = ((), (), s32[]{:S(2)}) async-start(), calls=%async_computation.10 | async-start | bytes 13246464 | tf_op jit(solution)/shard_map/while/body/eval_jaxpr/all_gather | solution.py:93
  1040.7 404.7 %reduce-scatter.9.cloned.1.call-start = ((), (), s32[]{:S(2)}) async-start(), calls=%async_computation.12 | async-start | bytes 4587520 | tf_op jit(solution)/shard_map/while/body/eval_jaxpr/reduce_scatter | solution.py:331
  1281.7 6.3 collective-permute-start.3
  1328.8 119.9 %reduce-scatter.11.cloned.1.call-start = ((), (), s32[]{:S(2)}) async-start(), calls=%async_computation.13 | async-start | bytes 4587520 | tf_op jit(solution)/shard_map/while/body/eval_jaxpr/reduce_scatter | solution.py:332
  1504.6 279.3 %reduce-scatter.5.cloned.1.call-start = ((), (), s32[]{:S(2)}) async-start(), calls=%async_computation.4 | async-start | bytes 26492928 | tf_op jit(solution)/shard_map/reduce_scatter | solution.py:387
  1505.2 558.3 %reduce-scatter.7.cloned.1.call-start = ((), (), s32[]{:S(2)}) async-start(), calls=%async_computation.5 | async-start | bytes 26492928 | tf_op jit(solution)/shard_map/reduce_scatter | solution.py:393
  (132 other events, 1473.1 us)
Sparse Core Ops, SparseCore 0:
  71.2 101.1 all-gather.6
  175.5 19.3 all-gather.8
  196.4 21.1 all-gather.10
  220.3 97.3 all-gather.12
  331.0 96.5 all-gather.16
  430.3 95.5 all-gather.14
  619.7 42.9 reduce-scatter.8
  677.4 42.8 reduce-scatter.10
  781.8 99.7 all-gather.6
  884.7 19.3 all-gather.8
  905.7 21.1 all-gather.10
  929.6 97.3 all-gather.12
  1040.2 96.5 all-gather.16
  1139.6 95.5 all-gather.14
  1328.9 42.9 reduce-scatter.8
  1395.7 43.1 reduce-scatter.10
Sparse Core Ops, SparseCore 1:
  1508.0 275.9 reduce-scatter.4
  1786.7 276.7 reduce-scatter.6
where the time goes:
time: 2080 us; the launch traced here: 2070 us
  waiting for transfers between devices  987 us (47%)
  matrix products  552 us (27%)
  blocking collectives  220 us (11%)
  local copies, waits for them, and re-layouts  163 us (8%)
  other arithmetic  103 us (5%)
  starting transfers between devices  25.8 us (1%)
    all_gather x4, waiting for transfers between devices, fetch_weights(): lax.all_gather(attn_part, ('dp', 'fsdp'), axis=0, tiled=True)  292 us
    reduce_scatter x1, waiting for transfers between devices, per_device(): lax.psum_scatter(totals[1].reshape(2 * FF, model_width), ('dp', 'fsdp'),...  280 us
    reduce_scatter x1, waiting for transfers between devices, per_device(): lax.psum_scatter(totals[0].reshape(8 * model_width, model_width), ('dp',...  222 us
    while x4, blocking collectives  165 us
    all_gather x4, waiting for transfers between devices, fetch_weights(): lax.all_gather(ffw_part, ('dp', 'fsdp'), axis=0, tiled=True)  138 us
    dot_general x20, matrix products, times_transposed(): lax.dot_general(left_side, right_side, (((1,), (1,)), ((), ())), preferre...  75.6 us
    dot_general x20, matrix products, product(): return jnp.dot(left_side, right_side, preferred_element_type=jnp.float32)  71.9 us
    dot_general x20, matrix products, transposed_times(): lax.dot_general(left_side, right_side, (((0,), (0,)), ((), ())), preferre...  59.3 us
  transfers between devices with their start and end apart: 26, of which 20 were waited for; matrix products, arithmetic and copies ran while one was open for 22% of the time, Pallas kernels for 0%

commit v1 on v0

v1 whole, which is shorter than its diff:
```python
import jax
import jax.numpy as jnp
from jax import lax
from jax.experimental import pallas as pl
from jax.experimental.pallas import tpu as pltpu
from jax.sharding import PartitionSpec as P

FF = 3584
SPAN = 64
PIECE = 256

relative_bucket_limits = (1, 2, 3, 4, 5, 6, 7, 8, 12, 16, 24, 32, 64, 128, 256)
norm_eps = 1e-06
gelu_scale = 0.7978845608028654
gelu_cubic = 0.044715
masked_score = -1e30
F32 = jnp.float32
BF16 = jnp.bfloat16
AXES = ("dp", "fsdp")


def from_behind(array, axis, by):
    length = lax.axis_size(axis)
    pairs = [(i, i + by) for i in range(length) if 0 <= i + by < length]
    return lax.ppermute(array, axis, pairs)


def product(left_side, right_side):
    return jnp.dot(left_side, right_side, preferred_element_type=F32)


def times_transposed(left_side, right_side):
    return lax.dot_general(left_side, right_side, (((1,), (1,)), ((), ())), preferred_element_type=F32)


def transposed_times(left_side, right_side):
    return lax.dot_general(left_side, right_side, (((0,), (0,)), ((), ())), preferred_element_type=F32)


def inverse_rms(residual):
    return lax.rsqrt(jnp.mean(residual * residual, axis=-1, keepdims=True) + norm_eps)


def norm_back(residual, scale, gain, incoming):
    weighted = gain * incoming
    return scale * weighted - residual * scale * scale * scale * jnp.mean(
        residual * weighted, axis=-1, keepdims=True
    )


def gelu_parts(values):
    tangent = jnp.tanh(gelu_scale * (values + gelu_cubic * values * values * values))
    result = 0.5 * values * (1.0 + tangent)
    slope = 0.5 * (1.0 + tangent) + 0.5 * values * (1.0 - tangent * tangent) * gelu_scale * (
        1.0 + 3.0 * gelu_cubic * values * values
    )
    return (result, slope)


def bucket_of(offset):
    magnitude = jnp.abs(offset)
    counted = jnp.zeros(offset.shape, jnp.int32)
    for threshold in relative_bucket_limits:
        counted = counted + (magnitude >= threshold).astype(jnp.int32)
    return counted + (offset > 0).astype(jnp.int32) * (len(relative_bucket_limits) + 1)


def piece_labels(positions, starts):
    inside = (positions[None, :, None] >= starts[:, None, :]) & (
        positions[None, :, None] < starts[:, None, :] + PIECE
    )
    labels = jnp.arange(1, starts.shape[1] + 1, dtype=jnp.int32)
    return jnp.sum(jnp.where(inside, labels[None, None, :], 0), axis=2)


def dot_t(left_side, right_side):
    return lax.dot_general(left_side, right_side, (((1,), (1,)), ((), ())), preferred_element_type=F32)


def own_lanes(values, which, width):
    lane = lax.broadcasted_iota(jnp.int32, values.shape, 1)
    return jnp.where((lane >= which * width) & (lane < (which + 1) * width), values, jnp.zeros_like(values))


def flipped(values):
    return values.astype(F32).T.astype(BF16)


def bias_tiles(rel_table, rows, reach):
    heads = rel_table.shape[1]
    width = 2 * rows
    count = 2 * reach + 1
    shift = jnp.arange(width, dtype=jnp.int32)
    behind = jnp.where(shift < rows, shift, shift - width)
    far = (jnp.arange(count, dtype=jnp.int32) - reach) * rows
    ids = bucket_of(far[:, None] - behind[None, :])
    hot = (ids[:, :, None] == jnp.arange(rel_table.shape[0], dtype=jnp.int32)).astype(F32)
    lines = jnp.einsum("dwb,bh->hdw", hot, rel_table, precision=lax.Precision.HIGHEST)
    lines = lines.reshape(heads, count, 1, width)

    def spread(line_ref, tile_ref):
        for d in range(count):
            wide = jnp.broadcast_to(line_ref[0, d], (rows, width))
            tile_ref[0, d] = pltpu.roll(wide, 0, 1, stride=1, stride_axis=0)[:, :rows]

    return pl.pallas_call(
        spread,
        out_shape=jax.ShapeDtypeStruct((heads, count, rows, rows), F32),
        grid=(heads,),
        in_specs=[pl.BlockSpec((1, count, 1, width), lambda i: (i, 0, 0, 0))],
        out_specs=pl.BlockSpec((1, count, rows, rows), lambda i: (i, 0, 0, 0)),
        name="bias_tiles",
    )(lines)


def tile_at(block, place, reach):
    return jnp.clip(block - place, -reach, reach) + reach


def self_attention(place, query, keys, values, tiles, hidden_mask, head_size, reach):
    count, rows, width = query.shape
    blocks = keys.shape[0]
    pair = 128
    per = pair // head_size

    def body(place_ref, q_ref, k_ref, v_ref, tile_ref, mask_ref, o_ref, ot_ref, lse_ref, s_ref, p_ref):
        for b in range(count):
            scaled = q_ref[b] * jnp.asarray(0.125, BF16)
            value_t = jnp.concatenate([flipped(v_ref[j, b]) for j in range(blocks)], axis=1)
            for h in range(per):
                mine = own_lanes(scaled, h, head_size)
                top = jnp.full((1, rows), -jnp.inf, F32)
                for j in range(blocks):
                    s = dot_t(k_ref[j, b], mine)
                    s = s + tile_ref[h, tile_at(j, place_ref[0], reach)] + mask_ref[b, j]
                    s_ref[j] = s
                    top = jnp.maximum(top, jnp.max(s, axis=0, keepdims=True))
                total = jnp.zeros((1, rows), F32)
                for j in range(blocks):
                    p = jnp.exp(s_ref[j] - top)
                    total = total + jnp.sum(p, axis=0, keepdims=True)
                    p_ref[j * rows : (j + 1) * rows, :] = p.astype(BF16)
                part = product(value_t[h * head_size : (h + 1) * head_size], p_ref[...]) / total
                ot_ref[0, b, h * head_size : (h + 1) * head_size, :] = part
                lse_ref[0, b * per + h : b * per + h + 1, :] = top + jnp.log(total)
            o_ref[b] = ot_ref[0, b].T.astype(BF16)

    steps = width // pair
    grid_spec = pltpu.PrefetchScalarGridSpec(
        num_scalar_prefetch=1,
        grid=(steps,),
        in_specs=[
            pl.BlockSpec((count, rows, pair), lambda i, _: (0, 0, i)),
            pl.BlockSpec((blocks, count, rows, pair), lambda i, _: (0, 0, 0, i)),
            pl.BlockSpec((blocks, count, rows, pair), lambda i, _: (0, 0, 0, i)),
            pl.BlockSpec((per,) + tiles.shape[1:], lambda i, _: (i, 0, 0, 0)),
            pl.BlockSpec(hidden_mask.shape, lambda i, _: (0, 0, 0, 0)),
        ],
        out_specs=[
            pl.BlockSpec((count, rows, pair), lambda i, _: (0, 0, i)),
            pl.BlockSpec((1, count, pair, rows), lambda i, _: (i, 0, 0, 0)),
            pl.BlockSpec((1, count * per, rows), lambda i, _: (i, 0, 0)),
        ],
        scratch_shapes=[
            pltpu.VMEM((blocks, rows, rows), F32),
            pltpu.VMEM((blocks * rows, rows), BF16),
        ],
    )
    cost = 4 * count * blocks * rows * rows * width
    return pl.pallas_call(
        body,
        grid_spec=grid_spec,
        out_shape=[
            jax.ShapeDtypeStruct((count, rows, width), BF16),
            jax.ShapeDtypeStruct((steps, count, pair, rows), F32),
            jax.ShapeDtypeStruct((steps, count * per, rows), F32),
        ],
        cost_estimate=pl.CostEstimate(flops=4 * cost, transcendentals=0, bytes_accessed=30_000_000),
        name="self_attention",
    )(place, query, keys, values, tiles, hidden_mask)


def self_attention_back(place, query, keys, values, tiles, hidden_mask, outer_t, lse, grad, head_size, reach):
    count, rows, width = query.shape
    blocks = keys.shape[0]
    pair = 128
    per = pair // head_size
    half = rows // 2

    def body(
        place_ref, q_ref, k_ref, v_ref, tile_ref, mask_ref, ot_ref, lse_ref, do_ref,
        dq_ref, dk_ref, dv_ref, sum_ref, acc_ref, dk_acc, dv_acc,
    ):
        for b in range(count):
            scaled = q_ref[b] * jnp.asarray(0.125, BF16)
            incoming = do_ref[b]
            key_t = jnp.concatenate([flipped(k_ref[j, b]) for j in range(blocks)], axis=1)
            weighed = incoming.astype(F32).T * ot_ref[0, b]
            query_parts = []
            for h in range(per):
                lanes = slice(h * head_size, (h + 1) * head_size)
                mine = own_lanes(scaled, h, head_size)
                theirs = own_lanes(incoming, h, head_size)
                delta = jnp.sum(weighed[lanes], axis=0, keepdims=True)
                level = lse_ref[0, b * per + h : b * per + h + 1, :]
                part = jnp.zeros((head_size, rows), F32)
                for j in range(blocks):
                    s = dot_t(k_ref[j, b], mine)
                    s = s + tile_ref[h, tile_at(j, place_ref[0], reach)] + mask_ref[b, j]
                    p = jnp.exp(s - level)
                    ds = p * (dot_t(v_ref[j, b], theirs) - delta)
                    p_low = p.astype(BF16)
                    ds_low = ds.astype(BF16)
                    dv = product(p_low, theirs)
                    dk = product(ds_low, mine)
                    if h == 0:
                        dv_acc[j] = dv
                        dk_acc[j] = dk
                    else:
                        dv_ref[j, b] = (dv_acc[j] + dv).astype(BF16)
                        dk_ref[j, b] = (dk_acc[j] + dk).astype(BF16)
                    part = part + product(key_t[lanes, j * rows : (j + 1) * rows], ds_low)
                    if b == 0:
                        acc_ref[h, j] = ds
                    else:
                        acc_ref[h, j] = acc_ref[h, j] + ds
                query_parts.append(part)
            dq_ref[b] = (jnp.concatenate(query_parts, axis=0) * 0.125).T.astype(BF16)
        for h in range(per):
            for j in range(blocks):
                upper, lower = acc_ref[h, j, :half, :], acc_ref[h, j, half:, :]
                folded = jnp.concatenate(
                    [lower[:, :half], lower[:, half:] + upper[:, :half], upper[:, half:], jnp.zeros((half, half), F32)],
                    axis=1,
                )
                left = half // 2
                while left >= 8:
                    folded = folded[left:] + pltpu.roll(folded[:left], left, 1)
                    left //= 2
                sum_ref[h, j] = folded

    steps = width // pair
    grid_spec = pltpu.PrefetchScalarGridSpec(
        num_scalar_prefetch=1,
        grid=(steps,),
        in_specs=[
            pl.BlockSpec((count, rows, pair), lambda i, _: (0, 0, i)),
            pl.BlockSpec((blocks, count, rows, pair), lambda i, _: (0, 0, 0, i)),
            pl.BlockSpec((blocks, count, rows, pair), lambda i, _: (0, 0, 0, i)),
            pl.BlockSpec((per,) + tiles.shape[1:], lambda i, _: (i, 0, 0, 0)),
            pl.BlockSpec(hidden_mask.shape, lambda i, _: (0, 0, 0, 0)),
            pl.BlockSpec((1, count, pair, rows), lambda i, _: (i, 0, 0, 0)),
            pl.BlockSpec((1, count * per, rows), lambda i, _: (i, 0, 0)),
            pl.BlockSpec((count, rows, pair), lambda i, _: (0, 0, i)),
        ],
        out_specs=[
            pl.BlockSpec((count, rows, pair), lambda i, _: (0, 0, i)),
            pl.BlockSpec((blocks, count, rows, pair), lambda i, _: (0, 0, 0, i)),
            pl.BlockSpec((blocks, count, rows, pair), lambda i, _: (0, 0, 0, i)),
            pl.BlockSpec((per, blocks, 8, 2 * rows), lambda i, _: (i, 0, 0, 0)),
        ],
        scratch_shapes=[
            pltpu.VMEM((per, blocks, rows, rows), F32),
            pltpu.VMEM((blocks, rows, pair), F32),
            pltpu.VMEM((blocks, rows, pair), F32),
        ],
    )
    cost = 4 * count * blocks * rows * rows * width
    return pl.pallas_call(
        body,
        grid_spec=grid_spec,
        out_shape=[
            jax.ShapeDtypeStruct((count, rows, width), BF16),
            jax.ShapeDtypeStruct((blocks, count, rows, width), BF16),
            jax.ShapeDtypeStruct((blocks, count, rows, width), BF16),
            jax.ShapeDtypeStruct((width // head_size, blocks, 8, 2 * rows), F32),
        ],
        cost_estimate=pl.CostEstimate(flops=10 * cost, transcendentals=0, bytes_accessed=40_000_000),
        name="self_attention_back",
    )(place, query, keys, values, tiles, hidden_mask, outer_t, lse, grad)


def both_heads(values, head_size):
    return jnp.concatenate([own_lanes(values, h, head_size) for h in range(128 // head_size)], axis=0)


def picked(wide, rows, head_size):
    total = own_lanes(wide[:rows], 0, head_size)
    for h in range(1, 128 // head_size):
        total = total + own_lanes(wide[h * rows : (h + 1) * rows], h, head_size)
    return total


def softmax_down(scores):
    raised = jnp.exp(scores - jnp.max(scores, axis=0, keepdims=True))
    return raised / jnp.sum(raised, axis=0, keepdims=True)


def span_attention(query, keys, values, head_size):
    blocks, rows, width = query.shape
    span_keys = keys.shape[1]

    def body(q_ref, k_ref, v_ref, o_ref):
        for i in range(width // 128):
            lanes = slice(i * 128, (i + 1) * 128)
            stacked = both_heads(q_ref[0, :, lanes] * jnp.asarray(0.125, BF16), head_size)
            p = softmax_down(dot_t(k_ref[0, :, lanes], stacked)).astype(BF16)
            wide = product(flipped(v_ref[0, :, lanes]), p).T
            o_ref[0, :, lanes] = picked(wide, rows, head_size).astype(BF16)

    q_spec = pl.BlockSpec((1, rows, width), lambda i: (i, 0, 0))
    k_spec = pl.BlockSpec((1, span_keys, width), lambda i: (i, 0, 0))
    return pl.pallas_call(
        body,
        grid=(blocks,),
        in_specs=[q_spec, k_spec, k_spec],
        out_specs=q_spec,
        out_shape=jax.ShapeDtypeStruct(query.shape, BF16),
        cost_estimate=pl.CostEstimate(flops=16 * blocks * rows * span_keys * width, transcendentals=0, bytes_accessed=12_000_000),
        name="span_attention",
    )(query, keys, values)


def span_attention_back(query, keys, values, grad, head_size):
    blocks, rows, width = query.shape
    span_keys = keys.shape[1]

    def body(q_ref, k_ref, v_ref, do_ref, dq_ref, dk_ref, dv_ref):
        for i in range(width // 128):
            lanes = slice(i * 128, (i + 1) * 128)
            stacked = both_heads(q_ref[0, :, lanes] * jnp.asarray(0.125, BF16), head_size)
            theirs = both_heads(do_ref[0, :, lanes], head_size)
            k, v = k_ref[0, :, lanes], v_ref[0, :, lanes]
            p = softmax_down(dot_t(k, stacked))
            dp = dot_t(v, theirs)
            ds = p * (dp - jnp.sum(p * dp, axis=0, keepdims=True))
            ds_low = ds.astype(BF16)
            dv_ref[0, :, lanes] = product(p.astype(BF16), theirs).astype(BF16)
            dk_ref[0, :, lanes] = product(ds_low, stacked).astype(BF16)
            wide = (product(flipped(k), ds_low) * 0.125).T
            dq_ref[0, :, lanes] = picked(wide, rows, head_size).astype(BF16)

    q_spec = pl.BlockSpec((1, rows, width), lambda i: (i, 0, 0))
    k_spec = pl.BlockSpec((1, span_keys, width), lambda i: (i, 0, 0))
    return pl.pallas_call(
        body,
        grid=(blocks,),
        in_specs=[q_spec, k_spec, k_spec, q_spec],
        out_specs=[q_spec, k_spec, k_spec],
        out_shape=[
            jax.ShapeDtypeStruct(query.shape, BF16),
            jax.ShapeDtypeStruct(keys.shape, BF16),
            jax.ShapeDtypeStruct(keys.shape, BF16),
        ],
        cost_estimate=pl.CostEstimate(flops=40 * blocks * rows * span_keys * width, transcendentals=0, bytes_accessed=24_000_000),
        name="span_attention_back",
    )(query, keys, values, grad)


def per_device(hidden, neighbours, piece_starts, out_grad, attn_weights, ffw_weights, vectors, rel_table):
    count, rows, width = hidden.shape
    group = lax.axis_size("fsdp")
    length = rows * group
    heads = rel_table.shape[1]
    head_size = width // heads
    buckets = rel_table.shape[0]
    spans = neighbours.shape[1]
    span_keys = neighbours.shape[2]
    carried = SPAN - 1
    kept = rows - carried
    tokens = count * rows
    reach = -(-relative_bucket_limits[-1] // rows) + 1
    place = lax.axis_index("fsdp").astype(jnp.int32)
    share = attn_weights.shape[0]

    gather = lambda array, axes: lax.all_gather(array, axes, axis=0, tiled=True)
    vector_row = jnp.pad(vectors.reshape(1, -1), ((0, 15), (0, width - vectors.shape[0])))
    hidden_all = gather(hidden[None], "fsdp")
    first_full = gather(jnp.concatenate([attn_weights, vector_row], axis=0)[None], AXES)
    ffw_full = gather(ffw_weights, AXES)
    matrices = first_full[:, :share].reshape(8, width, width)
    vector_full = first_full[:, share, : vectors.shape[0]].reshape(-1).astype(F32)
    w_input, w_output = ffw_full[:FF], ffw_full[FF:]
    bias_input = vector_full[:FF]
    gains = vector_full[FF : FF + 3 * width].reshape(3, width)
    bias_output = vector_full[FF + 3 * width :]

    tiles = bias_tiles(rel_table, rows, reach)
    key_pos = jnp.arange(length, dtype=jnp.int32)
    query_pos = place * rows + jnp.arange(rows, dtype=jnp.int32)
    key_piece = piece_labels(key_pos, piece_starts)
    query_piece = piece_labels(query_pos, piece_starts)
    allowed = (key_pos[:, None] <= query_pos[None, :])[None] | (
        (key_piece[:, :, None] == query_piece[:, None, :]) & (query_piece[:, None, :] > 0)
    )
    mask = jnp.where(allowed, 0.0, masked_score).reshape(count, group, rows, rows)
    place_arg = place.reshape(1)

    residual = hidden.reshape(tokens, width).astype(F32)
    every = hidden_all.reshape(group * tokens, width).astype(F32)
    normed_every = (every * inverse_rms(every) * gains[0]).astype(BF16)
    scale_one = inverse_rms(residual)
    normed_one = (residual * scale_one * gains[0]).astype(BF16)
    queries = product(normed_one, matrices[0]).astype(BF16).reshape(count, rows, width)
    keys = product(normed_every, matrices[1]).astype(BF16).reshape(group, count, rows, width)
    values = product(normed_every, matrices[2]).astype(BF16).reshape(group, count, rows, width)
    near_flat = neighbours.reshape(count * spans * span_keys, width)
    cross_keys = product(near_flat, matrices[5]).astype(BF16).reshape(count * spans, span_keys, width)
    cross_values = product(near_flat, matrices[6]).astype(BF16).reshape(count * spans, span_keys, width)
    context, context_t, lse = self_attention(
        place_arg, queries, keys, values, tiles, mask, head_size, reach
    )
    context = context.reshape(tokens, width)
    first_sum = residual + product(context, matrices[3])
    scale_two = inverse_rms(first_sum)
    normed_two = (first_sum * scale_two * gains[1]).astype(BF16)
    cross_queries = product(normed_two, matrices[4]).astype(BF16).reshape(count, rows, width)

    def ahead(array):
        incoming = from_behind(array[:, :carried], "fsdp", -1)
        return jnp.concatenate([array[:, carried:], incoming], axis=1).reshape(count * spans, SPAN, width)

    def behind(array):
        array = array.reshape(count, rows, width)
        arriving = from_behind(array[:, kept:], "fsdp", 1)
        return jnp.concatenate([arriving, array[:, :kept]], axis=1).reshape(tokens, width)

    block_queries = ahead(cross_queries)
    placed = behind(span_attention(block_queries, cross_keys, cross_values, head_size))
    second_sum = first_sum + product(placed, matrices[7])
    scale_three = inverse_rms(second_sum)
    normed_three = (second_sum * scale_three * gains[2]).astype(BF16)
    pre_act = times_transposed(normed_three, w_input) + bias_input
    act_value, act_slope = gelu_parts(pre_act)
    activated = act_value.astype(BF16)
    output = (second_sum + product(activated, w_output) + bias_output).astype(BF16)

    grad_out_low = out_grad.reshape(tokens, width)
    grad_out = grad_out_low.astype(F32)
    grad_bias_output = jnp.sum(grad_out, axis=0)
    grad_w_output = transposed_times(activated, grad_out_low).astype(BF16)
    grad_pre = times_transposed(grad_out_low, w_output) * act_slope
    grad_bias_input = jnp.sum(grad_pre, axis=0)
    grad_pre_low = grad_pre.astype(BF16)
    grad_w_input = transposed_times(grad_pre_low, normed_three).astype(BF16)
    scatter = lambda array: lax.psum_scatter(array, AXES, scatter_dimension=0, tiled=True)
    ffw_sum = scatter(jnp.concatenate([grad_w_input, grad_w_output], axis=0))
    grad_norm_three = product(grad_pre_low, w_input)
    grad_gain_three = jnp.sum(grad_norm_three * second_sum * scale_three, axis=0)
    grad_second = grad_out + norm_back(second_sum, scale_three, gains[2], grad_norm_three)
    grad_second_low = grad_second.astype(BF16)
    grad_cross_out = transposed_times(placed, grad_second_low)
    grad_placed = times_transposed(grad_second_low, matrices[7]).astype(BF16).reshape(count, rows, width)
    grad_block_queries, grad_cross_keys, grad_cross_values = span_attention_back(
        block_queries, cross_keys, cross_values, ahead(grad_placed), head_size
    )
    grad_cross_keys = grad_cross_keys.reshape(count * spans * span_keys, width)
    grad_cross_values = grad_cross_values.reshape(count * spans * span_keys, width)
    grad_cross_queries = behind(grad_block_queries)
    grad_cross_query_mat = transposed_times(normed_two, grad_cross_queries)
    grad_norm_two = times_transposed(grad_cross_queries, matrices[4])
    grad_gain_two = jnp.sum(grad_norm_two * first_sum * scale_two, axis=0)
    grad_first = grad_second + norm_back(first_sum, scale_two, gains[1], grad_norm_two)
    grad_first_low = grad_first.astype(BF16)
    grad_self_out = transposed_times(context, grad_first_low)
    grad_context = times_transposed(grad_first_low, matrices[3]).astype(BF16).reshape(count, rows, width)
    grad_queries, grad_keys, grad_values, diagonal = self_attention_back(
        place_arg, queries, keys, values, tiles, mask, context_t, lse, grad_context, head_size, reach
    )
    grad_queries = grad_queries.reshape(tokens, width)
    grad_keys = grad_keys.reshape(group * tokens, width)
    grad_values = grad_values.reshape(group * tokens, width)
    partial_one = (
        times_transposed(grad_keys, matrices[1]) + times_transposed(grad_values, matrices[2])
    ).astype(BF16)
    joined = lax.psum_scatter(
        partial_one.reshape(group, tokens, width), "fsdp", scatter_dimension=0, tiled=True
    ).reshape(tokens, width)
    grad_cross_key_mat = transposed_times(near_flat, grad_cross_keys)
    grad_cross_value_mat = transposed_times(near_flat, grad_cross_values)
    near_grad = times_transposed(grad_cross_keys, matrices[5]) + times_transposed(
        grad_cross_values, matrices[6]
    )
    grad_query_mat = transposed_times(normed_one, grad_queries)
    grad_key_mat = transposed_times(normed_every, grad_keys)
    grad_value_mat = transposed_times(normed_every, grad_values)
    grad_norm_one = times_transposed(grad_queries, matrices[0]) + joined.astype(F32)
    grad_gain_one = jnp.sum(grad_norm_one * residual * scale_one, axis=0)
    hidden_grad = grad_first + norm_back(residual, scale_one, gains[0], grad_norm_one)

    lane = jnp.arange(2 * rows, dtype=jnp.int32)
    line = jnp.arange(8, dtype=jnp.int32)
    block = jnp.arange(group, dtype=jnp.int32)
    between = (block[:, None, None] - place) * rows - (lane[None, None, :] - (rows - 8) - line[None, :, None])
    hot = (bucket_of(between)[..., None] == jnp.arange(buckets, dtype=jnp.int32)).astype(F32)
    table_step = jnp.einsum("hjsl,jslb->bh", diagonal, hot, precision=lax.Precision.HIGHEST)

    attn_sum = scatter(
        jnp.concatenate(
            [
                part.astype(BF16)
                for part in (
                    grad_query_mat,
                    grad_key_mat,
                    grad_value_mat,
                    grad_self_out,
                    grad_cross_query_mat,
                    grad_cross_key_mat,
                    grad_cross_value_mat,
                    grad_cross_out,
                )
            ],
            axis=0,
        )
    )
    vector_step = jnp.concatenate(
        [grad_bias_input, grad_gain_one, grad_gain_two, grad_gain_three, grad_bias_output]
    )
    vector_sum = lax.psum_scatter(vector_step, AXES, scatter_dimension=0, tiled=True)
    table_sum = lax.psum(table_step, AXES)
    return (
        output.reshape(count, rows, width),
        hidden_grad.reshape(count, rows, width),
        near_grad.reshape(count, spans, span_keys, width),
        attn_sum.astype(F32),
        ffw_sum.astype(F32),
        vector_sum,
        table_sum,
    )


def solution(mesh):
    placed = (
        P("dp", "fsdp", None),
        P("dp", "fsdp", None, None),
        P("dp", None),
        P("dp", "fsdp", None),
        P(("dp", "fsdp"), None),
        P(("dp", "fsdp"), None),
        P(("dp", "fsdp")),
        P(),
    )
    return jax.shard_map(
        per_device,
        mesh=mesh,
        in_specs=placed,
        out_specs=(
            P("dp", "fsdp", None),
            P("dp", "fsdp", None),
            P("dp", "fsdp", None, None),
            P(("dp", "fsdp"), None),
            P(("dp", "fsdp"), None),
            P(("dp", "fsdp")),
            P(),
        ),
        check_vma=False,
    )
```

time: 2080 us -> 746 us (0.36)
  waiting for transfers between devices: 987 us -> 333 us
  matrix products: 552 us -> 150 us
  blocking collectives: 220 us -> 47.5 us
  local copies, waits for them, and re-layouts: 163 us -> 34.9 us
  Pallas kernels: 0 us -> 101 us
  other arithmetic: 103 us -> 41.3 us
    all_gather x12 -> x3, waiting for transfers between devices: 474 us -> 119 us  [per_device(): gather = lambda array, axes: lax.all_gather(array, axes, axis=0, tiled=True)]
    dot_general x51 -> x12, matrix products: 370 us -> 51.9 us  [the longest x10 50.2 us: product(): return jnp.dot(left_side, right_side, preferred_element_type=F32)]
    reduce_scatter x6 -> x3, waiting for transfers between devices: 502 us -> 208 us  [the longest x2 208 us: per_device(): lax.psum_scatter(array, AXES, scatter_dimension=0, tiled=True)]
    while x4 -> x0, blocking collectives: 165 us -> none
    pallas_call x0 -> x5, Pallas kernels: none -> 101 us  [the longest x1 33 us: self_attention_back(): pl.pallas_call(body, grid_spec=grid_spec, out_shape=[jax.ShapeDtypeStruct...]
    add x18 -> x8, other arithmetic: 78.6 us -> 4.95 us  [the longest x1 3.42 us: per_device(): grad_first + norm_back(residual, scale_one, gains[0], grad_norm_one)]
    reshape x16 -> x2, local copies, waits for them, and re-layouts: 64.8 us -> 1.47 us  [the longest x1 0.81 us: bias_tiles(): lines = lines.reshape(heads, count, 1, width)]
    sub x2 -> x0, matrix products: 46.7 us -> none  [micro_step(): grad_self_w - jnp.sum(self_probs * grad_self_w, axis=-1, keepdims=True)]
  transfers between devices with their start and end apart: 26 -> 10, of which waited for: 20 -> 5; matrix products, arithmetic and copies ran while one was open for 22% -> 24% of each run, Pallas kernels for 0% -> 6%
where the time goes in v1:
time: 746 us; the launch traced here: 736 us
  waiting for transfers between devices  333 us (45%)
  matrix products  150 us (20%)
  Pallas kernels  101 us (14%)
  blocking collectives  47.5 us (6%)
  other arithmetic  41.3 us (6%)
  local copies, waits for them, and re-layouts  34.9 us (5%)
  between operations  15.1 us (2%)
  starting transfers between devices  13.6 us (2%)
    reduce_scatter x2, waiting for transfers between devices, per_device(): lax.psum_scatter(array, AXES, scatter_dimension=0, tiled=True)  208 us
    all_gather x3, waiting for transfers between devices, per_device(): gather = lambda array, axes: lax.all_gather(array, axes, axis=0, tiled=True)  119 us
    dot_general x10, matrix products, times_transposed(): lax.dot_general(left_side, right_side, (((1,), (1,)), ((), ())), preferre...  50.3 us
    dot_general x10, matrix products, product(): return jnp.dot(left_side, right_side, preferred_element_type=F32)  50.2 us
    dot_general x10, matrix products, transposed_times(): lax.dot_general(left_side, right_side, (((0,), (0,)), ((), ())), preferre...  48 us
    unnamed x1, blocking collectives  47.5 us
    pallas_call x1, Pallas kernels, self_attention_back(): pl.pallas_call(body, grid_spec=grid_spec, out_shape=[jax.ShapeDtypeStruct...  33 us
    pallas_call x1, Pallas kernels, self_attention(): pl.pallas_call(body, grid_spec=grid_spec, out_shape=[jax.ShapeDtypeStruct...  23.3 us
  transfers between devices with their start and end apart: 10, of which 5 were waited for; matrix products, arithmetic and copies ran while one was open for 24% of the time, Pallas kernels for 6%

profile of v1, /device:TPU:0, one launch (start us, length us, event | category | flops | bytes accessed | tf_op | source)
XLA Modules:
  0.0 736.1 jit_solution(13387102090312553571)
XLA Ops:
  12.4 11.9 %bias_tiles.1.tile_ref = f32[14,5,256,256]{3,2,1,0:T(8,128)} custom-call(f32[14,5,1,512]{3,2,1,0:T(1,128)} %copy.35.line_ref), custom_call_target="tpu_custom_call" | custom-call | tf_op jit(solution)/shard_map/bias_tiles/pallas_call | solution.py:106
  27.3 16.5 %all-gather.10.cloned.1.call-done = bf16[8,256,896]{2,1,0:T(8,128)(2,1)} async-done(((bf16[2,256,896]{2,1,0:T(8,128)(2,1)}), bf16[8,256,896]{2,1,0:T(8,128)(2,1)}) %all-gather.10.cloned.1.call-update) | async-done | bytes 3670032 | tf_op jit(solution)/shard_map/all_gather | solution.py:376
  46.7 102.2 %all-gather.8.cloned.1.call-done = bf16[7680,896]{1,0:T(8,128)(2,1)} async-done(((bf16[240,896]{1,0:T(8,128)(2,1)}), bf16[7680,896]{1,0:T(8,128)(2,1)}) %all-gather.8.cloned.1.call-update) | async-done | bytes 13762576 | tf_op jit(solution)/shard_map/all_gather | solution.py:376
  150.9 8.2 %fusion.82 = (bf16[4,224,896]{2,1,0:T(8,128)(2,1)}, bf16[4,224,896]{2,1,0:T(8,128)(2,1)S(1)}, bf16[4,224,896]{2,1,0:T(8,128)(2,1)}, bf16[4,224,896]{2,1,0:T(8,12...) fusion(bf16[32,240,896]{2,1,0:T(8,128)(2,1)} %bitcast.156), kind=kLoop, calls=%fused_computation.174 | loop fusion | bytes 25690112 | tf_op jit(solution)/shard_map/slice | solution.py:430
  176.1 23.3 %self_attention.1 = (bf16[2,256,896]{2,1,0:T(8,128)(2,1)}, f32[7,2,128,256]{3,2,1,0:T(8,128)}, f32[7,4,256]{2,1,0:T(4,128)}) custom-call(s32[1]{0:T(128)} %bitcast.1.place_ref, bf16[2,256,896]{2,1,0:T(8,128)(2,1)} %bitcast.199, bf16[4,2,256,896]{3,2,1,0:T(8,128)(2,1)} %bitcast.166, bf16[4,2,256,896]{3,2,1,0:T(8,128)(2,1)} %bitcast.168, ...), custom_call_target="tpu_custom_call" | custom-call | flops 7516192768 | bytes 30000000 | tf_op jit(solution)/shard_map/self_attention/pallas_call | solution.py:170
  217.9 6.1 copy.36
  224.0 6.1 copy.37
  231.1 10.6 %span_attention.1 = bf16[8,64,896]{2,1,0:T(8,128)(2,1)} custom-call(bf16[8,64,896]{2,1,0:T(8,128)(2,1)} %bitcast.159, bf16[8,256,896]{2,1,0:T(8,128)(2,1)} %bitcast.150, bf16[8,256,896]{2,1,0:T(8,128)(2,1)} %bitcast.152), custom_call_target="tpu_custom_call" | custom-call | flops 1879048192 | bytes 12000000 | tf_op jit(solution)/shard_map/span_attention/pallas_call | solution.py:313
  251.3 7.6 %fusion.14 = f32[512,3584]{1,0:T(8,128)S(1)} fusion(bf16[7168,896]{1,0:T(8,128)(2,1)} %all-gather.6.cloned.1.call-done, f32[512,896]{1,0:T(8,128)S(1)} %get-tuple-element.52, f32[896]{0:T(1024)S(1)} %slice.141, f32[512]{0:T(512)S(1)} %add_rsqrt_fusion.1), kind=kOutput, calls=%fused_computation.23 | convolution fusion | flops 3289710592 | bytes 15603200 | tf_op jit(solution)/shard_map/dot_general | solution.py:33
  259.0 9.2 %fusion.83 = (f32[3584]{0:T(1024)S(1)}, bf16[512,3584]{1,0:T(8,128)(2,1)}) fusion(f32[512,3584]{1,0:T(8,128)S(1)} %fusion.14, f32[3584]{0:T(1024)S(1)} %slice.144, bf16[512,896]{1,0:T(8,128)(2,1)S(1)} %bitcast.161, bf16[7168,896]{1,0:T(8,128)(2,1)S(1)} %copy-done.38), kind=kOutput, calls=%fused_computation.175 | convolution fusion | flops 3326865920 | bytes 18380800 | tf_op jit(solution)/shard_map/dot_general | solution.py:33
  268.1 6.1 multiply_reduce_fusion
  283.8 21.6 %span_attention_back.1 = (bf16[8,64,896]{2,1,0:T(8,128)(2,1)}, bf16[8,256,896]{2,1,0:T(8,128)(2,1)}, bf16[8,256,896]{2,1,0:T(8,128)(2,1)}) custom-call(bf16[8,64,896]{2,1,0:T(8,128)(2,1)} %bitcast.160, bf16[8,256,896]{2,1,0:T(8,128)(2,1)} %bitcast.151, bf16[8,256,896]{2,1,0:T(8,128)(2,1)} %bitcast.153, bf16[8,64,896]{2,1,0:T(8,128)(2,1)} %bitcast.197), custom_call_target="tpu_custom_call" | custom-call | flops 4697620480 | bytes 24000000 | tf_op jit(solution)/shard_map/span_attention_back/pallas_call | solution.py:345
  306.6 7.3 collective-permute-start.3
  320.7 33.0 %self_attention_back.1 = (bf16[2,256,896]{2,1,0:T(8,128)(2,1)}, bf16[4,2,256,896]{3,2,1,0:T(8,128)(2,1)}, bf16[4,2,256,896]{3,2,1,0:T(8,128)(2,1)}, f32[14,4,8,512]{3,2,1,0:T(8,128)}) custom-call(s32[1]{0:T(128)} %bitcast.1.place_ref, bf16[2,256,896]{2,1,0:T(8,128)(2,1)} %bitcast.200, bf16[4,2,256,896]{3,2,1,0:T(8,128)(2,1)} %bitcast.167, ...), custom_call_target="tpu_custom_call" | custom-call | flops 18790481920 | bytes 40000000 | tf_op jit(solution)/shard_map/self_attention_back/pallas_call | solution.py:269
  353.8 7.2 fusion.84
  361.0 5.8 add_convert_fusion
  367.1 6.7 convolution_convert_fusion.1
  373.8 9.4 %convolution_convert_fusion = bf16[3584,896]{1,0:T(8,128)(2,1)S(1)} fusion(bf16[512,896]{1,0:T(8,128)(2,1)S(1)} %bitcast.162, f32[512,3584]{1,0:T(8,128)} %copy-done.49, f32[3584]{0:T(1024)S(1)} %slice.144), kind=kOutput, calls=%fused_computation.16 | convolution fusion | flops 3309895680 | bytes 14694400 | tf_op jit(solution)/shard_map/dot_general | solution.py:37
  383.2 20.2 %pad_maximum_fusion = bf16[7168,896]{1,0:T(8,128)(2,1)} fusion(bf16[3584,896]{1,0:T(8,128)(2,1)S(1)} %convolution_convert_fusion, bf16[3584,896]{1,0:T(8,128)(2,1)S(1)} %convolution_convert_fusion.1), kind=kLoop, calls=%fused_computation | loop fusion | flops 25690112 | bytes 25690112 | tf_op jit(solution)/shard_map/concatenate | solution.py:447
  436.6 11.3 %add_convert_fusion.1 = bf16[512,896]{1,0:T(8,128)(2,1)} fusion(f32[512,896]{1,0:T(8,128)} %copy-done.11, bf16[7168,896]{1,0:T(8,128)(2,1)} %all-gather.6.cloned.1.call-done, f32[896]{0:T(1024)S(1)} %slice.147, f32[512,3584]{1,0:T(8,128)} %copy-done.49, f32[3584]{0:T(1024)S(1)} %slice.144), kind=kOutput, calls=%fused_computation.63 | convolution fusion | flops 3308060672 | bytes 16532992 | tf_op jit(solution)/shard_map/dot_general | solution.py:29
  452.4 6.7 convolution_add_fusion
  465.2 47.5 %all-reduce.2 = (f32[7168]{0:T(1024)S(1)}, f32[32,14]{0,1:T(8,128)}) all-reduce(f32[7168]{0:T(1024)S(1)} %constant_dynamic-update-slice_fusion.1, f32[32,14]{0,1:T(8,128)S(1)} %fusion.38), channel_id=7, replica_groups=mesh['dp'=8,'fsdp'=4] {'dp','fsdp'}, use_global_device_ids=true, to_apply=%region_17.18.clone | all-reduce | flops 7616 | bytes 60928
  516.8 52.6 %reduce-scatter.8.cloned.1.call-done = bf16[224,896]{1,0:T(8,128)(2,1)} async-done(((bf16[7168,896]{1,0:T(8,128)(2,1)}), bf16[224,896]{1,0:T(8,128)(2,1)}) %reduce-scatter.8.cloned.1.call-update) | async-done | bytes 401424 | tf_op jit(solution)/shard_map/reduce_scatter | solution.py:446
  571.3 155.8 %reduce-scatter.6.cloned.1.call-done = bf16[224,896]{1,0:T(8,128)(2,1)} async-done(((bf16[7168,896]{1,0:T(8,128)(2,1)}), bf16[224,896]{1,0:T(8,128)(2,1)}) %reduce-scatter.6.cloned.1.call-update) | async-done | bytes 401424 | tf_op jit(solution)/shard_map/reduce_scatter | solution.py:446
  (209 shorter events, 128.2 us)
Async XLA Ops:
  7.2 36.6 %all-gather.10.cloned.1.call-start = ((), (), s32[]{:S(2)}) async-start(), calls=%async_computation.8 | async-start | bytes 4587520 | tf_op jit(solution)/shard_map/all_gather | solution.py:376
  7.9 140.9 %all-gather.8.cloned.1.call-start = ((), (), s32[]{:S(2)}) async-start(), calls=%async_computation.7 | async-start | bytes 14192640 | tf_op jit(solution)/shard_map/all_gather | solution.py:376
  10.4 240.8 %all-gather.6.cloned.1.call-start = ((), (), s32[]{:S(2)}) async-start(), calls=%async_computation.3 | async-start | bytes 13246464 | tf_op jit(solution)/shard_map/all_gather | solution.py:376
  11.2 449.4 %reduce-scatter.4.cloned.1.call-start = ((), (), s32[]{:S(2)}) async-start(), calls=%async_computation.4 | async-start | bytes 4587520 | tf_op jit(solution)/shard_map/reduce_scatter | solution.py:476
  12.4 11.9 %copy-start.36 = (s32[2,2]{1,0:T(2,128)S(1)}, s32[2,2]{1,0:T(2,128)}, u32[]{:S(2)}) copy-start(s32[2,2]{1,0:T(2,128)} %param.10) | copy-start | bytes 52
  12.4 12.2 %copy-start.2 = (bf16[2,256,896]{2,1,0:T(8,128)(2,1)S(1)}, bf16[2,256,896]{2,1,0:T(8,128)(2,1)}, u32[]{:S(2)}) copy-start(bf16[2,256,896]{2,1,0:T(8,128)(2,1)} %param.8) | copy-start | bytes 2752516
  150.5 11.8 %copy-start.33 = (f32[896]{0:T(1024)}, f32[896]{0:T(1024)S(1)}, u32[]{:S(2)}) copy-start(f32[896]{0:T(1024)S(1)} %slice.125) | copy-start | bytes 10756
  150.8 8.2 %copy-start.32 = (bf16[2,256,896]{2,1,0:T(8,128)(2,1)}, bf16[2,256,896]{2,1,0:T(8,128)(2,1)S(1)}, u32[]{:S(2)}) copy-start(bf16[2,256,896]{2,1,0:T(8,128)(2,1)S(1)} %fusion.19) | copy-start | bytes 2752516
  159.0 11.3 %copy-start.20 = (bf16[4,224,896]{2,1,0:T(8,128)(2,1)}, bf16[4,224,896]{2,1,0:T(8,128)(2,1)S(1)}, u32[]{:S(2)}) copy-start(bf16[4,224,896]{2,1,0:T(8,128)(2,1)S(1)} %get-tuple-element.44) | copy-start | bytes 4816900
  159.1 53.1 %copy-start.16 = (bf16[4,224,896]{2,1,0:T(8,128)(2,1)}, bf16[4,224,896]{2,1,0:T(8,128)(2,1)S(1)}, u32[]{:S(2)}) copy-start(bf16[4,224,896]{2,1,0:T(8,128)(2,1)S(1)} %get-tuple-element.40) | copy-start | bytes 4816900
  205.3 24.9 %collective-permute-start = (bf16[2,63,896]{2,1,0:T(8,128)(2,1)S(1)}, bf16[2,63,896]{2,1,0:T(8,128)(2,1)S(1)}, u32[]{:S(2)}, u32[]{:S(2)}) collective-permute-start(bf16[2,63,896]{2,1,0:T(8,128)(2,1)S(1)} %slice.161), channel_id=1, source_target_pairs={{1,0},{2,1},{3,2},{5,4},{6,5},{7,6},{9,8},{10,9},{11,10},{13,12},{... | collective-permute-start | bytes 677384 | tf_op jit(solution)/shard_map/ppermute | solution.py:25
  242.8 4.6 collective-permute-start.1
  251.2 23.0 %copy-start.11 = (f32[512,896]{1,0:T(8,128)}, f32[512,896]{1,0:T(8,128)S(1)}, u32[]{:S(2)}) copy-start(f32[512,896]{1,0:T(8,128)S(1)} %get-tuple-element.52) | copy-start | bytes 5505028
  258.9 9.2 %copy-start.49 = (f32[512,3584]{1,0:T(8,128)}, f32[512,3584]{1,0:T(8,128)S(1)}, u32[]{:S(2)}) copy-start(f32[512,3584]{1,0:T(8,128)S(1)} %fusion.14) | copy-start | bytes 22020100
  276.9 5.8 collective-permute-start.2
  305.4 9.9 %copy-start.13 = (f32[512,896]{1,0:T(8,128)S(1)}, f32[512,896]{1,0:T(8,128)}, u32[]{:S(2)}) copy-start(f32[512,896]{1,0:T(8,128)} %copy-done.12) | copy-start | bytes 5505028
  305.4 9.9 %copy-start.25 = (bf16[4,224,896]{2,1,0:T(8,128)(2,1)S(1)}, bf16[4,224,896]{2,1,0:T(8,128)(2,1)}, u32[]{:S(2)}) copy-start(bf16[4,224,896]{2,1,0:T(8,128)(2,1)} %get-tuple-element.42) | copy-start | bytes 4816900
  306.6 8.5 %collective-permute-start.3 = (bf16[2,63,896]{2,1,0:T(8,128)(2,1)S(1)}, bf16[2,63,896]{2,1,0:T(8,128)(2,1)S(1)}, u32[]{:S(2)}, u32[]{:S(2)}) collective-permute-start(bf16[2,63,896]{2,1,0:T(8,128)(2,1)S(1)} %slice.174), channel_id=1, source_target_pairs={{0,1},{1,2},{2,3},{4,5},{5,6},{6,7},{8,9},{9,10},{10,11},{12,13},{... | collective-permute-start | bytes 677384 | tf_op jit(solution)/shard_map/ppermute | solution.py:25
  366.8 202.5 %reduce-scatter.8.cloned.1.call-start = ((), (), s32[]{:S(2)}) async-start(), calls=%async_computation.6 | async-start | bytes 13246464 | tf_op jit(solution)/shard_map/reduce_scatter | solution.py:446
  403.3 323.7 %reduce-scatter.6.cloned.1.call-start = ((), (), s32[]{:S(2)}) async-start(), calls=%async_computation.5 | async-start | bytes 13246464 | tf_op jit(solution)/shard_map/reduce_scatter | solution.py:446
  412.9 9.8 %copy-start.44 = (bf16[8,256,896]{2,1,0:T(8,128)(2,1)S(1)}, bf16[8,256,896]{2,1,0:T(8,128)(2,1)}, u32[]{:S(2)}) copy-start(bf16[8,256,896]{2,1,0:T(8,128)(2,1)} %get-tuple-element.24) | copy-start | bytes 11010052
  436.6 11.3 %copy-start.19 = (bf16[4,224,896]{2,1,0:T(8,128)(2,1)S(1)}, bf16[4,224,896]{2,1,0:T(8,128)(2,1)}, u32[]{:S(2)}) copy-start(bf16[4,224,896]{2,1,0:T(8,128)(2,1)} %get-tuple-element.41) | copy-start | bytes 4816900
  436.6 11.3 %copy-start.45 = (bf16[8,256,896]{2,1,0:T(8,128)(2,1)S(1)}, bf16[8,256,896]{2,1,0:T(8,128)(2,1)}, u32[]{:S(2)}) copy-start(bf16[8,256,896]{2,1,0:T(8,128)(2,1)} %get-tuple-element.24) | copy-start | bytes 11010052
  513.4 215.7 %copy-start.1 = (f32[32,14]{0,1:T(8,128)S(1)}, f32[32,14]{0,1:T(8,128)}, u32[]{:S(2)}) copy-start(f32[32,14]{0,1:T(8,128)} %param.15) | copy-start | bytes 5380
  (36 other events, 151.3 us)
Sparse Core Ops, SparseCore 0:
  9.6 34.1 all-gather.9
  47.3 101.4 all-gather.7
  151.7 97.7 all-gather.5
  366.9 42.6 reduce-scatter.3
  411.9 157.4 reduce-scatter.7
  571.6 155.4 reduce-scatter.5

commit v2 on v1

--- a/solution.py
+++ b/solution.py
@@ -1,3 +1,5 @@
+import functools
+
 import jax
 import jax.numpy as jnp
 from jax import lax
@@ -17,12 +19,461 @@
 F32 = jnp.float32
 BF16 = jnp.bfloat16
 AXES = ("dp", "fsdp")
+MESH = pl.DeviceIdType.MESH
+
+
+def layout_of(sizes):
+    dp, fsdp = sizes
+    known = {
+        (8, 4): (("fsdp", 1, 2), ("fsdp", 2, 2), ("dp", 1, 2), ("dp", 2, 4)),
+        (64, 4): (("dp", 1, 2), ("fsdp", 1, 4), ("dp", 16, 4), ("dp", 2, 8)),
+    }
+    if sizes in known:
+        return known[sizes]
+    if fsdp % 2 == 0:
+        return (("fsdp", 1, 2), ("fsdp", 2, fsdp // 2), ("dp", 1, 1), ("dp", 1, dp))
+    return (("dp", 1, 2), ("fsdp", 1, fsdp), ("dp", 2, 1), ("dp", 2, dp // 2))
+
+
+def pick(values, index):
+    total = jnp.int32(values[0])
+    for i in range(1, len(values)):
+        total = jnp.where(index == i, jnp.int32(values[i]), total)
+    return total
+
+
+def by_distance(position, places, k):
+    table = [sorted(range(places), key=lambda q, p=p: (abs(q - p), q))[k] for p in range(places)]
+    return pick(table, position)
+
+
+class Place:
+    def __init__(self, layout):
+        self.layout = layout
+        self.core_dim, self.y_dim, self.x_dim, self.z_dim = layout
+        self.swaps = self.x_dim[2] == self.y_dim[2]
+        self.index = {axis: lax.axis_index(axis).astype(jnp.int32) for axis in AXES}
+        where = [(self.index[axis] // step) % places for axis, step, places in layout]
+        self.core, self.y, self.x, self.z = where
+        self.a, self.b = self.roles(self.core, self.x, self.y)
+        self.na, self.nb, self.nz = self.x_dim[2], self.y_dim[2], self.z_dim[2]
+        self.cores = self.core_dim[2]
+
+    def roles(self, core, first, second):
+        if not self.swaps:
+            return first, second
+        return first + core * (second - first), second + core * (first - second)
+
+    def coords(self, core, z, a, b):
+        x, y = self.roles(core, a, b)
+        total = {axis: jnp.int32(0) for axis in AXES}
+        for (axis, step, _), at in zip(self.layout, (core, y, x, z), strict=True):
+            total[axis] = total[axis] + at * step
+        return total
+
+    def device(self, core=None, z=None, a=None, b=None, roles_of=None):
+        core_at = self.core if core is None else core
+        if core is not None and roles_of is None:
+            x, y = self.x, self.y
+            total = {axis: jnp.int32(0) for axis in AXES}
+            for (axis, step, _), at in zip(self.layout, (core_at, y, x, self.z), strict=True):
+                total[axis] = total[axis] + at * step
+            return total
+        return self.coords(
+            core_at, self.z if z is None else z, self.a if a is None else a, self.b if b is None else b
+        )
+
+    def block(self, core, z, a, b):
+        at = self.coords(core, z, a, b)
+        return at["dp"] * lax.axis_size("fsdp") + at["fsdp"]
+
+    def neighbours(self):
+        found = []
+        for name, places in (("z", self.nz), ("a", self.na), ("b", self.nb)):
+            at = getattr(self, name)
+            for move in (-1, 1):
+                if places == 1:
+                    continue
+                if places == 2:
+                    if move == 1:
+                        found.append((None, self.device(**{name: 1 - at})))
+                    continue
+                found.append(((at + move >= 0) & (at + move < places), self.device(**{name: at + move})))
+        if self.cores == 2:
+            found.append((None, self.device(core=1 - self.core)))
+        return found
+
+
+def when(condition, action):
+    if condition is None:
+        action()
+    else:
+        pl.when(condition)(action)
+
+
+def meet(place):
+    barrier = pltpu.get_barrier_semaphore()
+    count = jnp.int32(0)
+    for condition, device in place.neighbours():
+        when(
+            condition,
+            lambda device=device: pl.semaphore_signal(barrier, inc=1, device_id=device, device_id_type=MESH),
+        )
+        count = count + (1 if condition is None else condition.astype(jnp.int32))
+    pl.semaphore_wait(barrier, count)
+
+
+def part_of(ref, block, size):
+    if size is None:
+        return ref.at[block]
+    return ref.at[pl.ds(pl.multiple_of(block * size, size), size)]
+
+
+def gather_steps(layout, arrays, side_work):
+    place = Place(layout)
+    meet(place)
+    sent = []
+    a, b, z, core = place.a, place.b, place.z, place.core
+    sibling = place.device(core=1 - core)
+
+    def send(block, kind, slot, device, condition, own):
+        for x_ref, out_ref, size, send_sem, recv_sem, _ in arrays:
+            copy = pltpu.make_async_remote_copy(
+                src_ref=x_ref if own else part_of(out_ref, block, size),
+                dst_ref=part_of(out_ref, block, size),
+                send_sem=send_sem.at[kind, slot],
+                recv_sem=recv_sem.at[block],
+                device_id=device,
+                device_id_type=MESH,
+            )
+            when(condition, copy.start)
+            sent.append((condition, copy))
+
+    def arrived(block):
+        for x_ref, out_ref, size, send_sem, recv_sem, _ in arrays:
+            pltpu.make_async_remote_copy(
+                src_ref=x_ref, dst_ref=part_of(out_ref, block, size), send_sem=send_sem.at[0, 0], recv_sem=recv_sem.at[block],
+                device_id=sibling, device_id_type=MESH,
+            ).wait_recv()
+
+    def along(name, at, places, block, slot, origin, kinds, own=False):
+        if places == 1:
+            return
+        if places == 2:
+            if origin is None:
+                send(block, kinds[0], slot, place.device(**{name: 1 - at}), None, own)
+            return
+        if origin is None:
+            for move, kind in ((-1, kinds[0]), (1, kinds[1])):
+                inside = (at + move >= 0) & (at + move < places)
+                send(block, kind, slot, place.device(**{name: at + move}), inside, own)
+            return
+        move = jnp.where(origin < at, 1, -1)
+        inside = (at + move >= 0) & (at + move < places)
+        send(block, kinds[0], slot, place.device(**{name: at + move}), inside, own)
+
+    mine = place.block(core, z, a, b)
+    keeps = []
+    slot = 0
+    along("z", z, place.nz, mine, slot, None, (0, 1), True)
+    along("a", a, place.na, mine, slot, None, (2, 3), True)
+    along("b", b, place.nb, mine, slot, None, (4, 5), True)
+    if place.cores == 2:
+        send(mine, 6, slot, sibling, None, True)
+    for x_ref, out_ref, size, _, _, own_sem in arrays:
+        keep = pltpu.make_async_copy(x_ref, part_of(out_ref, mine, size), own_sem)
+        keep.start()
+        keeps.append(keep)
+    visits = []
+    for kz in range(place.nz):
+        visits.append((kz, 0, 0))
+        if kz:
+            visits += [(kz - 1, ka, 0) for ka in range(1, place.na)]
+    visits += [(place.nz - 1, ka, 0) for ka in range(1, place.na)]
+    visits += [(kz, ka, kb) for kb in range(1, place.nb) for ka in range(place.na) for kz in range(place.nz)]
+    side_work = list(side_work)
+    for kz, ka, kb in visits[1:]:
+        if side_work:
+            side_work.pop(0)()
+        slot += 1
+        zb, ab, bb = by_distance(z, place.nz, kz), by_distance(a, place.na, ka), by_distance(b, place.nb, kb)
+        block = place.block(core, zb, ab, bb)
+        arrived(block)
+        if kb == 0 and ka == 0:
+            along("z", z, place.nz, block, slot, zb, (0, 1))
+        if kb == 0:
+            along("a", a, place.na, block, slot, None if ka == 0 else ab, (2, 3))
+        along("b", b, place.nb, block, slot, None if kb == 0 else bb, (4, 5))
+        if place.cores == 2:
+            send(block, 6, slot, sibling, None, False)
+    for action in side_work:
+        action()
+    if place.cores == 2:
+        for bb in range(place.nb):
+            for ab in range(place.na):
+                for zb in range(place.nz):
+                    arrived(place.block(1 - core, jnp.int32(zb), jnp.int32(ab), jnp.int32(bb)))
+    for condition, copy in sent:
+        when(condition, copy.wait_send)
+    for keep in keeps:
+        keep.wait()
+
+
+def gather_with_tiles(layout, blocks, lines, rows):
+    n = 1
+    for _, _, places in layout:
+        n *= places
+    per_core = n // layout[0][2]
+    count = len(blocks)
+    heads, reach_count, _, width = lines.shape
+    sizes = [block.shape[0] if block.shape[0] % 16 == 0 else None for block in blocks]
+
+    def body(*refs):
+        xs, line_ref, outs, tile_ref = refs[:count], refs[count], refs[count + 1 : 2 * count + 1], refs[2 * count + 1]
+        tile_buf, tile_sem = refs[2 * count + 2 : 2 * count + 4]
+        sems = refs[2 * count + 4 :]
+        arrays = [(xs[i], outs[i], sizes[i], *sems[3 * i : 3 * i + 3]) for i in range(count)]
+
+        def tile_copy(h):
+            return pltpu.make_async_copy(tile_buf.at[h], tile_ref.at[h], tile_sem.at[h])
+
+        def spread(h):
+            for d in range(reach_count):
+                wide = jnp.broadcast_to(line_ref[h, d], (rows, width))
+                tile_buf[h, d] = pltpu.roll(wide, 0, 1, stride=1, stride_axis=0)[:, :rows]
+            tile_copy(h).start()
+
+        gather_steps(layout, arrays, [functools.partial(spread, h) for h in range(heads)])
+        for h in range(heads):
+            tile_copy(h).wait()
+
+    scratch = [pltpu.VMEM((heads, reach_count, rows, rows), F32), pltpu.SemaphoreType.DMA((heads,))]
+    for _ in blocks:
+        scratch += [pltpu.SemaphoreType.DMA((7, per_core)), pltpu.SemaphoreType.DMA((n,)), pltpu.SemaphoreType.DMA]
+    anywhere = pl.BlockSpec(memory_space=pl.ANY)
+    inside = pl.BlockSpec(memory_space=pltpu.VMEM)
+    *gathered, tiles = pl.pallas_call(
+        body,
+        out_shape=[
+            jax.ShapeDtypeStruct((n,) + block.shape if size is None else (n * size,) + block.shape[1:], block.dtype)
+            for block, size in zip(blocks, sizes, strict=True)
+        ]
+        + [jax.ShapeDtypeStruct((heads, reach_count, rows, rows), F32)],
+        in_specs=[inside] * (count + 1),
+        out_specs=[anywhere] * (count + 1),
+        scratch_shapes=scratch,
+        compiler_params=pltpu.CompilerParams(collective_id=1, has_side_effects=True, vmem_limit_bytes=40_000_000),
+        name="gather_all",
+    )(*blocks, lines)
+    return gathered, tiles
+
+
+class Payload:
+    def __init__(self, source, own, sib, line_b, line_a, line_z, load_sem, send_sem, sems):
+        self.source, self.own, self.sib = source, own, sib
+        self.lines = {"b": line_b, "a": line_a, "z": line_z}
+        self.load_sem, self.send_sem, self.sems = load_sem, send_sem, sems
+
+
+def buffers_of(layout, block_shape, dtype):
+    _, (_, _, nb), (_, _, na), (_, _, nz) = layout
+    per_core = nz * na * nb
+    deep = lambda places: 1 if places <= 2 else places + 1
+    vm = lambda *lead: pltpu.VMEM(lead + block_shape, dtype)
+    dma = pltpu.SemaphoreType.DMA
+    counts = {"s": per_core, "b": deep(nb) * nz * na, "a": deep(na) * nz, "z": deep(nz)}
+    return [
+        vm(per_core), vm(per_core), vm(counts["b"]), vm(counts["a"]), vm(counts["z"]),
+        dma((per_core,)), dma((2, per_core)),
+        dma((per_core,)), dma((counts["b"],)), dma((counts["a"],)), dma((counts["z"],)),
+    ]
+
+
+def scatter_steps(layout, payloads, finish):
+    place = Place(layout)
+    a, b, z, core = place.a, place.b, place.z, place.core
+    na, nb, nz = place.na, place.nb, place.nz
+    slot_of = lambda zb, ab, bb: (zb * na + ab) * nb + bb
+    meet(place)
+    sent = []
+
+    def remote(src, dst, send_sem, recv_sem, device):
+        return pltpu.make_async_remote_copy(
+            src_ref=src, dst_ref=dst, send_sem=send_sem, recv_sem=recv_sem, device_id=device, device_id_type=MESH
+        )
+
+    def order(a_at, b_at):
+        found = []
+        for kz in reversed(range(nz)):
+            for kb in reversed(range(nb)):
+                for ka in reversed(range(na)):
+                    found.append((by_distance(z, nz, kz), by_distance(a_at, na, ka), by_distance(b_at, nb, kb)))
+        return found
+
+    sibling = place.device(core=1 - core)
+    own_order = order(a, b)
+    their_a, their_b = (b, a) if place.swaps else (a, b)
+    for (zo, ao, bo), (zt, at, bt) in zip(own_order, order(their_a, their_b), strict=True):
+        for p in payloads:
+            slot = slot_of(zo, ao, bo)
+            pltpu.make_async_copy(p.source.at[place.block(core, zo, ao, bo)], p.own.at[slot], p.load_sem.at[slot]).start()
+            slot = slot_of(zt, at, bt)
+            copy = remote(
+                p.source.at[place.block(1 - core, zt, at, bt)], p.sib.at[slot], p.send_sem.at[0, slot], p.sems["s"].at[slot], sibling
+            )
+            copy.start()
+            sent.append((None, copy))
+
+    waiting = []
+
+    def release():
+        while waiting:
+            condition, copy = waiting.pop(0)
+            when(condition, copy.start)
+            sent.append((condition, copy))
+
+    def add_arrival(p, slot, buffer, sem, at):
+        remote(p.own.at[slot], buffer.at[at], p.send_sem.at[1, slot], sem.at[at], sibling).wait_recv()
+        p.own[slot] = (p.own[slot].astype(F32) + buffer[at].astype(F32)).astype(p.own.dtype)
+
+    def start_sum(zb, ab, bb):
+        for p in payloads:
+            slot = slot_of(zb, ab, bb)
+            pltpu.make_async_copy(p.source.at[place.block(core, zb, ab, bb)], p.own.at[slot], p.load_sem.at[slot]).wait()
+            add_arrival(p, slot, p.sib, p.sems["s"], slot)
+
+    def pass_on(name, at, places, target, inner, inner_count, zb, ab, bb):
+        move = jnp.where(target > at, 1, -1)
+        for p in payloads:
+            slot = slot_of(zb, ab, bb)
+            line, sem = p.lines[name], p.sems[name]
+            if places == 2:
+                there = inner
+            else:
+                outer = (at - move >= 0) & (at - move < places)
+                here = target * inner_count + inner
+                pl.when(outer)(lambda p=p, slot=slot, line=line, sem=sem, here=here: add_arrival(p, slot, line, sem, here))
+                last = (target == at + move) & (move < 0)
+                there = jnp.where(last, places, target) * inner_count + inner
+            waiting.append(
+                (None, remote(p.own.at[slot], line.at[there], p.send_sem.at[1, slot], sem.at[there], place.device(**{name: at + move})))
+            )
+        release()
+
+    def take_in(name, at, places, inner, inner_count, zb, ab, bb):
+        for p in payloads:
+            slot = slot_of(zb, ab, bb)
+            line, sem = p.lines[name], p.sems[name]
+            if places == 1:
+                continue
+            if places == 2:
+                add_arrival(p, slot, line, sem, inner)
+                continue
+            pl.when(at > 0)(lambda p=p, slot=slot, line=line, sem=sem: add_arrival(p, slot, line, sem, at * inner_count + inner))
+            pl.when(at < places - 1)(
+                lambda p=p, slot=slot, line=line, sem=sem: add_arrival(p, slot, line, sem, places * inner_count + inner)
+            )
+
+    def first_stage(zb):
+        for kb in reversed(range(1, nb)):
+            bb = by_distance(b, nb, kb)
+            for ka in reversed(range(na)):
+                ab = by_distance(a, na, ka)
+                start_sum(zb, ab, bb)
+                release()
+                pass_on("b", b, nb, bb, zb * na + ab, nz * na, zb, ab, bb)
+        for ka in reversed(range(na)):
+            start_sum(zb, by_distance(a, na, ka), b)
+            release()
+
+    def second_stage(zb):
+        for ka in reversed(range(1, na)):
+            ab = by_distance(a, na, ka)
+            take_in("b", b, nb, zb * na + ab, nz * na, zb, ab, b)
+            release()
+            pass_on("a", a, na, ab, zb, nz, zb, ab, b)
+        take_in("b", b, nb, zb * na + a, nz * na, zb, a, b)
+        release()
+
+    def third_stage(zb, onward):
+        take_in("a", a, na, zb, nz, zb, a, b)
+        release()
+        if onward:
+            pass_on("z", z, nz, zb, 0, 1, zb, a, b)
+
+    far_first = [by_distance(z, nz, kz) for kz in reversed(range(nz))]
+    for i in range(nz + 2):
+        if i < nz:
+            first_stage(far_first[i])
+        if 0 <= i - 1 < nz:
+            second_stage(far_first[i - 1])
+        if 0 <= i - 2 < nz:
+            third_stage(far_first[i - 2], i - 2 < nz - 1)
+    release()
+    take_in("z", z, nz, 0, 1, z, a, b)
+    mine = slot_of(z, a, b)
+    for p, done in zip(payloads, finish, strict=True):
+        done(p.own[mine])
+    for condition, copy in sent:
+        when(condition, copy.wait_send)
+
+
+def scatter_all(layout, blocks, collective_id):
+    count = len(blocks)
+
+    def body(*refs):
+        sources, outs, rest = refs[:count], refs[count : 2 * count], refs[2 * count :]
+        payloads, finish = [], []
+        for i in range(count):
+            own, sib, line_b, line_a, line_z, load, send, s, sb, sa, sz = rest[11 * i : 11 * (i + 1)]
+            payloads.append(
+                Payload(sources[i], own, sib, line_b, line_a, line_z, load, send, {"s": s, "b": sb, "a": sa, "z": sz})
+            )
+
+            def done(value, i=i):
+                outs[i][...] = value.astype(F32)
+
+            finish.append(done)
+        scatter_steps(layout, payloads, finish)
+
+    scratch = []
+    for block in blocks:
+        scratch += buffers_of(layout, block.shape[1:], block.dtype)
+    return pl.pallas_call(
+        body,
+        out_shape=[jax.ShapeDtypeStruct(block.shape[1:], F32) for block in blocks],
+        in_specs=[pl.BlockSpec(memory_space=pl.ANY)] * count,
+        out_specs=[pl.BlockSpec(memory_space=pltpu.VMEM)] * count,
+        scratch_shapes=scratch,
+        compiler_params=pltpu.CompilerParams(
+            collective_id=collective_id, has_side_effects=True, vmem_limit_bytes=60_000_000
+        ),
+        name="scatter_all",
+    )(*blocks)
 
 
 def from_behind(array, axis, by):
     length = lax.axis_size(axis)
     pairs = [(i, i + by) for i in range(length) if 0 <= i + by < length]
     return lax.ppermute(array, axis, pairs)
+
+
+def sum_of_group(parts, place):
+    group = parts.shape[0]
+    if group & (group - 1):
+        return lax.psum_scatter(parts, "fsdp", scatter_dimension=0, tiled=True)[0].astype(F32)
+    step = 1
+    while step < group:
+        halves = parts.reshape((parts.shape[0] // 2, 2) + parts.shape[1:])
+        bit = (place // step) % 2
+        away = lax.dynamic_index_in_dim(halves, 1 - bit, axis=1, keepdims=False)
+        kept = lax.dynamic_index_in_dim(halves, bit, axis=1, keepdims=False)
+        came = lax.ppermute(away, "fsdp", [(i, i ^ step) for i in range(group)])
+        parts = kept.astype(F32) + came.astype(F32)
+        step *= 2
+        if step < group:
+            parts = parts.astype(BF16)
+    return parts[0]
 
 
 def product(left_side, right_side):
@@ -86,7 +537,7 @@
     return values.astype(F32).T.astype(BF16)
 
 
-def bias_tiles(rel_table, rows, reach):
+def bias_lines(rel_table, rows, reach):
     heads = rel_table.shape[1]
     width = 2 * rows
     count = 2 * reach + 1
@@ -96,21 +547,7 @@
     ids = bucket_of(far[:, None] - behind[None, :])
     hot = (ids[:, :, None] == jnp.arange(rel_table.shape[0], dtype=jnp.int32)).astype(F32)
     lines = jnp.einsum("dwb,bh->hdw", hot, rel_table, precision=lax.Precision.HIGHEST)
-    lines = lines.reshape(heads, count, 1, width)
-
-    def spread(line_ref, tile_ref):
-        for d in range(count):
-            wide = jnp.broadcast_to(line_ref[0, d], (rows, width))
-            tile_ref[0, d] = pltpu.roll(wide, 0, 1, stride=1, stride_axis=0)[:, :rows]
-
-    return pl.pallas_call(
-        spread,
-        out_shape=jax.ShapeDtypeStruct((heads, count, rows, rows), F32),
-        grid=(heads,),
-        in_specs=[pl.BlockSpec((1, count, 1, width), lambda i: (i, 0, 0, 0))],
-        out_specs=pl.BlockSpec((1, count, rows, rows), lambda i: (i, 0, 0, 0)),
-        name="bias_tiles",
-    )(lines)
+    return lines.reshape(heads, count, 1, width)
 
 
 def tile_at(block, place, reach):
@@ -374,18 +811,21 @@
     share = attn_weights.shape[0]
 
     gather = lambda array, axes: lax.all_gather(array, axes, axis=0, tiled=True)
-    vector_row = jnp.pad(vectors.reshape(1, -1), ((0, 15), (0, width - vectors.shape[0])))
+    layout = layout_of((lax.axis_size("dp"), group))
+    vector_rows = -(-vectors.shape[0] // 2048) * 16
+    vector_block = jnp.pad(vectors, (0, vector_rows * 128 - vectors.shape[0])).reshape(vector_rows, 128)
     hidden_all = gather(hidden[None], "fsdp")
-    first_full = gather(jnp.concatenate([attn_weights, vector_row], axis=0)[None], AXES)
-    ffw_full = gather(ffw_weights, AXES)
-    matrices = first_full[:, :share].reshape(8, width, width)
-    vector_full = first_full[:, share, : vectors.shape[0]].reshape(-1).astype(F32)
+    (attn_full, vector_full), tiles = gather_with_tiles(
+        layout, [attn_weights, vector_block], bias_lines(rel_table, rows, reach), rows
+    )
+    ffw_full = gather(lax.optimization_barrier((ffw_weights, vector_full))[0], AXES)
+    matrices = attn_full.reshape(8, width, width)
+    vector_full = vector_full.reshape(-1, vector_rows * 128)[:, : vectors.shape[0]].reshape(-1).astype(F32)
     w_input, w_output = ffw_full[:FF], ffw_full[FF:]
     bias_input = vector_full[:FF]
     gains = vector_full[FF : FF + 3 * width].reshape(3, width)
     bias_output = vector_full[FF + 3 * width :]
 
-    tiles = bias_tiles(rel_table, rows, reach)
     key_pos = jnp.arange(length, dtype=jnp.int32)
     query_pos = place * rows + jnp.arange(rows, dtype=jnp.int32)
     key_piece = piece_labels(key_pos, piece_starts)
@@ -444,7 +884,9 @@
     grad_pre_low = grad_pre.astype(BF16)
     grad_w_input = transposed_times(grad_pre_low, normed_three).astype(BF16)
     scatter = lambda array: lax.psum_scatter(array, AXES, scatter_dimension=0, tiled=True)
-    ffw_sum = scatter(jnp.concatenate([grad_w_input, grad_w_output], axis=0))
+    ffw_step = jnp.stack([grad_w_input, grad_w_output]).reshape(2 * FF, width)
+    ffw_step, grad_pre_low = lax.optimization_barrier((ffw_step, grad_pre_low))
+    ffw_sum = scatter(ffw_step)
     grad_norm_three = product(grad_pre_low, w_input)
     grad_gain_three = jnp.sum(grad_norm_three * second_sum * scale_three, axis=0)
     grad_second = grad_out + norm_back(second_sum, scale_three, gains[2], grad_norm_three)
@@ -473,9 +915,7 @@
     partial_one = (
         times_transposed(grad_keys, matrices[1]) + times_transposed(grad_values, matrices[2])
     ).astype(BF16)
-    joined = lax.psum_scatter(
-        partial_one.reshape(group, tokens, width), "fsdp", scatter_dimension=0, tiled=True
-    ).reshape(tokens, width)
+    joined = sum_of_group(partial_one.reshape(group, tokens, width), place)
     grad_cross_key_mat = transposed_times(near_flat, grad_cross_keys)
     grad_cross_value_mat = transposed_times(near_flat, grad_cross_values)
     near_grad = times_transposed(grad_cross_keys, matrices[5]) + times_transposed(
@@ -495,34 +935,39 @@
     hot = (bucket_of(between)[..., None] == jnp.arange(buckets, dtype=jnp.int32)).astype(F32)
     table_step = jnp.einsum("hjsl,jslb->bh", diagonal, hot, precision=lax.Precision.HIGHEST)
 
-    attn_sum = scatter(
-        jnp.concatenate(
-            [
-                part.astype(BF16)
-                for part in (
-                    grad_query_mat,
-                    grad_key_mat,
-                    grad_value_mat,
-                    grad_self_out,
-                    grad_cross_query_mat,
-                    grad_cross_key_mat,
-                    grad_cross_value_mat,
-                    grad_cross_out,
-                )
-            ],
-            axis=0,
-        )
+    attn_step = jnp.stack(
+        [
+            part.astype(BF16)
+            for part in (
+                grad_query_mat,
+                grad_key_mat,
+                grad_value_mat,
+                grad_self_out,
+                grad_cross_query_mat,
+                grad_cross_key_mat,
+                grad_cross_value_mat,
+                grad_cross_out,
+            )
+        ]
     )
     vector_step = jnp.concatenate(
         [grad_bias_input, grad_gain_one, grad_gain_two, grad_gain_three, grad_bias_output]
-    )
-    vector_sum = lax.psum_scatter(vector_step, AXES, scatter_dimension=0, tiled=True)
-    table_sum = lax.psum(table_step, AXES)
+    ).reshape(-1, vectors.shape[0])
+    devices = vector_step.shape[0]
+    small = jnp.concatenate(
+        [vector_step, jnp.broadcast_to(table_step.reshape(1, -1), (devices, buckets * heads))], axis=1
+    )
+    small_rows = -(-small.shape[1] // 1024) * 8
+    small = jnp.pad(small, ((0, 0), (0, small_rows * 128 - small.shape[1]))).reshape(devices, small_rows, 128)
+    attn_sum, small_sum = scatter_all(layout, [attn_step.reshape(devices, share, width), small], 2)
+    small_sum = small_sum.reshape(-1)
+    vector_sum = small_sum[: vectors.shape[0]]
+    table_sum = small_sum[vectors.shape[0] : vectors.shape[0] + buckets * heads].reshape(buckets, heads)
     return (
         output.reshape(count, rows, width),
         hidden_grad.reshape(count, rows, width),
         near_grad.reshape(count, spans, span_keys, width),
-        attn_sum.astype(F32),
+        attn_sum,
         ffw_sum.astype(F32),
         vector_sum,
         table_sum,

time: 746 us -> 525 us (0.70)
  waiting for transfers between devices: 333 us -> 11.1 us
  Pallas kernels: 101 us -> 237 us
  blocking collectives: 47.5 us -> 0 us
  matrix products: 150 us -> 172 us
  other arithmetic: 41.3 us -> 28.1 us
    reduce_scatter x2 -> x1, waiting for transfers between devices: 208 us -> 0.01 us  [per_device(): lax.psum_scatter(array, AXES, scatter_dimension=0, tiled=True)]
    pallas_call x1 -> x2, Pallas kernels: 11.9 us -> 150 us  [the longest x1 80.9 us: gather_with_tiles(): pl.pallas_call(body, out_shape=[jax.ShapeDtypeStruct((n,) + block.shape i...]
    all_gather x3 -> x2, waiting for transfers between devices: 119 us -> 0.01 us  [per_device(): gather = lambda array, axes: lax.all_gather(array, axes, axis=0, tiled=True)]
    unnamed x1 -> x0, blocking collectives: 47.5 us -> none
    concatenate x2 -> x1, other arithmetic: 22 us -> 0.01 us  [per_device(): jnp.concatenate([vector_step, jnp.broadcast_to(table_step.reshape(1, -1),...]
    dot_general x10, matrix products: 50.3 us -> 63.3 us  [times_transposed(): lax.dot_general(left_side, right_side, (((1,), (1,)), ((), ())), preferre...]
    dot_general x10, matrix products: 50.2 us -> 61.5 us  [product(): return jnp.dot(left_side, right_side, preferred_element_type=F32)]
    ppermute x0 -> x2, waiting for transfers between devices: none -> 10.3 us  [sum_of_group(): came = lax.ppermute(away, 'fsdp', [(i, i ^ step) for i in range(group)])]
  transfers between devices with their start and end apart: 10 -> 9, of which waited for: 5 -> 1; matrix products, arithmetic and copies ran while one was open for 24% -> 36% of each run, Pallas kernels for 6% -> 46%
where the time goes in v2:
time: 525 us; the launch traced here: 518 us
  Pallas kernels  237 us (45%)
  matrix products  172 us (33%)
  local copies, waits for them, and re-layouts  38.4 us (7%)
  other arithmetic  28.1 us (5%)
  starting transfers between devices  16.5 us (3%)
  between operations  14.9 us (3%)
  waiting for transfers between devices  11.1 us (2%)
    pallas_call x1, Pallas kernels, gather_with_tiles(): pl.pallas_call(body, out_shape=[jax.ShapeDtypeStruct((n,) + block.shape i...  80.9 us
    pallas_call x1, Pallas kernels, scatter_all(): pl.pallas_call(body, out_shape=[jax.ShapeDtypeStruct(block.shape[1:], F32...  68.8 us
    dot_general x10, matrix products, times_transposed(): lax.dot_general(left_side, right_side, (((1,), (1,)), ((), ())), preferre...  63.3 us
    dot_general x10, matrix products, product(): return jnp.dot(left_side, right_side, preferred_element_type=F32)  61.5 us
    dot_general x10, matrix products, transposed_times(): lax.dot_general(left_side, right_side, (((0,), (0,)), ((), ())), preferre...  45.9 us
    pallas_call x1, Pallas kernels, self_attention_back(): pl.pallas_call(body, grid_spec=grid_spec, out_shape=[jax.ShapeDtypeStruct...  32.9 us
    pallas_call x1, Pallas kernels, self_attention(): pl.pallas_call(body, grid_spec=grid_spec, out_shape=[jax.ShapeDtypeStruct...  21.9 us
    pallas_call x1, Pallas kernels, span_attention_back(): pl.pallas_call(body, grid=(blocks,), in_specs=[q_spec, k_spec, k_spec, q_...  21.6 us
  transfers between devices with their start and end apart: 9, of which 1 were waited for; matrix products, arithmetic and copies ran while one was open for 36% of the time, Pallas kernels for 46%

profile of v2, /device:TPU:0, one launch (start us, length us, event | category | flops | bytes accessed | tf_op | source)
XLA Modules:
  0.0 518.1 jit_solution(959325803724743950)
XLA Ops:
  10.2 80.9 %gather_all.1 = (bf16[7168,896]{1,0:T(8,128)(2,1)S(1)}, bf16[512,128]{1,0:T(8,128)(2,1)S(1)}, f32[14,5,256,256]{3,2,1,0:T(8,128)}) custom-call(bf16[224,896]{1,0:T(8,128)(2,1)S(1)} %copy-done.2, bf16[16,128]{1,0:T(8,128)(2,1)S(1)} %pad_bitcast_fusion.1.refs_1_, f32[14,5,1,512]{3,2,1,0:T(1,128)S(1)} %copy.39.refs_2_), custom_call_target="tpu_custom_call" | custom-call | tf_op jit(solution)/shard_map/gather_all/pallas_call | solution.py:255
  104.5 7.0 %convert_bitcast_fusion.1 = bf16[2048,896]{0,1:T(8,128)(2,1)} fusion(bf16[2048,896]{1,0:T(8,128)(2,1)S(1)} %bitcast.211, bf16[7168,896]{1,0:T(8,128)(2,1)} %copy-done.3), kind=kOutput, calls=%fused_computation.30 | convolution fusion | flops 3290169344 | bytes 8945664 | tf_op jit(solution)/shard_map/dot_general | solution.py:480
  116.0 7.2 %convolution_convert_fusion.3 = bf16[2048,896]{1,0:T(8,128)(2,1)} fusion(bf16[2048,896]{1,0:T(8,128)(2,1)S(1)} %fusion.7, bf16[7168,896]{1,0:T(8,128)(2,1)} %copy-done.3), kind=kOutput, calls=%fused_computation.33 | convolution fusion | flops 3290169344 | bytes 8945664 | tf_op jit(solution)/shard_map/dot_general | solution.py:480
  123.2 7.5 %convolution_convert_fusion.2 = bf16[2048,896]{1,0:T(8,128)(2,1)} fusion(bf16[2048,896]{1,0:T(8,128)(2,1)S(1)} %fusion.7, bf16[7168,896]{1,0:T(8,128)(2,1)} %copy-done.3), kind=kOutput, calls=%fused_computation.32 | convolution fusion | flops 3290169344 | bytes 8945664 | tf_op jit(solution)/shard_map/dot_general | solution.py:480
  130.7 21.9 %self_attention.1 = (bf16[2,256,896]{2,1,0:T(8,128)(2,1)}, f32[7,2,128,256]{3,2,1,0:T(8,128)}, f32[7,4,256]{2,1,0:T(4,128)}) custom-call(s32[1]{0:T(128)} %bitcast.1.place_ref, bf16[2,256,896]{2,1,0:T(8,128)(2,1)} %bitcast.200, bf16[4,2,256,896]{3,2,1,0:T(8,128)(2,1)} %bitcast.186, bf16[4,2,256,896]{3,2,1,0:T(8,128)(2,1)} %bitcast.188, ...), custom_call_target="tpu_custom_call" | custom-call | flops 7516192768 | bytes 30000000 | tf_op jit(solution)/shard_map/self_attention/pallas_call | solution.py:607
  159.8 7.1 %convert_bitcast_fusion = bf16[2048,896]{0,1:T(8,128)(2,1)} fusion(bf16[2048,896]{1,0:T(8,128)(2,1)S(1)} %bitcast.212, bf16[7168,896]{1,0:T(8,128)(2,1)} %copy-done.3), kind=kOutput, calls=%fused_computation.29 | convolution fusion | flops 3290169344 | bytes 8945664 | tf_op jit(solution)/shard_map/dot_general | solution.py:480
  172.9 6.0 %copy.41 = bf16[2048,896]{1,0:T(8,128)(2,1)} copy(bf16[2048,896]{0,1:T(8,128)(2,1)} %convert_bitcast_fusion) | data formatting | bytes 7340032 | tf_op jit(solution)/shard_map/convert_element_type | solution.py:849
  180.2 10.6 %span_attention.1 = bf16[8,64,896]{2,1,0:T(8,128)(2,1)} custom-call(bf16[8,64,896]{2,1,0:T(8,128)(2,1)} %bitcast.178, bf16[8,256,896]{2,1,0:T(8,128)(2,1)} %bitcast.170, bf16[8,256,896]{2,1,0:T(8,128)(2,1)} %bitcast.172), custom_call_target="tpu_custom_call" | custom-call | flops 1879048192 | bytes 12000000 | tf_op jit(solution)/shard_map/span_attention/pallas_call | solution.py:750
  201.3 10.6 %fusion.15 = f32[512,3584]{1,0:T(8,128)} fusion(bf16[7168,896]{1,0:T(8,128)(2,1)} %all-gather.4.cloned.1.call-done, f32[512,896]{1,0:T(8,128)} %get-tuple-element.84, f32[896]{0:T(1024)S(1)} %slice.138, f32[512]{0:T(512)S(1)} %add_rsqrt_fusion.1), kind=kOutput, calls=%fused_computation.25 | convolution fusion | flops 3289710592 | bytes 15603200 | tf_op jit(solution)/shard_map/dot_general | solution.py:484
  211.9 8.8 %fusion.9 = bf16[1,3584,896]{2,1,0:T(8,128)(2,1)S(1)} fusion(bf16[512,896]{1,0:T(8,128)(2,1)S(1)} %bitcast.180, f32[512,3584]{1,0:T(8,128)} %fusion.15, f32[3584]{0:T(1024)S(1)} %slice.141), kind=kOutput, calls=%fused_computation.19 | convolution fusion | flops 3309895680 | bytes 14694400 | tf_op jit(solution)/shard_map/dot_general | solution.py:488
  220.8 11.2 %fusion.100 = (f32[3584]{0:T(1024)S(1)}, bf16[512,3584]{1,0:T(8,128)(2,1)}) fusion(f32[512,3584]{1,0:T(8,128)} %fusion.15, f32[3584]{0:T(1024)S(1)} %slice.141, bf16[512,896]{1,0:T(8,128)(2,1)S(1)} %bitcast.181, bf16[7168,896]{1,0:T(8,128)(2,1)S(1)} %bitcast.210), kind=kOutput, calls=%fused_computation.198 | convolution fusion | flops 3326865920 | bytes 18380800 | tf_op jit(solution)/shard_map/dot_general | solution.py:484
  231.9 6.4 %fusion.8 = bf16[1,3584,896]{2,1,0:T(8,128)(2,1)S(1)} fusion(bf16[512,3584]{1,0:T(8,128)(2,1)} %get-tuple-element.30, f32[512,896]{1,0:T(8,128)S(1)} %copy-done.7, f32[896]{0:T(1024)S(1)} %slice.138, f32[512]{0:T(512)S(1)} %add_rsqrt_fusion.1), kind=kOutput, calls=%fused_computation.18 | convolution fusion | flops 3292921856 | bytes 11933184 | tf_op jit(solution)/shard_map/dot_general | solution.py:488
  244.3 6.3 %copy.44 = f32[4,2,256,896]{2,3,1,0:T(8,128)} copy(bf16[4,2,256,896]{3,2,1,0:T(8,128)(2,1)} %bitcast.169) | data formatting | bytes 11010048 | tf_op jit(solution)/shard_map/convert_element_type | solution.py:840
  250.6 8.7 %multiply_reduce_fusion.1 = (f32[896]{0:T(1024)S(1)}, f32[512]{0:T(512)S(1)}, f32[512,896]{1,0:T(8,128)S(1)}) fusion(f32[512,896]{1,0:T(8,128)} %get-tuple-element.84, f32[512]{0:T(512)S(1)} %add_rsqrt_fusion.1, f32[896]{0:T(1024)S(1)} %slice.138, bf16[512,3584]{1,0:T(8,128)(2,1)} %get-tuple-element.30, bf16[7168,896]{1,0:T(8,128)(2,1)} %all-gather.4.cloned.1.call-done), kind=kOutput, calls=%fused_computation.61 | convolution fusion | flops 3291085312 | bytes 13773824 | tf_op jit(solution)/shard_map/dot_general | solution.py:480
  265.4 10.6 %add_convert_fusion.1 = bf16[512,896]{1,0:T(8,128)(2,1)} fusion(f32[512,896]{1,0:T(8,128)S(1)} %copy-done.8, bf16[7168,896]{1,0:T(8,128)(2,1)} %all-gather.4.cloned.1.call-done, f32[896]{0:T(1024)S(1)} %slice.144, f32[512,3584]{1,0:T(8,128)} %fusion.15, f32[3584]{0:T(1024)S(1)} %slice.141), kind=kOutput, calls=%fused_computation.68 | convolution fusion | flops 3308060672 | bytes 16532992 | tf_op jit(solution)/shard_map/dot_general | solution.py:480
  277.1 21.6 %span_attention_back.1 = (bf16[8,64,896]{2,1,0:T(8,128)(2,1)}, bf16[8,256,896]{2,1,0:T(8,128)(2,1)}, bf16[8,256,896]{2,1,0:T(8,128)(2,1)}) custom-call(bf16[8,64,896]{2,1,0:T(8,128)(2,1)} %bitcast.179, bf16[8,256,896]{2,1,0:T(8,128)(2,1)} %bitcast.171, bf16[8,256,896]{2,1,0:T(8,128)(2,1)} %bitcast.173, bf16[8,64,896]{2,1,0:T(8,128)(2,1)} %bitcast.199), custom_call_target="tpu_custom_call" | custom-call | flops 4697620480 | bytes 24000000 | tf_op jit(solution)/shard_map/span_attention_back/pallas_call | solution.py:782
  299.7 7.0 %collective-permute-start.3 = (bf16[2,63,896]{2,1,0:T(8,128)(2,1)S(1)}, bf16[2,63,896]{2,1,0:T(8,128)(2,1)S(1)}, u32[]{:S(2)}, u32[]{:S(2)}) collective-permute-start(bf16[2,63,896]{2,1,0:T(8,128)(2,1)S(1)} %slice.165), channel_id=1, source_target_pairs={{0,1},{1,2},{2,3},{4,5},{5,6},{6,7},{8,9},{9,10},{10,11},{12,13},{... | collective-permute-start | bytes 677384 | tf_op jit(solution)/shard_map/ppermute | solution.py:458
  306.7 7.2 %fusion.38 = f32[2048,896]{1,0:T(8,128)S(1)} fusion(bf16[2048,896]{1,0:T(8,128)(2,1)} %bitcast.220, bf16[7168,896]{1,0:T(8,128)(2,1)} %copy-done.3), kind=kOutput, calls=%fused_computation.95 | convolution fusion | flops 3288334336 | bytes 12615680 | tf_op jit(solution)/shard_map/dot_general | solution.py:484
  314.0 8.3 %convolution_add_fusion = f32[2048,896]{1,0:T(8,128)} fusion(f32[2048,896]{1,0:T(8,128)S(1)} %fusion.38, bf16[2048,896]{1,0:T(8,128)(2,1)S(1)} %bitcast.218, bf16[7168,896]{1,0:T(8,128)(2,1)} %copy-done.3), kind=kOutput, calls=%fused_computation.31 | convolution fusion | flops 3290169344 | bytes 19955712 | tf_op jit(solution)/shard_map/dot_general | solution.py:484
  331.3 32.9 %self_attention_back.1 = (bf16[2,256,896]{2,1,0:T(8,128)(2,1)}, bf16[4,2,256,896]{3,2,1,0:T(8,128)(2,1)}, bf16[4,2,256,896]{3,2,1,0:T(8,128)(2,1)}, f32[14,4,8,512]{3,2,1,0:T(8,128)}) custom-call(s32[1]{0:T(128)} %bitcast.1.place_ref, bf16[2,256,896]{2,1,0:T(8,128)(2,1)} %bitcast.201, bf16[4,2,256,896]{3,2,1,0:T(8,128)(2,1)} %bitcast.187, ...), custom_call_target="tpu_custom_call" | custom-call | flops 18790481920 | bytes 40000000 | tf_op jit(solution)/shard_map/self_attention_back/pallas_call | solution.py:706
  364.2 7.2 %fusion.48 = f32[2048,896]{1,0:T(8,128)S(1)} fusion(bf16[2048,896]{1,0:T(8,128)(2,1)} %bitcast.223, bf16[7168,896]{1,0:T(8,128)(2,1)} %copy-done.3), kind=kOutput, calls=%fused_computation.105 | convolution fusion | flops 3288334336 | bytes 12615680 | tf_op jit(solution)/shard_map/dot_general | solution.py:484
  371.5 6.2 %add_convert_fusion = bf16[2048,896]{1,0:T(8,128)(2,1)S(1)} fusion(f32[2048,896]{1,0:T(8,128)S(1)} %fusion.48, bf16[2048,896]{1,0:T(8,128)(2,1)S(1)} %bitcast.222, bf16[7168,896]{1,0:T(8,128)(2,1)} %copy-done.3), kind=kOutput, calls=%fused_computation.13 | convolution fusion | flops 3292004352 | bytes 16285696 | tf_op jit(solution)/shard_map/dot_general | solution.py:484
  418.5 10.3 %collective-permute-done.5 = bf16[1,512,896]{2,1,0:T(8,128)(2,1)} collective-permute-done((bf16[1,512,896]{2,1,0:T(8,128)(2,1)}, bf16[1,512,896]{2,1,0:T(8,128)(2,1)}, u32[]{:S(2)}, u32[]{:S(2)}) %collective-permute-start.5) | collective-permute-done | bytes 917536 | tf_op jit(solution)/shard_map/ppermute | solution.py:471
  432.9 68.8 %scatter_all.1 = (f32[224,896]{1,0:T(8,128)}, f32[8,128]{1,0:T(8,128)}) custom-call(bf16[32,224,896]{2,1,0:T(8,128)(2,1)} %bitcast.58.refs_0_, f32[32,8,128]{2,1,0:T(8,128)} %bitcast.202), custom_call_target="tpu_custom_call" | custom-call | tf_op jit(solution)/shard_map/scatter_all/pallas_call | solution.py:442
  (214 shorter events, 123.0 us)
Async XLA Ops:
  7.2 91.5 %copy-start.5 = (bf16[2,256,896]{2,1,0:T(8,128)(2,1)S(1)}, bf16[2,256,896]{2,1,0:T(8,128)(2,1)}, u32[]{:S(2)}) copy-start(bf16[2,256,896]{2,1,0:T(8,128)(2,1)} %param.8) | copy-start | bytes 2752516
  7.2 90.9 %copy-start.27 = (s32[2,2]{1,0:T(2,128)S(1)}, s32[2,2]{1,0:T(2,128)}, u32[]{:S(2)}) copy-start(s32[2,2]{1,0:T(2,128)} %param.10) | copy-start | bytes 52
  7.2 104.2 %all-gather.6.cloned.1.call-start = ((), (), s32[]{:S(2)}) async-start(), calls=%async_computation.3 | async-start | bytes 4587520 | tf_op jit(solution)/shard_map/all_gather | solution.py:813
  7.9 193.4 %all-gather.4.cloned.1.call-start = ((), (), s32[]{:S(2)}) async-start(), calls=%async_computation.1 | async-start | bytes 13246464 | tf_op jit(solution)/shard_map/all_gather | solution.py:813
  95.7 412.8 %reduce-scatter.2.cloned.1.call-start = ((), (), s32[]{:S(2)}) async-start(), calls=%async_computation.2 | async-start | bytes 13246464 | tf_op jit(solution)/shard_map/reduce_scatter | solution.py:886
  96.1 18.9 %copy-start.23 = (f32[896]{0:T(1024)}, f32[896]{0:T(1024)S(1)}, u32[]{:S(2)}) copy-start(f32[896]{0:T(1024)S(1)} %slice.122) | copy-start | bytes 10756
  158.5 20.6 %collective-permute-start = (bf16[2,63,896]{2,1,0:T(8,128)(2,1)S(1)}, bf16[2,63,896]{2,1,0:T(8,128)(2,1)S(1)}, u32[]{:S(2)}, u32[]{:S(2)}) collective-permute-start(bf16[2,63,896]{2,1,0:T(8,128)(2,1)S(1)} %slice.155), channel_id=1, source_target_pairs={{1,0},{2,1},{3,2},{5,4},{6,5},{7,6},{9,8},{10,9},{11,10},{13,12},{... | collective-permute-start | bytes 677384 | tf_op jit(solution)/shard_map/ppermute | solution.py:458
  191.8 4.5 collective-permute-start.1
  201.3 10.6 %copy-start.16 = (bf16[2,256,896]{2,1,0:T(8,128)(2,1)S(1)}, bf16[2,256,896]{2,1,0:T(8,128)(2,1)}, u32[]{:S(2)}) copy-start(bf16[2,256,896]{2,1,0:T(8,128)(2,1)} %param.11) | copy-start | bytes 2752516
  201.3 19.4 %slice-start.2 = ((s8[12845056]{0:T(1024)(128)(4,1)}), s8[4194304]{0:T(1024)(128)(4,1)S(1)}, s32[]{:S(2)}) async-start(s8[12845056]{0:T(1024)(128)(4,1)} %bitcast.209), calls=%async_computation.6 | async-start | bytes 8388608
  201.3 19.4 %slice-start.3 = ((s8[12845056]{0:T(1024)(128)(4,1)}), s8[4194304]{0:T(1024)(128)(4,1)S(1)}, s32[]{:S(2)}) async-start(s8[12845056]{0:T(1024)(128)(4,1)} %bitcast.209), calls=%async_computation.7 | async-start | bytes 8388608
  211.9 8.8 %slice-start.4 = ((s8[12845056]{0:T(1024)(128)(4,1)}), s8[4194304]{0:T(1024)(128)(4,1)S(1)}, s32[]{:S(2)}) async-start(s8[12845056]{0:T(1024)(128)(4,1)} %bitcast.209), calls=%async_computation.8 | async-start | bytes 8388608
  211.9 8.8 %slice-start.5 = ((s8[12845056]{0:T(1024)(128)(4,1)}), s8[262144]{0:T(1024)(128)(4,1)S(1)}, s32[]{:S(2)}) async-start(s8[12845056]{0:T(1024)(128)(4,1)} %bitcast.209), calls=%async_computation.9 | async-start | bytes 524288
  220.8 11.2 %copy-start.7 = (f32[512,896]{1,0:T(8,128)S(1)}, f32[512,896]{1,0:T(8,128)}, u32[]{:S(2)}) copy-start(f32[512,896]{1,0:T(8,128)} %get-tuple-element.84) | copy-start | bytes 5505028
  250.6 8.7 %copy-start.8 = (f32[512,896]{1,0:T(8,128)S(1)}, f32[512,896]{1,0:T(8,128)}, u32[]{:S(2)}) copy-start(f32[512,896]{1,0:T(8,128)} %get-tuple-element.84) | copy-start | bytes 5505028
  263.9 12.3 %collective-permute-start.2 = (bf16[2,63,896]{2,1,0:T(8,128)(2,1)S(1)}, bf16[2,63,896]{2,1,0:T(8,128)(2,1)S(1)}, u32[]{:S(2)}, u32[]{:S(2)}) collective-permute-start(bf16[2,63,896]{2,1,0:T(8,128)(2,1)S(1)} %slice.164), channel_id=1, source_target_pairs={{1,0},{2,1},{3,2},{5,4},{6,5},{7,6},{9,8},{10,9},{11,10},{13,12},{... | collective-permute-start | bytes 677384 | tf_op jit(solution)/shard_map/ppermute | solution.py:458
  299.7 22.6 %collective-permute-start.3 = (bf16[2,63,896]{2,1,0:T(8,128)(2,1)S(1)}, bf16[2,63,896]{2,1,0:T(8,128)(2,1)S(1)}, u32[]{:S(2)}, u32[]{:S(2)}) collective-permute-start(bf16[2,63,896]{2,1,0:T(8,128)(2,1)S(1)} %slice.165), channel_id=1, source_target_pairs={{0,1},{1,2},{2,3},{4,5},{5,6},{6,7},{8,9},{9,10},{10,11},{12,13},{... | collective-permute-start | bytes 677384 | tf_op jit(solution)/shard_map/ppermute | solution.py:458
  314.0 8.3 %copy-start.19 = (bf16[8,64,896]{2,1,0:T(8,128)(2,1)S(1)}, bf16[8,64,896]{2,1,0:T(8,128)(2,1)}, u32[]{:S(2)}) copy-start(bf16[8,64,896]{2,1,0:T(8,128)(2,1)} %get-tuple-element.31) | copy-start | bytes 2752516
  364.2 17.9 %slice-start = ((s8[7340032]{0:T(1024)(128)(4,1)}), s8[4194304]{0:T(1024)(128)(4,1)S(1)}, s32[]{:S(2)}) async-start(s8[7340032]{0:T(1024)(128)(4,1)} %bitcast.174), calls=%async_computation.4 | async-start | bytes 8388608
  371.5 10.7 %slice-start.1 = ((s8[7340032]{0:T(1024)(128)(4,1)}), s8[3145728]{0:T(1024)(128)(4,1)S(1)}, s32[]{:S(2)}) async-start(s8[7340032]{0:T(1024)(128)(4,1)} %bitcast.174), calls=%async_computation.5 | async-start | bytes 6291456
  377.9 25.0 %collective-permute-start.4 = (bf16[2,512,896]{2,1,0:T(8,128)(2,1)S(1)}, bf16[2,512,896]{2,1,0:T(8,128)(2,1)S(1)}, u32[]{:S(2)}, u32[]{:S(2)}) collective-permute-start(bf16[2,512,896]{2,1,0:T(8,128)(2,1)S(1)} %dynamic-slice_bitcast_fusion), channel_id=1, source_target_pairs={{0,1},{1,0},{2,3},{3,2},{4,5},{5,4},{6,7},{7,6},{8,9},{9,8},{10,11... | collective-permute-start | bytes 5505032 | tf_op jit(solution)/shard_map/ppermute | solution.py:471
  404.5 24.3 %collective-permute-start.5 = (bf16[1,512,896]{2,1,0:T(8,128)(2,1)}, bf16[1,512,896]{2,1,0:T(8,128)(2,1)}, u32[]{:S(2)}, u32[]{:S(2)}) collective-permute-start(bf16[1,512,896]{2,1,0:T(8,128)(2,1)} %constant_dynamic-slice_fusion), channel_id=1, source_target_pairs={{0,2},{1,3},{2,0},{3,1},{4,6},{5,7},{6,4},{7,5},{8,10},{9,11},{10,... | collective-permute-start | bytes 2752520 | tf_op jit(solution)/shard_map/ppermute | solution.py:471
  412.9 15.9 %copy-start.15 = (bf16[2,512,896]{2,1,0:T(8,128)(2,1)S(1)}, bf16[2,512,896]{2,1,0:T(8,128)(2,1)}, u32[]{:S(2)}) copy-start(bf16[2,512,896]{2,1,0:T(8,128)(2,1)} %copy-done.14) | copy-start | bytes 5505028
  412.9 15.9 %copy-start.26 = (f32[1,2,2,128]{3,1,2,0:T(2,128)S(1)}, f32[1,2,2,128]{3,1,2,0:T(2,128)}, u32[]{:S(2)}) copy-start(f32[1,2,2,128]{3,1,2,0:T(2,128)} %copy-done.25) | copy-start | bytes 6148
  (32 other events, 120.9 us)
Sparse Core Ops, SparseCore 0:
  9.6 52.8 all-gather.5
  95.9 100.0 all-gather.3
  243.9 167.9 reduce-scatter.1

commit v3 on v2

--- a/solution.py
+++ b/solution.py
@@ -26,7 +26,7 @@
     dp, fsdp = sizes
     known = {
         (8, 4): (("fsdp", 1, 2), ("fsdp", 2, 2), ("dp", 1, 2), ("dp", 2, 4)),
-        (64, 4): (("dp", 1, 2), ("fsdp", 1, 4), ("dp", 16, 4), ("dp", 2, 8)),
+        (64, 4): (("dp", 1, 2), ("fsdp", 1, 4), ("dp", 2, 8), ("dp", 16, 4)),
     }
     if sizes in known:
         return known[sizes]
@@ -111,10 +111,10 @@
         pl.when(condition)(action)
 
 
-def meet(place):
+def meet(place, others=()):
     barrier = pltpu.get_barrier_semaphore()
     count = jnp.int32(0)
-    for condition, device in place.neighbours():
+    for condition, device in place.neighbours() + [(None, other) for other in others]:
         when(
             condition,
             lambda device=device: pl.semaphore_signal(barrier, inc=1, device_id=device, device_id_type=MESH),
@@ -268,20 +268,144 @@
     return gathered, tiles
 
 
-class Payload:
-    def __init__(self, source, own, sib, line_b, line_a, line_z, load_sem, send_sem, sems):
-        self.source, self.own, self.sib = source, own, sib
-        self.lines = {"b": line_b, "a": line_a, "z": line_z}
-        self.load_sem, self.send_sem, self.sems = load_sem, send_sem, sems
-
-
-def buffers_of(layout, block_shape, dtype):
+class Reduction:
+    def __init__(self, place, source, size, lanes, buffers):
+        self.place, self.source, self.size, self.lanes = place, source, size, lanes
+        self.own, self.sib, line_b, line_a, line_z, self.load_sem, self.send_sem, self.sib_sem, sem_b, sem_a, sem_z = buffers
+        self.lines = {"b": (line_b, sem_b), "a": (line_a, sem_a), "z": (line_z, sem_z)}
+        self.order = [by_distance(place.z, place.nz, k) for k in reversed(range(place.nz))]
+        self.sibling = place.device(core=1 - place.core)
+
+    def slot(self, zb, ab, bb):
+        return (zb * self.place.na + ab) * self.place.nb + bb
+
+    def piece(self, core, zb, ab, bb):
+        block = self.place.block(core, zb, ab, bb)
+        if self.size is None:
+            return self.source.at[block, :, pl.ds(*self.lanes)]
+        return self.source.at[pl.ds(pl.multiple_of(block * self.size, self.size), self.size), pl.ds(*self.lanes)]
+
+    def remote(self, src, dst, send_sem, recv_sem, device):
+        return pltpu.make_async_remote_copy(
+            src_ref=src, dst_ref=dst, send_sem=send_sem, recv_sem=recv_sem, device_id=device, device_id_type=MESH
+        )
+
+    def inner(self, a_at, b_at):
+        place = self.place
+        return [
+            (by_distance(a_at, place.na, ka), by_distance(b_at, place.nb, kb))
+            for kb in reversed(range(place.nb))
+            for ka in reversed(range(place.na))
+        ]
+
+    def open(self, i):
+        place, zb = self.place, self.order[i]
+        their_a, their_b = (place.b, place.a) if place.swaps else (place.a, place.b)
+        for (ao, bo), (at, bt) in zip(self.inner(place.a, place.b), self.inner(their_a, their_b), strict=True):
+            slot = self.slot(zb, ao, bo)
+            pltpu.make_async_copy(self.piece(place.core, zb, ao, bo), self.own.at[slot], self.load_sem.at[slot]).start()
+            slot = self.slot(zb, at, bt)
+            copy = self.remote(
+                self.piece(1 - place.core, zb, at, bt), self.sib.at[slot], self.send_sem.at[0, slot], self.sib_sem.at[slot], self.sibling
+            )
+            copy.start()
+
+    def add(self, slot, buffer, sem, at):
+        self.remote(self.own.at[slot], buffer.at[at], self.send_sem.at[1, slot], sem.at[at], self.sibling).wait_recv()
+        self.own[slot] = (self.own[slot].astype(F32) + buffer[at].astype(F32)).astype(self.own.dtype)
+
+    def both_cores(self, zb, ab, bb):
+        slot = self.slot(zb, ab, bb)
+        pltpu.make_async_copy(self.piece(self.place.core, zb, ab, bb), self.own.at[slot], self.load_sem.at[slot]).wait()
+        self.add(slot, self.sib, self.sib_sem, slot)
+
+    def pass_on(self, name, at, places, target, inner, inner_count, slot, condition=None):
+        line, sem = self.lines[name]
+        move = jnp.where(target > at, 1, -1)
+        if places == 2:
+            there = inner
+        else:
+            outer = (at - move >= 0) & (at - move < places)
+            if condition is not None:
+                outer = outer & condition
+            pl.when(outer)(lambda: self.add(slot, line, sem, target * inner_count + inner))
+            there = jnp.where((target == at + move) & (move < 0), places, target) * inner_count + inner
+        device = self.place.device(**{name: at + move})
+        copy = self.remote(self.own.at[slot], line.at[there], self.send_sem.at[1, slot], sem.at[there], device)
+        when(condition, copy.start)
+
+    def take_in(self, name, at, places, inner, inner_count, slot, condition=None):
+        line, sem = self.lines[name]
+        if places == 1:
+            return
+        if places == 2:
+            when(condition, lambda: self.add(slot, line, sem, inner))
+            return
+        lower, upper = at > 0, at < places - 1
+        if condition is not None:
+            lower, upper = lower & condition, upper & condition
+        pl.when(lower)(lambda: self.add(slot, line, sem, at * inner_count + inner))
+        pl.when(upper)(lambda: self.add(slot, line, sem, places * inner_count + inner))
+
+    def first(self, i):
+        place, zb = self.place, self.order[i]
+        for kb in reversed(range(1, place.nb)):
+            bb = by_distance(place.b, place.nb, kb)
+            for ka in reversed(range(place.na)):
+                ab = by_distance(place.a, place.na, ka)
+                self.both_cores(zb, ab, bb)
+                inner, count = zb * place.na + ab, place.nz * place.na
+                self.pass_on("b", place.b, place.nb, bb, inner, count, self.slot(zb, ab, bb))
+        for ka in reversed(range(place.na)):
+            self.both_cores(zb, by_distance(place.a, place.na, ka), place.b)
+
+    def second(self, i):
+        place, zb = self.place, self.order[i]
+        for ka in reversed(range(place.na)):
+            ab = by_distance(place.a, place.na, ka)
+            slot = self.slot(zb, ab, place.b)
+            self.take_in("b", place.b, place.nb, zb * place.na + ab, place.nz * place.na, slot)
+            if ka:
+                self.pass_on("a", place.a, place.na, ab, zb, place.nz, slot)
+
+    def third(self, i):
+        place, zb = self.place, self.order[i]
+        slot = self.slot(zb, place.a, place.b)
+        self.take_in("a", place.a, place.na, zb, place.nz, slot)
+        if i < place.nz - 1:
+            self.pass_on("z", place.z, place.nz, zb, 0, 1, slot)
+
+    def last(self, out_ref):
+        place = self.place
+        slot = self.slot(place.z, place.a, place.b)
+        self.take_in("z", place.z, place.nz, 0, 1, slot)
+        out_ref[...] = self.own[slot].astype(F32)
+
+    def actions(self):
+        n = self.place.nz
+        found = []
+        for i in range(n + 2):
+            for step, back in ((self.first, 0), (self.second, 1), (self.third, 2)):
+                if 0 <= i - back < n:
+                    found.append(functools.partial(step, i - back))
+        return found
+
+    def drain(self):
+        place = self.place
+        mine = self.slot(place.z, place.a, place.b)
+        for slot in range(place.nz * place.na * place.nb):
+            for kind in range(2):
+                copy = self.remote(self.sib.at[slot], self.sib.at[slot], self.send_sem.at[kind, slot], self.sib_sem.at[slot], self.sibling)
+                when(None if kind == 0 else mine != slot, copy.wait_send)
+
+
+def reduction_scratch(layout, block_shape, dtype):
     _, (_, _, nb), (_, _, na), (_, _, nz) = layout
-    per_core = nz * na * nb
     deep = lambda places: 1 if places <= 2 else places + 1
     vm = lambda *lead: pltpu.VMEM(lead + block_shape, dtype)
     dma = pltpu.SemaphoreType.DMA
-    counts = {"s": per_core, "b": deep(nb) * nz * na, "a": deep(na) * nz, "z": deep(nz)}
+    per_core = nz * na * nb
+    counts = {"b": deep(nb) * nz * na, "a": deep(na) * nz, "z": deep(nz)}
     return [
         vm(per_core), vm(per_core), vm(counts["b"]), vm(counts["a"]), vm(counts["z"]),
         dma((per_core,)), dma((2, per_core)),
@@ -289,167 +413,189 @@
     ]
 
 
-def scatter_steps(layout, payloads, finish):
-    place = Place(layout)
-    a, b, z, core = place.a, place.b, place.z, place.core
-    na, nb, nz = place.na, place.nb, place.nz
-    slot_of = lambda zb, ab, bb: (zb * na + ab) * nb + bb
-    meet(place)
-    sent = []
-
-    def remote(src, dst, send_sem, recv_sem, device):
-        return pltpu.make_async_remote_copy(
-            src_ref=src, dst_ref=dst, send_sem=send_sem, recv_sem=recv_sem, device_id=device, device_id_type=MESH
-        )
-
-    def order(a_at, b_at):
-        found = []
-        for kz in reversed(range(nz)):
-            for kb in reversed(range(nb)):
-                for ka in reversed(range(na)):
-                    found.append((by_distance(z, nz, kz), by_distance(a_at, na, ka), by_distance(b_at, nb, kb)))
-        return found
-
-    sibling = place.device(core=1 - core)
-    own_order = order(a, b)
-    their_a, their_b = (b, a) if place.swaps else (a, b)
-    for (zo, ao, bo), (zt, at, bt) in zip(own_order, order(their_a, their_b), strict=True):
-        for p in payloads:
-            slot = slot_of(zo, ao, bo)
-            pltpu.make_async_copy(p.source.at[place.block(core, zo, ao, bo)], p.own.at[slot], p.load_sem.at[slot]).start()
-            slot = slot_of(zt, at, bt)
-            copy = remote(
-                p.source.at[place.block(1 - core, zt, at, bt)], p.sib.at[slot], p.send_sem.at[0, slot], p.sems["s"].at[slot], sibling
-            )
-            copy.start()
-            sent.append((None, copy))
-
-    waiting = []
-
-    def release():
-        while waiting:
-            condition, copy = waiting.pop(0)
-            when(condition, copy.start)
-            sent.append((condition, copy))
-
-    def add_arrival(p, slot, buffer, sem, at):
-        remote(p.own.at[slot], buffer.at[at], p.send_sem.at[1, slot], sem.at[at], sibling).wait_recv()
-        p.own[slot] = (p.own[slot].astype(F32) + buffer[at].astype(F32)).astype(p.own.dtype)
-
-    def start_sum(zb, ab, bb):
-        for p in payloads:
-            slot = slot_of(zb, ab, bb)
-            pltpu.make_async_copy(p.source.at[place.block(core, zb, ab, bb)], p.own.at[slot], p.load_sem.at[slot]).wait()
-            add_arrival(p, slot, p.sib, p.sems["s"], slot)
-
-    def pass_on(name, at, places, target, inner, inner_count, zb, ab, bb):
-        move = jnp.where(target > at, 1, -1)
-        for p in payloads:
-            slot = slot_of(zb, ab, bb)
-            line, sem = p.lines[name], p.sems[name]
-            if places == 2:
-                there = inner
-            else:
-                outer = (at - move >= 0) & (at - move < places)
-                here = target * inner_count + inner
-                pl.when(outer)(lambda p=p, slot=slot, line=line, sem=sem, here=here: add_arrival(p, slot, line, sem, here))
-                last = (target == at + move) & (move < 0)
-                there = jnp.where(last, places, target) * inner_count + inner
-            waiting.append(
-                (None, remote(p.own.at[slot], line.at[there], p.send_sem.at[1, slot], sem.at[there], place.device(**{name: at + move})))
-            )
-        release()
-
-    def take_in(name, at, places, inner, inner_count, zb, ab, bb):
-        for p in payloads:
-            slot = slot_of(zb, ab, bb)
-            line, sem = p.lines[name], p.sems[name]
-            if places == 1:
+BUFFERS = 11
+
+
+def row_tiles(rows):
+    return rows if rows % 16 == 0 else None
+
+
+def projection_grads(every, grad_keys, grad_values, pairs, near_grads, share):
+    width = every.shape[1]
+    rows = pairs[0][0].shape[0]
+    tall = 2 * rows if every.shape[0] % (2 * rows) == 0 else rows
+    many = every.shape[0] // tall
+    order = [(7, 1), (4, 1), (3, 1), (5, 1), (6, 1), (0, 1), (1, many), (2, many)]
+    matrix_of, start_of = [], {}
+    for matrix, count in order:
+        start_of[matrix] = len(matrix_of)
+        matrix_of += [matrix] * count
+    steps = len(matrix_of)
+
+    def body(table_ref, every_ref, gk_ref, gv_ref, l0, r0, l1, r1, l2, r2, l3, r3, n5, n6, out_ref, acc_ref):
+        step = pl.program_id(0)
+        sources = {0: (l0, r0), 3: (l1, r1), 4: (l2, r2), 7: (l3, r3), 1: (every_ref, gk_ref), 2: (every_ref, gv_ref)}
+        for matrix, count in order:
+            start = start_of[matrix]
+            if matrix in (5, 6):
+
+                @pl.when(step == start)
+                def _(near_ref=n5 if matrix == 5 else n6):
+                    out_ref[0] = near_ref[...]
+
                 continue
-            if places == 2:
-                add_arrival(p, slot, line, sem, inner)
-                continue
-            pl.when(at > 0)(lambda p=p, slot=slot, line=line, sem=sem: add_arrival(p, slot, line, sem, at * inner_count + inner))
-            pl.when(at < places - 1)(
-                lambda p=p, slot=slot, line=line, sem=sem: add_arrival(p, slot, line, sem, places * inner_count + inner)
-            )
-
-    def first_stage(zb):
-        for kb in reversed(range(1, nb)):
-            bb = by_distance(b, nb, kb)
-            for ka in reversed(range(na)):
-                ab = by_distance(a, na, ka)
-                start_sum(zb, ab, bb)
-                release()
-                pass_on("b", b, nb, bb, zb * na + ab, nz * na, zb, ab, bb)
-        for ka in reversed(range(na)):
-            start_sum(zb, by_distance(a, na, ka), b)
-            release()
-
-    def second_stage(zb):
-        for ka in reversed(range(1, na)):
-            ab = by_distance(a, na, ka)
-            take_in("b", b, nb, zb * na + ab, nz * na, zb, ab, b)
-            release()
-            pass_on("a", a, na, ab, zb, nz, zb, ab, b)
-        take_in("b", b, nb, zb * na + a, nz * na, zb, a, b)
-        release()
-
-    def third_stage(zb, onward):
-        take_in("a", a, na, zb, nz, zb, a, b)
-        release()
-        if onward:
-            pass_on("z", z, nz, zb, 0, 1, zb, a, b)
-
-    far_first = [by_distance(z, nz, kz) for kz in reversed(range(nz))]
-    for i in range(nz + 2):
-        if i < nz:
-            first_stage(far_first[i])
-        if 0 <= i - 1 < nz:
-            second_stage(far_first[i - 1])
-        if 0 <= i - 2 < nz:
-            third_stage(far_first[i - 2], i - 2 < nz - 1)
-    release()
-    take_in("z", z, nz, 0, 1, z, a, b)
-    mine = slot_of(z, a, b)
-    for p, done in zip(payloads, finish, strict=True):
-        done(p.own[mine])
-    for condition, copy in sent:
-        when(condition, copy.wait_send)
-
-
-def scatter_all(layout, blocks, collective_id):
-    count = len(blocks)
-
-    def body(*refs):
-        sources, outs, rest = refs[:count], refs[count : 2 * count], refs[2 * count :]
-        payloads, finish = [], []
-        for i in range(count):
-            own, sib, line_b, line_a, line_z, load, send, s, sb, sa, sz = rest[11 * i : 11 * (i + 1)]
-            payloads.append(
-                Payload(sources[i], own, sib, line_b, line_a, line_z, load, send, {"s": s, "b": sb, "a": sa, "z": sz})
-            )
-
-            def done(value, i=i):
-                outs[i][...] = value.astype(F32)
-
-            finish.append(done)
-        scatter_steps(layout, payloads, finish)
-
-    scratch = []
-    for block in blocks:
-        scratch += buffers_of(layout, block.shape[1:], block.dtype)
+            left, right = sources[matrix]
+
+            @pl.when((step >= start) & (step < start + count))
+            def _(left=left, right=right, start=start, count=count):
+                if count == 1:
+                    out_ref[0] = transposed_times(left[...], right[...]).astype(BF16)
+                    return
+                term = transposed_times(left[...], right[...])
+
+                @pl.when(step == start)
+                def _():
+                    acc_ref[...] = term
+
+                @pl.when(step > start)
+                def _():
+                    acc_ref[...] += term
+
+                @pl.when(step == start + count - 1)
+                def _():
+                    out_ref[0] = acc_ref[...].astype(BF16)
+
+    def chunk(start):
+        return pl.BlockSpec((tall, width), lambda i, _: (jnp.clip(i - start, 0, many - 1), 0))
+
+    both = pl.BlockSpec(
+        (tall, width), lambda i, _: (jnp.clip(jnp.where(i < start_of[2], i - start_of[1], i - start_of[2]), 0, many - 1), 0)
+    )
+    square = pl.BlockSpec((width, width), lambda i, _: (0, 0))
+    in_specs = [both, chunk(start_of[1]), chunk(start_of[2])] + [pl.BlockSpec((rows, width), lambda i, _: (0, 0))] * 8
     return pl.pallas_call(
         body,
-        out_shape=[jax.ShapeDtypeStruct(block.shape[1:], F32) for block in blocks],
-        in_specs=[pl.BlockSpec(memory_space=pl.ANY)] * count,
-        out_specs=[pl.BlockSpec(memory_space=pltpu.VMEM)] * count,
+        grid_spec=pltpu.PrefetchScalarGridSpec(
+            num_scalar_prefetch=1,
+            grid=(steps,),
+            in_specs=in_specs + [square, square],
+            out_specs=pl.BlockSpec((1, width, width), lambda i, table: (table[i], 0, 0)),
+            scratch_shapes=[pltpu.VMEM((width, width), F32)],
+        ),
+        out_shape=jax.ShapeDtypeStruct((8, width, width), BF16),
+        cost_estimate=pl.CostEstimate(
+            flops=2 * width * width * (2 * every.shape[0] + 4 * pairs[0][0].shape[0]), transcendentals=0, bytes_accessed=40_000_000
+        ),
+        compiler_params=pltpu.CompilerParams(vmem_limit_bytes=50_000_000),
+        name="projection_grads",
+    )(jnp.asarray(matrix_of, jnp.int32), every, grad_keys, grad_values, *[side for pair in pairs for side in pair], *near_grads)
+
+
+def last_steps(layout, sizes, matrix_grads, share, lines, grad_queries, query_matrix, joined, hidden, gain, grad_first):
+    tokens, width = grad_queries.shape
+    bits = lambda count: [1 << i for i in range(count.bit_length() - 1)]
+    rounds = [("fsdp", step) for step in bits(sizes[1])] + [("dp", step) for step in bits(sizes[0])]
+    given = [line for line in lines if line is not None]
+    per_gain = width // 128
+    total_rows = sum(per_gain if line is None else line.shape[0] for line in lines)
+    held_rows = -(-total_rows // 8) * 8
+
+    def body(*refs):
+        (mats_ref, dq_ref, m0_ref, in_ref, hid_ref, gf_ref, gain_ref), refs = refs[:7], refs[7:]
+        line_refs, refs = list(refs[: len(given)]), refs[len(given) :]
+        (attn_ref, sum_ref, hg_ref), refs = refs[:3], refs[3:]
+        (q_buf, m0, in_buf, hid_buf, first_buf, load_sem), refs = refs[:6], refs[6:]
+        (line_out, line_in, line_send, line_recv), buffers = refs[:4], refs[4:]
+        place = Place(layout)
+        index = {axis: lax.axis_index(axis).astype(jnp.int32) for axis in AXES}
+        across = lambda axis, step: {axis: index[axis] + step * (1 - 2 * ((index[axis] // step) % 2))}
+        meet(place, [across(axis, step) for axis, step in rounds])
+        loads = [
+            pltpu.make_async_copy(src, dst, load_sem.at[i])
+            for i, (src, dst) in enumerate(
+                ((dq_ref, q_buf), (m0_ref, m0), (in_ref, in_buf), (hid_ref, hid_buf), (gf_ref, first_buf))
+            )
+        ]
+        big = Reduction(place, mats_ref, row_tiles(share), (0, width), buffers)
+        for i in range(place.nz):
+            big.open(i)
+            if i == 0:
+                for load in loads:
+                    load.start()
+        actions = big.actions()
+        actions.pop(0)()
+        for load in loads:
+            load.wait()
+        piece = tokens // 4
+
+        def finish(i, total):
+            rows = pl.ds(pl.multiple_of(i * piece, piece), piece)
+            held = hid_buf[rows, :].astype(F32)
+            scale = inverse_rms(held)
+            grad = dot_t(q_buf[rows, :], m0[...]) + in_buf[rows, :]
+            hg_ref[rows, :] = first_buf[rows, :] + norm_back(held, scale, gain_ref[...], grad)
+            return total + jnp.sum(grad * held * scale, axis=0, keepdims=True)
+
+        gain_grad = lax.fori_loop(0, 4, finish, jnp.zeros((1, width), F32))
+        at = 0
+        for line in lines:
+            if line is None:
+                for i in range(per_gain):
+                    sum_ref[at + i : at + i + 1, :] = gain_grad[:, i * 128 : (i + 1) * 128]
+                at += per_gain
+            else:
+                ref = line_refs.pop(0)
+                sum_ref[at : at + ref.shape[0], :] = ref[...]
+                at += ref.shape[0]
+        if at < held_rows:
+            sum_ref[at:, :] = jnp.zeros((held_rows - at, 128), F32)
+
+        def round_copy(i):
+            axis, step = rounds[i]
+            return pltpu.make_async_remote_copy(
+                src_ref=line_out.at[i], dst_ref=line_in.at[i], send_sem=line_send.at[i], recv_sem=line_recv.at[i],
+                device_id=across(axis, step), device_id_type=MESH,
+            )
+
+        for i in range(len(rounds)):
+            line_out[i] = sum_ref[...]
+            round_copy(i).start()
+            for _ in range(2):
+                if actions:
+                    actions.pop(0)()
+            round_copy(i).wait_recv()
+            sum_ref[...] += line_in[i]
+        for action in actions:
+            action()
+        big.last(attn_ref)
+        for i in range(len(rounds)):
+            round_copy(i).wait_send()
+        big.drain()
+
+    anywhere = pl.BlockSpec(memory_space=pl.ANY)
+    inside = pl.BlockSpec(memory_space=pltpu.VMEM)
+    block = (share, width)
+    dma = pltpu.SemaphoreType.DMA
+    scratch = [
+        pltpu.VMEM(grad_queries.shape, BF16), pltpu.VMEM((width, width), BF16), pltpu.VMEM(joined.shape, joined.dtype),
+        pltpu.VMEM(hidden.shape, hidden.dtype), pltpu.VMEM(grad_first.shape, F32), dma((5,)),
+        pltpu.VMEM((len(rounds), held_rows, 128), F32), pltpu.VMEM((len(rounds), held_rows, 128), F32),
+        dma((len(rounds),)), dma((len(rounds),)),
+    ]
+    scratch += reduction_scratch(layout, block, BF16)
+    return pl.pallas_call(
+        body,
+        out_shape=[
+            jax.ShapeDtypeStruct(block, F32),
+            jax.ShapeDtypeStruct((held_rows, 128), F32),
+            jax.ShapeDtypeStruct((tokens, width), F32),
+        ],
+        in_specs=[anywhere] * 6 + [inside] * (1 + len(given)),
+        out_specs=[inside] * 3,
         scratch_shapes=scratch,
-        compiler_params=pltpu.CompilerParams(
-            collective_id=collective_id, has_side_effects=True, vmem_limit_bytes=60_000_000
-        ),
-        name="scatter_all",
-    )(*blocks)
+        compiler_params=pltpu.CompilerParams(collective_id=2, has_side_effects=True, vmem_limit_bytes=50_000_000),
+        name="last_steps",
+    )(matrix_grads, grad_queries, query_matrix, joined, hidden, grad_first, gain.reshape(1, width), *given)
 
 
 def from_behind(array, axis, by):
@@ -717,6 +863,118 @@
     )(place, query, keys, values, tiles, hidden_mask, outer_t, lse, grad)
 
 
+def whole(shape):
+    return pl.BlockSpec(shape, lambda *_: (0,) * len(shape))
+
+
+def feed_forward(second_sum, gain, grad_out_low, weights, bias_input, bias_output):
+    tokens, width = second_sum.shape
+    units = bias_input.shape[0]
+    tile = 512
+    steps = units // tile
+    part = 256
+
+    def body(sum_ref, gain_ref, go_ref, wi_ref, wo_ref, bi_ref, bo_ref, out_ref, gs_ref, gg_ref, gbi_ref, gbo_ref, gw_ref, n_ref, acc_ref, gn_ref):
+        step = pl.program_id(0)
+
+        @pl.when(step == 0)
+        def _():
+            held = sum_ref[...]
+            n_ref[...] = (held * inverse_rms(held) * gain_ref[...]).astype(BF16)
+            acc_ref[...] = jnp.zeros_like(acc_ref)
+            gn_ref[...] = jnp.zeros_like(gn_ref)
+
+        normed = n_ref[...]
+        incoming = go_ref[...]
+        for at in range(0, tile, part):
+            rows = slice(at, at + part)
+            w_in, w_out = wi_ref[rows, :], wo_ref[rows, :]
+            value, slope = gelu_parts(dot_t(normed, w_in) + bi_ref[0, :, rows])
+            value_low = value.astype(BF16)
+            grad_pre = dot_t(incoming, w_out) * slope
+            bias_grad = jnp.sum(grad_pre, axis=0, keepdims=True)
+            for i in range(part // 128):
+                gbi_ref[0, at // 128 + i : at // 128 + i + 1, :] = bias_grad[:, i * 128 : (i + 1) * 128]
+            grad_pre_low = grad_pre.astype(BF16)
+            acc_ref[...] += product(value_low, w_out)
+            gn_ref[...] += product(grad_pre_low, w_in)
+            gw_ref[0, 0, rows, :] = transposed_times(grad_pre_low, normed).astype(BF16)
+            gw_ref[1, 0, rows, :] = transposed_times(value_low, incoming).astype(BF16)
+
+        @pl.when(step == steps - 1)
+        def _():
+            held = sum_ref[...]
+            scale = inverse_rms(held)
+            out_ref[...] = (held + acc_ref[...] + bo_ref[...]).astype(BF16)
+            grad_norm = gn_ref[...]
+            grad_out = incoming.astype(F32)
+            for ref, line in (
+                (gbo_ref, jnp.sum(grad_out, axis=0, keepdims=True)),
+                (gg_ref, jnp.sum(grad_norm * held * scale, axis=0, keepdims=True)),
+            ):
+                for i in range(width // 128):
+                    ref[i : i + 1, :] = line[:, i * 128 : (i + 1) * 128]
+            gs_ref[...] = grad_out + norm_back(held, scale, gain_ref[...], grad_norm)
+
+    tall, line = whole((tokens, width)), whole((1, width))
+    rows_of_128 = whole((width // 128, 128))
+    return pl.pallas_call(
+        body,
+        grid=(steps,),
+        in_specs=[
+            tall, line, tall,
+            pl.BlockSpec((tile, width), lambda i: (i, 0)),
+            pl.BlockSpec((tile, width), lambda i: (i + steps, 0)),
+            pl.BlockSpec((1, 1, tile), lambda i: (i, 0, 0)),
+            line,
+        ],
+        out_specs=[
+            tall, tall, rows_of_128,
+            pl.BlockSpec((1, tile // 128, 128), lambda i: (i, 0, 0)),
+            rows_of_128,
+            pl.BlockSpec((2, 1, tile, width), lambda i: (0, i, 0, 0)),
+        ],
+        out_shape=[
+            jax.ShapeDtypeStruct((tokens, width), BF16),
+            jax.ShapeDtypeStruct((tokens, width), F32),
+            jax.ShapeDtypeStruct((width // 128, 128), F32),
+            jax.ShapeDtypeStruct((steps, tile // 128, 128), F32),
+            jax.ShapeDtypeStruct((width // 128, 128), F32),
+            jax.ShapeDtypeStruct((2, steps, tile, width), BF16),
+        ],
+        scratch_shapes=[
+            pltpu.VMEM((tokens, width), BF16),
+            pltpu.VMEM((tokens, width), F32),
+            pltpu.VMEM((tokens, width), F32),
+        ],
+        cost_estimate=pl.CostEstimate(flops=12 * tokens * width * units, transcendentals=0, bytes_accessed=40_000_000),
+        compiler_params=pltpu.CompilerParams(vmem_limit_bytes=50_000_000),
+        name="feed_forward",
+    )(
+        second_sum, gain.reshape(1, width), grad_out_low, weights, weights,
+        bias_input.reshape(steps, 1, tile), bias_output.reshape(1, width),
+    )
+
+
+def span_projection(near, key_matrix, value_matrix):
+    blocks, rows, width = near.shape
+
+    def body(near_ref, mk_ref, mv_ref, k_ref, v_ref):
+        k_ref[0] = product(near_ref[0], mk_ref[...]).astype(BF16)
+        v_ref[0] = product(near_ref[0], mv_ref[...]).astype(BF16)
+
+    block = pl.BlockSpec((1, rows, width), lambda i: (i, 0, 0))
+    return pl.pallas_call(
+        body,
+        grid=(blocks,),
+        in_specs=[block, whole((width, width)), whole((width, width))],
+        out_specs=[block, block],
+        out_shape=[jax.ShapeDtypeStruct(near.shape, BF16)] * 2,
+        cost_estimate=pl.CostEstimate(flops=4 * blocks * rows * width * width, transcendentals=0, bytes_accessed=15_000_000),
+        name="span_projection",
+    )(near, key_matrix, value_matrix)
+
+
 def both_heads(values, head_size):
     return jnp.concatenate([own_lanes(values, h, head_size) for h in range(128 // head_size)], axis=0)
 
@@ -733,17 +991,26 @@
     return raised / jnp.sum(raised, axis=0, keepdims=True)
 
 
+def lane_groups(width):
+    return [slice(i, i + 128) for i in range(0, width, 128)]
+
+
+def side_by_side(parts):
+    return jnp.concatenate(parts, axis=1)
+
+
 def span_attention(query, keys, values, head_size):
     blocks, rows, width = query.shape
     span_keys = keys.shape[1]
 
     def body(q_ref, k_ref, v_ref, o_ref):
-        for i in range(width // 128):
-            lanes = slice(i * 128, (i + 1) * 128)
-            stacked = both_heads(q_ref[0, :, lanes] * jnp.asarray(0.125, BF16), head_size)
-            p = softmax_down(dot_t(k_ref[0, :, lanes], stacked)).astype(BF16)
-            wide = product(flipped(v_ref[0, :, lanes]), p).T
-            o_ref[0, :, lanes] = picked(wide, rows, head_size).astype(BF16)
+        groups = lane_groups(width)
+        scaled = q_ref[0] * jnp.asarray(0.125, BF16)
+        scores = side_by_side([dot_t(k_ref[0, :, g], both_heads(scaled[:, g], head_size)) for g in groups])
+        weights = softmax_down(scores).astype(BF16)
+        turned = flipped(v_ref[0])
+        wide = [product(turned[g], weights[:, g]).T for g in groups]
+        o_ref[0] = side_by_side([picked(w, rows, head_size) for w in wide]).astype(BF16)
 
     q_spec = pl.BlockSpec((1, rows, width), lambda i: (i, 0, 0))
     k_spec = pl.BlockSpec((1, span_keys, width), lambda i: (i, 0, 0))
@@ -758,40 +1025,64 @@
     )(query, keys, values)
 
 
-def span_attention_back(query, keys, values, grad, head_size):
+def span_attention_back(query, keys, values, grad, near, key_matrix, value_matrix, head_size):
     blocks, rows, width = query.shape
     span_keys = keys.shape[1]
 
-    def body(q_ref, k_ref, v_ref, do_ref, dq_ref, dk_ref, dv_ref):
-        for i in range(width // 128):
-            lanes = slice(i * 128, (i + 1) * 128)
-            stacked = both_heads(q_ref[0, :, lanes] * jnp.asarray(0.125, BF16), head_size)
-            theirs = both_heads(do_ref[0, :, lanes], head_size)
-            k, v = k_ref[0, :, lanes], v_ref[0, :, lanes]
-            p = softmax_down(dot_t(k, stacked))
-            dp = dot_t(v, theirs)
-            ds = p * (dp - jnp.sum(p * dp, axis=0, keepdims=True))
-            ds_low = ds.astype(BF16)
-            dv_ref[0, :, lanes] = product(p.astype(BF16), theirs).astype(BF16)
-            dk_ref[0, :, lanes] = product(ds_low, stacked).astype(BF16)
-            wide = (product(flipped(k), ds_low) * 0.125).T
-            dq_ref[0, :, lanes] = picked(wide, rows, head_size).astype(BF16)
+    def body(q_ref, k_ref, v_ref, do_ref, near_ref, mk_ref, mv_ref, dq_ref, dn_ref, gk_ref, gv_ref, gk_acc, gv_acc):
+        step = pl.program_id(0)
+        groups = lane_groups(width)
+        scaled = q_ref[0] * jnp.asarray(0.125, BF16)
+        incoming = do_ref[0]
+        stacked = [both_heads(scaled[:, g], head_size) for g in groups]
+        theirs = [both_heads(incoming[:, g], head_size) for g in groups]
+        k, v = k_ref[0], v_ref[0]
+        p = softmax_down(side_by_side([dot_t(k[:, g], s) for g, s in zip(groups, stacked)]))
+        dp = side_by_side([dot_t(v[:, g], t) for g, t in zip(groups, theirs)])
+        ds = p * (dp - jnp.sum(p * dp, axis=0, keepdims=True))
+        ds_low, p_low = ds.astype(BF16), p.astype(BF16)
+        dv = side_by_side([product(p_low[:, g], t) for g, t in zip(groups, theirs)]).astype(BF16)
+        dk = side_by_side([product(ds_low[:, g], s) for g, s in zip(groups, stacked)]).astype(BF16)
+        turned = flipped(k)
+        wide = [(product(turned[g], ds_low[:, g]) * 0.125).T for g in groups]
+        dq_ref[0] = side_by_side([picked(w, rows, head_size) for w in wide]).astype(BF16)
+        dn_ref[0] = dot_t(dk, mk_ref[...]) + dot_t(dv, mv_ref[...])
+        near_t = flipped(near_ref[0])
+
+        @pl.when(step == 0)
+        def _():
+            gk_acc[...] = product(near_t, dk)
+            gv_acc[...] = product(near_t, dv)
+
+        @pl.when(step > 0)
+        def _():
+            gk_acc[...] += product(near_t, dk)
+            gv_acc[...] += product(near_t, dv)
+
+        @pl.when(step == blocks - 1)
+        def _():
+            gk_ref[...] = gk_acc[...].astype(BF16)
+            gv_ref[...] = gv_acc[...].astype(BF16)
 
     q_spec = pl.BlockSpec((1, rows, width), lambda i: (i, 0, 0))
     k_spec = pl.BlockSpec((1, span_keys, width), lambda i: (i, 0, 0))
+    square = whole((width, width))
     return pl.pallas_call(
         body,
         grid=(blocks,),
-        in_specs=[q_spec, k_spec, k_spec, q_spec],
-        out_specs=[q_spec, k_spec, k_spec],
+        in_specs=[q_spec, k_spec, k_spec, q_spec, k_spec, square, square],
+        out_specs=[q_spec, k_spec, square, square],
         out_shape=[
             jax.ShapeDtypeStruct(query.shape, BF16),
-            jax.ShapeDtypeStruct(keys.shape, BF16),
-            jax.ShapeDtypeStruct(keys.shape, BF16),
-        ],
-        cost_estimate=pl.CostEstimate(flops=40 * blocks * rows * span_keys * width, transcendentals=0, bytes_accessed=24_000_000),
+            jax.ShapeDtypeStruct(keys.shape, F32),
+            jax.ShapeDtypeStruct((width, width), BF16),
+            jax.ShapeDtypeStruct((width, width), BF16),
+        ],
+        scratch_shapes=[pltpu.VMEM((width, width), F32), pltpu.VMEM((width, width), F32)],
+        cost_estimate=pl.CostEstimate(flops=20 * blocks * span_keys * width * width, transcendentals=0, bytes_accessed=40_000_000),
+        compiler_params=pltpu.CompilerParams(vmem_limit_bytes=50_000_000),
         name="span_attention_back",
-    )(query, keys, values, grad)
+    )(query, keys, values, grad, near, key_matrix, value_matrix)
 
 
 def per_device(hidden, neighbours, piece_starts, out_grad, attn_weights, ffw_weights, vectors, rel_table):
@@ -821,7 +1112,6 @@
     ffw_full = gather(lax.optimization_barrier((ffw_weights, vector_full))[0], AXES)
     matrices = attn_full.reshape(8, width, width)
     vector_full = vector_full.reshape(-1, vector_rows * 128)[:, : vectors.shape[0]].reshape(-1).astype(F32)
-    w_input, w_output = ffw_full[:FF], ffw_full[FF:]
     bias_input = vector_full[:FF]
     gains = vector_full[FF : FF + 3 * width].reshape(3, width)
     bias_output = vector_full[FF + 3 * width :]
@@ -844,9 +1134,8 @@
     queries = product(normed_one, matrices[0]).astype(BF16).reshape(count, rows, width)
     keys = product(normed_every, matrices[1]).astype(BF16).reshape(group, count, rows, width)
     values = product(normed_every, matrices[2]).astype(BF16).reshape(group, count, rows, width)
-    near_flat = neighbours.reshape(count * spans * span_keys, width)
-    cross_keys = product(near_flat, matrices[5]).astype(BF16).reshape(count * spans, span_keys, width)
-    cross_values = product(near_flat, matrices[6]).astype(BF16).reshape(count * spans, span_keys, width)
+    near = neighbours.reshape(count * spans, span_keys, width)
+    cross_keys, cross_values = span_projection(near, matrices[5], matrices[6])
     context, context_t, lse = self_attention(
         place_arg, queries, keys, values, tiles, mask, head_size, reach
     )
@@ -868,66 +1157,44 @@
     block_queries = ahead(cross_queries)
     placed = behind(span_attention(block_queries, cross_keys, cross_values, head_size))
     second_sum = first_sum + product(placed, matrices[7])
-    scale_three = inverse_rms(second_sum)
-    normed_three = (second_sum * scale_three * gains[2]).astype(BF16)
-    pre_act = times_transposed(normed_three, w_input) + bias_input
-    act_value, act_slope = gelu_parts(pre_act)
-    activated = act_value.astype(BF16)
-    output = (second_sum + product(activated, w_output) + bias_output).astype(BF16)
-
-    grad_out_low = out_grad.reshape(tokens, width)
-    grad_out = grad_out_low.astype(F32)
-    grad_bias_output = jnp.sum(grad_out, axis=0)
-    grad_w_output = transposed_times(activated, grad_out_low).astype(BF16)
-    grad_pre = times_transposed(grad_out_low, w_output) * act_slope
-    grad_bias_input = jnp.sum(grad_pre, axis=0)
-    grad_pre_low = grad_pre.astype(BF16)
-    grad_w_input = transposed_times(grad_pre_low, normed_three).astype(BF16)
-    scatter = lambda array: lax.psum_scatter(array, AXES, scatter_dimension=0, tiled=True)
-    ffw_step = jnp.stack([grad_w_input, grad_w_output]).reshape(2 * FF, width)
-    ffw_step, grad_pre_low = lax.optimization_barrier((ffw_step, grad_pre_low))
-    ffw_sum = scatter(ffw_step)
-    grad_norm_three = product(grad_pre_low, w_input)
-    grad_gain_three = jnp.sum(grad_norm_three * second_sum * scale_three, axis=0)
-    grad_second = grad_out + norm_back(second_sum, scale_three, gains[2], grad_norm_three)
+    output, grad_second, grad_gain_three, grad_bias_input, grad_bias_output, ffw_step = feed_forward(
+        second_sum, gains[2], out_grad.reshape(tokens, width), ffw_full, bias_input, bias_output
+    )
+    blocks_of = lambda array: array.reshape((-1, width) if row_tiles(share) else (-1, share, width))
+    ffw_sum = lax.psum_scatter(ffw_step.reshape(2 * FF, width), AXES, scatter_dimension=0, tiled=True)
     grad_second_low = grad_second.astype(BF16)
-    grad_cross_out = transposed_times(placed, grad_second_low)
     grad_placed = times_transposed(grad_second_low, matrices[7]).astype(BF16).reshape(count, rows, width)
-    grad_block_queries, grad_cross_keys, grad_cross_values = span_attention_back(
-        block_queries, cross_keys, cross_values, ahead(grad_placed), head_size
-    )
-    grad_cross_keys = grad_cross_keys.reshape(count * spans * span_keys, width)
-    grad_cross_values = grad_cross_values.reshape(count * spans * span_keys, width)
+    grad_block_queries, near_grad, grad_cross_key_mat, grad_cross_value_mat = span_attention_back(
+        block_queries, cross_keys, cross_values, ahead(grad_placed), near, matrices[5], matrices[6], head_size
+    )
     grad_cross_queries = behind(grad_block_queries)
-    grad_cross_query_mat = transposed_times(normed_two, grad_cross_queries)
     grad_norm_two = times_transposed(grad_cross_queries, matrices[4])
     grad_gain_two = jnp.sum(grad_norm_two * first_sum * scale_two, axis=0)
     grad_first = grad_second + norm_back(first_sum, scale_two, gains[1], grad_norm_two)
     grad_first_low = grad_first.astype(BF16)
-    grad_self_out = transposed_times(context, grad_first_low)
     grad_context = times_transposed(grad_first_low, matrices[3]).astype(BF16).reshape(count, rows, width)
     grad_queries, grad_keys, grad_values, diagonal = self_attention_back(
         place_arg, queries, keys, values, tiles, mask, context_t, lse, grad_context, head_size, reach
     )
     grad_queries = grad_queries.reshape(tokens, width)
-    grad_keys = grad_keys.reshape(group * tokens, width)
-    grad_values = grad_values.reshape(group * tokens, width)
     partial_one = (
-        times_transposed(grad_keys, matrices[1]) + times_transposed(grad_values, matrices[2])
+        times_transposed(grad_keys.reshape(group * tokens, width), matrices[1])
+        + times_transposed(grad_values.reshape(group * tokens, width), matrices[2])
     ).astype(BF16)
     joined = sum_of_group(partial_one.reshape(group, tokens, width), place)
-    grad_cross_key_mat = transposed_times(near_flat, grad_cross_keys)
-    grad_cross_value_mat = transposed_times(near_flat, grad_cross_values)
-    near_grad = times_transposed(grad_cross_keys, matrices[5]) + times_transposed(
-        grad_cross_values, matrices[6]
-    )
-    grad_query_mat = transposed_times(normed_one, grad_queries)
-    grad_key_mat = transposed_times(normed_every, grad_keys)
-    grad_value_mat = transposed_times(normed_every, grad_values)
-    grad_norm_one = times_transposed(grad_queries, matrices[0]) + joined.astype(F32)
-    grad_gain_one = jnp.sum(grad_norm_one * residual * scale_one, axis=0)
-    hidden_grad = grad_first + norm_back(residual, scale_one, gains[0], grad_norm_one)
-
+    matrix_step = projection_grads(
+        normed_every,
+        grad_keys.reshape(group * tokens, width),
+        grad_values.reshape(group * tokens, width),
+        [
+            (normed_one, grad_queries),
+            (context, grad_first_low),
+            (normed_two, grad_cross_queries),
+            (placed, grad_second_low),
+        ],
+        (grad_cross_key_mat, grad_cross_value_mat),
+        share,
+    )
     lane = jnp.arange(2 * rows, dtype=jnp.int32)
     line = jnp.arange(8, dtype=jnp.int32)
     block = jnp.arange(group, dtype=jnp.int32)
@@ -935,34 +1202,18 @@
     hot = (bucket_of(between)[..., None] == jnp.arange(buckets, dtype=jnp.int32)).astype(F32)
     table_step = jnp.einsum("hjsl,jslb->bh", diagonal, hot, precision=lax.Precision.HIGHEST)
 
-    attn_step = jnp.stack(
-        [
-            part.astype(BF16)
-            for part in (
-                grad_query_mat,
-                grad_key_mat,
-                grad_value_mat,
-                grad_self_out,
-                grad_cross_query_mat,
-                grad_cross_key_mat,
-                grad_cross_value_mat,
-                grad_cross_out,
-            )
-        ]
-    )
-    vector_step = jnp.concatenate(
-        [grad_bias_input, grad_gain_one, grad_gain_two, grad_gain_three, grad_bias_output]
-    ).reshape(-1, vectors.shape[0])
-    devices = vector_step.shape[0]
-    small = jnp.concatenate(
-        [vector_step, jnp.broadcast_to(table_step.reshape(1, -1), (devices, buckets * heads))], axis=1
-    )
-    small_rows = -(-small.shape[1] // 1024) * 8
-    small = jnp.pad(small, ((0, 0), (0, small_rows * 128 - small.shape[1]))).reshape(devices, small_rows, 128)
-    attn_sum, small_sum = scatter_all(layout, [attn_step.reshape(devices, share, width), small], 2)
-    small_sum = small_sum.reshape(-1)
-    vector_sum = small_sum[: vectors.shape[0]]
-    table_sum = small_sum[vectors.shape[0] : vectors.shape[0] + buckets * heads].reshape(buckets, heads)
+    lines_of = lambda array: array.reshape(-1, 128)
+    table_rows = -(-buckets * heads // 128)
+    table_line = jnp.pad(table_step.reshape(-1), (0, table_rows * 128 - buckets * heads)).reshape(table_rows, 128)
+    attn_sum, line_sum, hidden_grad = last_steps(
+        layout, (lax.axis_size("dp"), group), blocks_of(matrix_step), share,
+        [lines_of(grad_bias_input), None, lines_of(grad_gain_two), grad_gain_three, grad_bias_output, table_line],
+        grad_queries, matrices[0], joined, hidden.reshape(tokens, width), gains[0], grad_first,
+    )
+    line_sum = line_sum.reshape(-1)
+    own = vectors.shape[0]
+    vector_sum = lax.dynamic_slice(line_sum, (lax.axis_index(AXES) * own,), (own,))
+    table_sum = line_sum[FF + 4 * width : FF + 4 * width + buckets * heads].reshape(buckets, heads)
     return (
         output.reshape(count, rows, width),
         hidden_grad.reshape(count, rows, width),

time: 525 us -> 495 us (0.943)
  matrix products: 172 us -> 56.2 us
  Pallas kernels: 237 us -> 312 us
  waiting for transfers between devices: 11.1 us -> 25.6 us
  starting transfers between devices: 16.5 us -> 30.6 us
  other arithmetic: 28.1 us -> 16 us
  local copies, waits for them, and re-layouts: 38.4 us -> 33 us
    pallas_call x1 -> x4, Pallas kernels: 68.8 us -> 135 us  [the longest x1 65.5 us: last_steps(): pl.pallas_call(body, out_shape=[jax.ShapeDtypeStruct(block, F32), jax.Sha...]
    dot_general x10 -> x0, matrix products: 45.9 us -> none  [transposed_times(): lax.dot_general(left_side, right_side, (((0,), (0,)), ((), ())), preferre...]
    dot_general x10 -> x5, matrix products: 63.3 us -> 23.5 us  [times_transposed(): lax.dot_general(left_side, right_side, (((1,), (1,)), ((), ())), preferre...]
    dot_general x10 -> x6, matrix products: 61.5 us -> 29.8 us  [product(): return jnp.dot(left_side, right_side, preferred_element_type=F32)]
    convert_element_type x3 -> x0, local copies, waits for them, and re-layouts: 18.4 us -> none  [the longest x1 6.29 us: per_device(): every = hidden_all.reshape(group * tokens, width).astype(F32)]
    ppermute x2, waiting for transfers between devices: 10.3 us -> 20.9 us  [sum_of_group(): came = lax.ppermute(away, 'fsdp', [(i, i ^ step) for i in range(group)])]
    pallas_call x1, Pallas kernels: 21.6 us -> 30.4 us  [span_attention_back(): pl.pallas_call(body, grid=(blocks,), in_specs=[q_spec, k_spec, k_spec, q_...]
    unnamed x104 -> x81, local copies, waits for them, and re-layouts: 11.6 us -> 19 us
  transfers between devices with their start and end apart: 9 -> 9, of which waited for: 1 -> 4; matrix products, arithmetic and copies ran while one was open for 36% -> 17% of each run, Pallas kernels for 46% -> 57%
where the time goes in v3:
time: 495 us; the launch traced here: 488 us
  Pallas kernels  312 us (63%)
  matrix products  56.2 us (11%)
  local copies, waits for them, and re-layouts  33 us (7%)
  starting transfers between devices  30.6 us (6%)
  waiting for transfers between devices  25.6 us (5%)
  other arithmetic  16 us (3%)
  between operations  14.9 us (3%)
    pallas_call x1, Pallas kernels, gather_with_tiles(): pl.pallas_call(body, out_shape=[jax.ShapeDtypeStruct((n,) + block.shape i...  80.9 us
    pallas_call x1, Pallas kernels, last_steps(): pl.pallas_call(body, out_shape=[jax.ShapeDtypeStruct(block, F32), jax.Sha...  65.5 us
    pallas_call x1, Pallas kernels, feed_forward(): pl.pallas_call(body, grid=(steps,), in_specs=[tall, line, tall, pl.BlockS...  33.8 us
    pallas_call x1, Pallas kernels, self_attention_back(): pl.pallas_call(body, grid_spec=grid_spec, out_shape=[jax.ShapeDtypeStruct...  33.3 us
    pallas_call x1, Pallas kernels, span_attention_back(): pl.pallas_call(body, grid=(blocks,), in_specs=[q_spec, k_spec, k_spec, q_...  30.4 us
    dot_general x6, matrix products, product(): return jnp.dot(left_side, right_side, preferred_element_type=F32)  29.8 us
    dot_general x5, matrix products, times_transposed(): lax.dot_general(left_side, right_side, (((1,), (1,)), ((), ())), preferre...  23.5 us
    pallas_call x1, Pallas kernels, self_attention(): pl.pallas_call(body, grid_spec=grid_spec, out_shape=[jax.ShapeDtypeStruct...  22.8 us
  transfers between devices with their start and end apart: 9, of which 4 were waited for; matrix products, arithmetic and copies ran while one was open for 17% of the time, Pallas kernels for 57%

profile of v3, /device:TPU:0, one launch (start us, length us, event | category | flops | bytes accessed | tf_op | source)
XLA Modules:
  0.0 488.4 jit_solution(8067021627416644408)
XLA Ops:
  10.2 80.9 %gather_all.1 = (bf16[7168,896]{1,0:T(8,128)(2,1)S(1)}, bf16[512,128]{1,0:T(8,128)(2,1)S(1)}, f32[14,5,256,256]{3,2,1,0:T(8,128)}) custom-call(bf16[224,896]{1,0:T(8,128)(2,1)S(1)} %copy-done.21, bf16[16,128]{1,0:T(8,128)(2,1)S(1)} %pad_bitcast_fusion.refs_1_, f32[14,5,1,512]{3,2,1,0:T(1,128)S(1)} %copy.28.refs_2_), custom_call_target="tpu_custom_call" | custom-call | tf_op jit(solution)/shard_map/gather_all/pallas_call | solution.py:255
  91.0 4.6 copy-done.7
  99.0 3.6 convolution_convert_fusion.5
  102.5 4.9 %fusion.57 = (bf16[896,896]{1,0:T(8,128)(2,1)}, bf16[896,896]{1,0:T(8,128)(2,1)}, bf16[896,896]{1,0:T(8,128)(2,1)}) fusion(bf16[7168,896]{1,0:T(8,128)(2,1)} %copy-done.7), kind=kLoop, calls=%fused_computation.114 | loop fusion | bytes 9633792 | tf_op jit(solution)/shard_map/slice | solution.py:1134
  111.5 8.4 %convolution_convert_fusion = bf16[2048,896]{1,0:T(8,128)(2,1)} fusion(bf16[2048,896]{1,0:T(8,128)(2,1)S(1)} %fusion.1.every_ref, bf16[7168,896]{1,0:T(8,128)(2,1)} %copy-done.7), kind=kOutput, calls=%fused_computation.7 | convolution fusion | flops 3290169344 | bytes 8945664 | tf_op jit(solution)/shard_map/dot_general | solution.py:626
  119.9 7.2 %convolution_convert_fusion.1 = bf16[2048,896]{1,0:T(8,128)(2,1)} fusion(bf16[2048,896]{1,0:T(8,128)(2,1)S(1)} %fusion.1.every_ref, bf16[7168,896]{1,0:T(8,128)(2,1)} %copy-done.7), kind=kOutput, calls=%fused_computation.8 | convolution fusion | flops 3290169344 | bytes 8945664 | tf_op jit(solution)/shard_map/dot_general | solution.py:626
  127.1 22.8 %self_attention.1 = (bf16[2,256,896]{2,1,0:T(8,128)(2,1)}, f32[7,2,128,256]{3,2,1,0:T(8,128)}, f32[7,4,256]{2,1,0:T(4,128)}) custom-call(s32[1]{0:T(128)} %bitcast.1.place_ref, bf16[2,256,896]{2,1,0:T(8,128)(2,1)} %bitcast.108, bf16[4,2,256,896]{3,2,1,0:T(8,128)(2,1)} %bitcast.102, bf16[4,2,256,896]{3,2,1,0:T(8,128)(2,1)} %bitcast.100, ...), custom_call_target="tpu_custom_call" | custom-call | flops 7516192768 | bytes 30000000 | tf_op jit(solution)/shard_map/self_attention/pallas_call | solution.py:753
  149.9 3.4 multiply_reduce_fusion.3
  159.6 12.9 %span_projection.1 = (bf16[8,256,896]{2,1,0:T(8,128)(2,1)}, bf16[8,256,896]{2,1,0:T(8,128)(2,1)}) custom-call(bf16[8,256,896]{2,1,0:T(8,128)(2,1)} %bitcast.112, bf16[896,896]{1,0:T(8,128)(2,1)} %get-tuple-element.86.mk_ref, bf16[896,896]{1,0:T(8,128)(2,1)} %get-tuple-element.85.mv_ref), custom_call_target="tpu_custom_call" | custom-call | flops 6576668672 | bytes 15000000 | tf_op jit(solution)/shard_map/span_projection/pallas_call | solution.py:967
  174.8 9.7 %span_attention.1 = bf16[8,64,896]{2,1,0:T(8,128)(2,1)} custom-call(bf16[8,64,896]{2,1,0:T(8,128)(2,1)} %bitcast.76, bf16[8,256,896]{2,1,0:T(8,128)(2,1)} %get-tuple-element.37.k_ref, bf16[8,256,896]{2,1,0:T(8,128)(2,1)} %get-tuple-element.38.v_ref), custom_call_target="tpu_custom_call" | custom-call | flops 1879048192 | bytes 12000000 | tf_op jit(solution)/shard_map/span_attention/pallas_call | solution.py:1017
  185.6 3.4 collective-permute-start.1
  190.8 3.9 convolution_add_fusion.sum_ref
  198.5 33.8 %feed_forward.1 = (bf16[512,896]{1,0:T(8,128)(2,1)}, f32[512,896]{1,0:T(8,128)S(1)}, f32[7,128]{1,0:T(8,128)S(1)}, f32[7,4,128]{2,1,0:T(4,128)S(1)}, f32[7,128]{...) custom-call(f32[512,896]{1,0:T(8,128)S(1)} %copy-done.8, f32[1,896]{1,0:T(1,128)S(1)} %slice.133.gain_ref, ...), custom_call_target="tpu_custom_call" | custom-call | flops 19730006016 | bytes 40000000 | tf_op jit(solution)/shard_map/feed_forward/pallas_call | solution.py:921
  237.2 3.8 collective-permute-done.2
  241.2 30.4 %span_attention_back.1 = (bf16[8,64,896]{2,1,0:T(8,128)(2,1)S(1)}, f32[8,256,896]{2,1,0:T(8,128)}, bf16[896,896]{1,0:T(8,128)(2,1)S(1)}, bf16[896,896]{1,0:T(8,128)(2,1)S(1)}) custom-call(bf16[8,64,896]{2,1,0:T(8,128)(2,1)S(1)} %bitcast.77, bf16[8,256,896]{2,1,0:T(8,128)(2,1)} %get-tuple-element.37.k_ref, bf16[8,256,896]{2,1,0:T(8,128)(2,1)} %get-tuple-element.38.v_ref, ...), custom_call_target="tpu_custom_call" | custom-call | flops 32883343360 | bytes 40000000 | tf_op jit(solution)/shard_map/span_attention_back/pallas_call | solution.py:1070
  274.9 13.1 %collective-permute-start.3 = (bf16[2,63,896]{2,1,0:T(8,128)(2,1)S(1)}, bf16[2,63,896]{2,1,0:T(8,128)(2,1)S(1)}, u32[]{:S(2)}, u32[]{:S(2)}) collective-permute-start(bf16[2,63,896]{2,1,0:T(8,128)(2,1)S(1)} %slice.157), channel_id=1, source_target_pairs={{0,1},{1,2},{2,3},{4,5},{5,6},{6,7},{8,9},{9,10},{10,11},{12,13},{... | collective-permute-start | bytes 677384 | tf_op jit(solution)/shard_map/ppermute | solution.py:604
  294.8 3.9 convolution_convert_fusion.2
  298.7 33.3 %self_attention_back.1 = (bf16[2,256,896]{2,1,0:T(8,128)(2,1)}, bf16[4,2,256,896]{3,2,1,0:T(8,128)(2,1)}, bf16[4,2,256,896]{3,2,1,0:T(8,128)(2,1)}, f32[14,4,8,512]{3,2,1,0:T(8,128)}) custom-call(s32[1]{0:T(128)} %bitcast.1.place_ref, bf16[2,256,896]{2,1,0:T(8,128)(2,1)} %bitcast.109, bf16[4,2,256,896]{3,2,1,0:T(8,128)(2,1)} %bitcast.103, ...), custom_call_target="tpu_custom_call" | custom-call | flops 18790481920 | bytes 40000000 | tf_op jit(solution)/shard_map/self_attention_back/pallas_call | solution.py:852
  332.1 7.2 %fusion.15 = f32[2048,896]{1,0:T(8,128)S(1)} fusion(bf16[2048,896]{1,0:T(8,128)(2,1)} %bitcast.115, bf16[7168,896]{1,0:T(8,128)(2,1)} %copy-done.7), kind=kOutput, calls=%fused_computation.38 | convolution fusion | flops 3288334336 | bytes 12615680 | tf_op jit(solution)/shard_map/dot_general | solution.py:630
  339.3 6.3 %add_convert_fusion = bf16[2048,896]{1,0:T(8,128)(2,1)S(1)} fusion(f32[2048,896]{1,0:T(8,128)S(1)} %fusion.15, bf16[2048,896]{1,0:T(8,128)(2,1)S(1)} %bitcast.118, bf16[7168,896]{1,0:T(8,128)(2,1)} %copy-done.7), kind=kOutput, calls=%fused_computation.4 | convolution fusion | flops 3292004352 | bytes 16285696 | tf_op jit(solution)/shard_map/dot_general | solution.py:630
  348.1 7.4 %collective-permute-start.4 = (bf16[2,512,896]{2,1,0:T(8,128)(2,1)}, bf16[2,512,896]{2,1,0:T(8,128)(2,1)S(1)}, u32[]{:S(2)}, u32[]{:S(2)}) collective-permute-start(bf16[2,512,896]{2,1,0:T(8,128)(2,1)} %dynamic-slice_bitcast_fusion), channel_id=1, source_target_pairs={{0,1},{1,0},{2,3},{3,2},{4,5},{5,4},{6,7},{7,6},{8,9},{9,8},{10,11... | collective-permute-start | bytes 5505032 | tf_op jit(solution)/shard_map/ppermute | solution.py:617
  364.5 22.7 %projection_grads.1 = bf16[8,896,896]{2,1,0:T(8,128)(2,1)} custom-call(s32[10]{0:T(128)S(1)} %copy-done.24, bf16[2048,896]{1,0:T(8,128)(2,1)} %copy-done.30, bf16[2048,896]{1,0:T(8,128)(2,1)} %bitcast.116, bf16[2048,896]{1,0:T(8,128)(2,1)} %bitcast.117, bf16[512,896]{1,0:T(8,128)(2,1)S(1)} %copy-done.15, bf16[512,896]{1,0:T(8,128)(2,1)S(1)} %bitcast.86, ...), custom_call_target="tpu_custom_call" | custom-call | flops 9865003008 | bytes 40000000 | tf_op jit(solution)/shard_map/projection_grads/pallas_call | solution.py:476
  387.2 20.3 %collective-permute-done.5 = bf16[1,512,896]{2,1,0:T(8,128)(2,1)S(1)} collective-permute-done((bf16[1,512,896]{2,1,0:T(8,128)(2,1)S(1)}, bf16[1,512,896]{2,1,0:T(8,128)(2,1)S(1)}, u32[]{:S(2)}, u32[]{:S(2)}) %collective-permute-start.5) | collective-permute-done | bytes 917536 | tf_op jit(solution)/shard_map/ppermute | solution.py:617
  409.0 65.5 %last_steps.1 = (f32[224,896]{1,0:T(8,128)S(1)}, f32[64,128]{1,0:T(8,128)S(1)}, f32[512,896]{1,0:T(8,128)S(1)}) custom-call(bf16[7168,896]{1,0:T(8,128)(2,1)} %bitcast.95, bf16[512,896]{1,0:T(8,128)(2,1)S(1)} %bitcast.87, bf16[896,896]{1,0:T(8,128)(2,1)S(1)} %copy-done.3, f32[512,896]{1,0:T(8,128)} %add_bitcast_fusion.refs_3_, ...), custom_call_target="tpu_custom_call" | custom-call | tf_op jit(solution)/shard_map/last_steps/pallas_call | solution.py:586
  (164 shorter events, 59.9 us)
Async XLA Ops:
  7.2 89.1 %copy-start.2 = (bf16[2,256,896]{2,1,0:T(8,128)(2,1)S(1)}, bf16[2,256,896]{2,1,0:T(8,128)(2,1)}, u32[]{:S(2)}) copy-start(bf16[2,256,896]{2,1,0:T(8,128)(2,1)} %param.9) | copy-start | bytes 2752516
  7.2 88.9 %copy-start.36 = (s32[2,2]{1,0:T(2,128)S(1)}, s32[2,2]{1,0:T(2,128)}, u32[]{:S(2)}) copy-start(s32[2,2]{1,0:T(2,128)} %param.11) | copy-start | bytes 52
  7.2 100.2 %all-gather.6.cloned.1.call-start = ((), (), s32[]{:S(2)}) async-start(), calls=%async_computation.3 | async-start | bytes 4587520 | tf_op jit(solution)/shard_map/all_gather | solution.py:1104
  7.9 187.9 %all-gather.4.cloned.1.call-start = ((), (), s32[]{:S(2)}) async-start(), calls=%async_computation.1 | async-start | bytes 13246464 | tf_op jit(solution)/shard_map/all_gather | solution.py:1104
  91.0 4.6 copy-start.7
  95.7 381.1 %reduce-scatter.2.cloned.1.call-start = ((), (), s32[]{:S(2)}) async-start(), calls=%async_computation.2 | async-start | bytes 13246464 | tf_op jit(solution)/shard_map/reduce_scatter | solution.py:1164
  111.5 8.4 %copy-start.30 = (bf16[2048,896]{1,0:T(8,128)(2,1)}, bf16[2048,896]{1,0:T(8,128)(2,1)S(1)}, u32[]{:S(2)}) copy-start(bf16[2048,896]{1,0:T(8,128)(2,1)S(1)} %fusion.1.every_ref) | copy-start | bytes 11010052
  153.3 37.4 %copy-start.27 = (f32[512,896]{1,0:T(8,128)}, f32[512,896]{1,0:T(8,128)S(1)}, u32[]{:S(2)}) copy-start(f32[512,896]{1,0:T(8,128)S(1)} %get-tuple-element.92) | copy-start | bytes 5505028
  157.9 15.9 %collective-permute-start = (bf16[2,63,896]{2,1,0:T(8,128)(2,1)S(1)}, bf16[2,63,896]{2,1,0:T(8,128)(2,1)S(1)}, u32[]{:S(2)}, u32[]{:S(2)}) collective-permute-start(bf16[2,63,896]{2,1,0:T(8,128)(2,1)S(1)} %slice.149), channel_id=1, source_target_pairs={{1,0},{2,1},{3,2},{5,4},{6,5},{7,6},{9,8},{10,9},{11,10},{13,12},{... | collective-permute-start | bytes 677384 | tf_op jit(solution)/shard_map/ppermute | solution.py:604
  185.6 5.0 %collective-permute-start.1 = (bf16[2,63,896]{2,1,0:T(8,128)(2,1)S(1)}, bf16[2,63,896]{2,1,0:T(8,128)(2,1)S(1)}, u32[]{:S(2)}, u32[]{:S(2)}) collective-permute-start(bf16[2,63,896]{2,1,0:T(8,128)(2,1)S(1)} %slice.150), channel_id=1, source_target_pairs={{0,1},{1,2},{2,3},{4,5},{5,6},{6,7},{8,9},{9,10},{10,11},{12,13},{... | collective-permute-start | bytes 677384 | tf_op jit(solution)/shard_map/ppermute | solution.py:604
  235.4 5.7 %copy-start.4 = (bf16[2,256,896]{2,1,0:T(8,128)(2,1)S(1)}, bf16[2,256,896]{2,1,0:T(8,128)(2,1)}, u32[]{:S(2)}) copy-start(bf16[2,256,896]{2,1,0:T(8,128)(2,1)} %pad_maximum_fusion) | copy-start | bytes 2752516
  235.5 5.6 %collective-permute-start.2 = (bf16[2,63,896]{2,1,0:T(8,128)(2,1)S(1)}, bf16[2,63,896]{2,1,0:T(8,128)(2,1)S(1)}, u32[]{:S(2)}, u32[]{:S(2)}) collective-permute-start(bf16[2,63,896]{2,1,0:T(8,128)(2,1)S(1)} %slice.156), channel_id=1, source_target_pairs={{1,0},{2,1},{3,2},{5,4},{6,5},{7,6},{9,8},{10,9},{11,10},{13,12},{... | collective-permute-start | bytes 677384 | tf_op jit(solution)/shard_map/ppermute | solution.py:604
  274.9 14.5 %collective-permute-start.3 = (bf16[2,63,896]{2,1,0:T(8,128)(2,1)S(1)}, bf16[2,63,896]{2,1,0:T(8,128)(2,1)S(1)}, u32[]{:S(2)}, u32[]{:S(2)}) collective-permute-start(bf16[2,63,896]{2,1,0:T(8,128)(2,1)S(1)} %slice.157), channel_id=1, source_target_pairs={{0,1},{1,2},{2,3},{4,5},{5,6},{6,7},{8,9},{9,10},{10,11},{12,13},{... | collective-permute-start | bytes 677384 | tf_op jit(solution)/shard_map/ppermute | solution.py:604
  294.8 3.9 copy-start.10
  332.1 7.2 %copy-start.37 = (bf16[4,2,256,896]{3,2,1,0:T(8,128)(2,1)S(1)}, bf16[4,2,256,896]{3,2,1,0:T(8,128)(2,1)}, u32[]{:S(2)}) copy-start(bf16[4,2,256,896]{3,2,1,0:T(8,128)(2,1)} %get-tuple-element.46) | copy-start | bytes 11010052
  345.7 9.8 %copy-start.35 = (f32[4,224]{1,0:T(4,128)S(1)}, f32[4,224]{1,0:T(4,128)}, u32[]{:S(2)}) copy-start(f32[4,224]{1,0:T(4,128)} %copy-done.34) | copy-start | bytes 10756
  348.1 11.0 %collective-permute-start.4 = (bf16[2,512,896]{2,1,0:T(8,128)(2,1)}, bf16[2,512,896]{2,1,0:T(8,128)(2,1)S(1)}, u32[]{:S(2)}, u32[]{:S(2)}) collective-permute-start(bf16[2,512,896]{2,1,0:T(8,128)(2,1)} %dynamic-slice_bitcast_fusion), channel_id=1, source_target_pairs={{0,1},{1,0},{2,3},{3,2},{4,5},{5,4},{6,7},{7,6},{8,9},{9,8},{10,11... | collective-permute-start | bytes 5505032 | tf_op jit(solution)/shard_map/ppermute | solution.py:617
  359.1 5.4 %copy-start.13 = (bf16[2,256,896]{2,1,0:T(8,128)(2,1)S(1)}, bf16[2,256,896]{2,1,0:T(8,128)(2,1)}, u32[]{:S(2)}) copy-start(bf16[2,256,896]{2,1,0:T(8,128)(2,1)} %copy-done.12) | copy-start | bytes 2752516
  359.1 5.4 %copy-start.15 = (bf16[512,896]{1,0:T(8,128)(2,1)S(1)}, bf16[512,896]{1,0:T(8,128)(2,1)}, u32[]{:S(2)}) copy-start(bf16[512,896]{1,0:T(8,128)(2,1)} %copy-done.14) | copy-start | bytes 2752516
  359.1 5.4 %copy-start.17 = (bf16[512,896]{1,0:T(8,128)(2,1)S(1)}, bf16[512,896]{1,0:T(8,128)(2,1)}, u32[]{:S(2)}) copy-start(bf16[512,896]{1,0:T(8,128)(2,1)} %copy-done.16) | copy-start | bytes 2752516
  359.1 5.4 %copy-start.18 = (bf16[2,256,896]{2,1,0:T(8,128)(2,1)S(1)}, bf16[2,256,896]{2,1,0:T(8,128)(2,1)}, u32[]{:S(2)}) copy-start(bf16[2,256,896]{2,1,0:T(8,128)(2,1)} %get-tuple-element.47) | copy-start | bytes 2752516
  359.2 5.4 %copy-start.23 = (bf16[2,256,896]{2,1,0:T(8,128)(2,1)S(1)}, bf16[2,256,896]{2,1,0:T(8,128)(2,1)}, u32[]{:S(2)}) copy-start(bf16[2,256,896]{2,1,0:T(8,128)(2,1)} %get-tuple-element.36) | copy-start | bytes 2752516
  361.4 46.1 %collective-permute-start.5 = (bf16[1,512,896]{2,1,0:T(8,128)(2,1)S(1)}, bf16[1,512,896]{2,1,0:T(8,128)(2,1)S(1)}, u32[]{:S(2)}, u32[]{:S(2)}) collective-permute-start(bf16[1,512,896]{2,1,0:T(8,128)(2,1)S(1)} %constant_dynamic-slice_fusion), channel_id=1, source_target_pairs={{0,2},{1,3},{2,0},{3,1},{4,6},{5,7},{6,4},{7,5},{8,10},{9,11},{10,... | collective-permute-start | bytes 2752520 | tf_op jit(solution)/shard_map/ppermute | solution.py:617
  387.2 21.7 %copy-start.3 = (bf16[896,896]{1,0:T(8,128)(2,1)S(1)}, bf16[896,896]{1,0:T(8,128)(2,1)}, u32[]{:S(2)}) copy-start(bf16[896,896]{1,0:T(8,128)(2,1)} %get-tuple-element.84.refs_2_) | copy-start | bytes 4816900
  (23 other events, 46.1 us)
Sparse Core Ops, SparseCore 0:
  9.6 52.8 all-gather.5
  95.8 99.9 all-gather.3
  232.4 173.2 reduce-scatter.1

commit v4 on v3

--- a/solution.py
+++ b/solution.py
@@ -262,7 +262,7 @@
         in_specs=[inside] * (count + 1),
         out_specs=[anywhere] * (count + 1),
         scratch_shapes=scratch,
-        compiler_params=pltpu.CompilerParams(collective_id=1, has_side_effects=True, vmem_limit_bytes=40_000_000),
+        compiler_params=pltpu.CompilerParams(collective_id=1, has_side_effects=True, vmem_limit_bytes=60_000_000),
         name="gather_all",
     )(*blocks, lines)
     return gathered, tiles
@@ -513,7 +513,7 @@
         loads = [
             pltpu.make_async_copy(src, dst, load_sem.at[i])
             for i, (src, dst) in enumerate(
-                ((dq_ref, q_buf), (m0_ref, m0), (in_ref, in_buf), (hid_ref, hid_buf), (gf_ref, first_buf))
+                ((dq_ref, q_buf), (m0_ref.at[0], m0), (in_ref, in_buf), (hid_ref, hid_buf), (gf_ref, first_buf))
             )
         ]
         big = Reduction(place, mats_ref, row_tiles(share), (0, width), buffers)
@@ -867,57 +867,42 @@
     return pl.BlockSpec(shape, lambda *_: (0,) * len(shape))
 
 
-def feed_forward(second_sum, gain, grad_out_low, weights, bias_input, bias_output):
+FF_TILE = 512
+
+
+def feed_forward_grads(second_sum, gain, grad_out_low, weights, bias_input):
     tokens, width = second_sum.shape
     units = bias_input.shape[0]
-    tile = 512
+    tile = FF_TILE
     steps = units // tile
     part = 256
 
-    def body(sum_ref, gain_ref, go_ref, wi_ref, wo_ref, bi_ref, bo_ref, out_ref, gs_ref, gg_ref, gbi_ref, gbo_ref, gw_ref, n_ref, acc_ref, gn_ref):
+    def body(sum_ref, gain_ref, go_ref, wi_ref, wo_ref, bi_ref, act_ref, gp_ref, gbi_ref, gw_ref, n_ref):
         step = pl.program_id(0)
 
         @pl.when(step == 0)
         def _():
             held = sum_ref[...]
             n_ref[...] = (held * inverse_rms(held) * gain_ref[...]).astype(BF16)
-            acc_ref[...] = jnp.zeros_like(acc_ref)
-            gn_ref[...] = jnp.zeros_like(gn_ref)
 
         normed = n_ref[...]
         incoming = go_ref[...]
         for at in range(0, tile, part):
             rows = slice(at, at + part)
-            w_in, w_out = wi_ref[rows, :], wo_ref[rows, :]
-            value, slope = gelu_parts(dot_t(normed, w_in) + bi_ref[0, :, rows])
+            value, slope = gelu_parts(dot_t(normed, wi_ref[rows, :]) + bi_ref[0, :, rows])
             value_low = value.astype(BF16)
-            grad_pre = dot_t(incoming, w_out) * slope
+            grad_pre = dot_t(incoming, wo_ref[rows, :]) * slope
             bias_grad = jnp.sum(grad_pre, axis=0, keepdims=True)
             for i in range(part // 128):
                 gbi_ref[0, at // 128 + i : at // 128 + i + 1, :] = bias_grad[:, i * 128 : (i + 1) * 128]
             grad_pre_low = grad_pre.astype(BF16)
-            acc_ref[...] += product(value_low, w_out)
-            gn_ref[...] += product(grad_pre_low, w_in)
+            act_ref[:, rows] = value_low
+            gp_ref[:, rows] = grad_pre_low
             gw_ref[0, 0, rows, :] = transposed_times(grad_pre_low, normed).astype(BF16)
             gw_ref[1, 0, rows, :] = transposed_times(value_low, incoming).astype(BF16)
 
-        @pl.when(step == steps - 1)
-        def _():
-            held = sum_ref[...]
-            scale = inverse_rms(held)
-            out_ref[...] = (held + acc_ref[...] + bo_ref[...]).astype(BF16)
-            grad_norm = gn_ref[...]
-            grad_out = incoming.astype(F32)
-            for ref, line in (
-                (gbo_ref, jnp.sum(grad_out, axis=0, keepdims=True)),
-                (gg_ref, jnp.sum(grad_norm * held * scale, axis=0, keepdims=True)),
-            ):
-                for i in range(width // 128):
-                    ref[i : i + 1, :] = line[:, i * 128 : (i + 1) * 128]
-            gs_ref[...] = grad_out + norm_back(held, scale, gain_ref[...], grad_norm)
-
     tall, line = whole((tokens, width)), whole((1, width))
-    rows_of_128 = whole((width // 128, 128))
+    across = pl.BlockSpec((tokens, tile), lambda i: (0, i))
     return pl.pallas_call(
         body,
         grid=(steps,),
@@ -926,53 +911,146 @@
             pl.BlockSpec((tile, width), lambda i: (i, 0)),
             pl.BlockSpec((tile, width), lambda i: (i + steps, 0)),
             pl.BlockSpec((1, 1, tile), lambda i: (i, 0, 0)),
-            line,
         ],
         out_specs=[
-            tall, tall, rows_of_128,
+            across, across,
             pl.BlockSpec((1, tile // 128, 128), lambda i: (i, 0, 0)),
-            rows_of_128,
             pl.BlockSpec((2, 1, tile, width), lambda i: (0, i, 0, 0)),
         ],
+        out_shape=[
+            jax.ShapeDtypeStruct((tokens, units), BF16),
+            jax.ShapeDtypeStruct((tokens, units), BF16),
+            jax.ShapeDtypeStruct((steps, tile // 128, 128), F32),
+            jax.ShapeDtypeStruct((2, steps, tile, width), BF16),
+        ],
+        scratch_shapes=[pltpu.VMEM((tokens, width), BF16)],
+        cost_estimate=pl.CostEstimate(flops=8 * tokens * width * units, transcendentals=0, bytes_accessed=40_000_000),
+        compiler_params=pltpu.CompilerParams(vmem_limit_bytes=50_000_000),
+        name="feed_forward_grads",
+    )(second_sum, gain.reshape(1, width), grad_out_low, weights, weights, bias_input.reshape(steps, 1, tile))
+
+
+def feed_forward_sums(second_sum, gain, grad_out_low, weights, activated, grad_pre_low, bias_output):
+    tokens, width = second_sum.shape
+    tile = FF_TILE
+    steps = activated.shape[1] // tile
+
+    def body(sum_ref, gain_ref, go_ref, wi_ref, wo_ref, act_ref, gp_ref, bo_ref, out_ref, gs_ref, gg_ref, gbo_ref, acc_ref, gn_ref):
+        step = pl.program_id(0)
+        out_part = product(act_ref[...], wo_ref[...])
+        norm_part = product(gp_ref[...], wi_ref[...])
+
+        @pl.when(step == 0)
+        def _():
+            acc_ref[...] = out_part
+            gn_ref[...] = norm_part
+
+        @pl.when(step > 0)
+        def _():
+            acc_ref[...] += out_part
+            gn_ref[...] += norm_part
+
+        @pl.when(step == steps - 1)
+        def _():
+            held = sum_ref[...]
+            scale = inverse_rms(held)
+            out_ref[...] = (held + acc_ref[...] + bo_ref[...]).astype(BF16)
+            grad_norm = gn_ref[...]
+            grad_out = go_ref[...].astype(F32)
+            for ref, line in (
+                (gbo_ref, jnp.sum(grad_out, axis=0, keepdims=True)),
+                (gg_ref, jnp.sum(grad_norm * held * scale, axis=0, keepdims=True)),
+            ):
+                for i in range(width // 128):
+                    ref[i : i + 1, :] = line[:, i * 128 : (i + 1) * 128]
+            gs_ref[...] = grad_out + norm_back(held, scale, gain_ref[...], grad_norm)
+
+    tall, line = whole((tokens, width)), whole((1, width))
+    rows_of_128 = whole((width // 128, 128))
+    across = pl.BlockSpec((tokens, tile), lambda i: (0, i))
+    return pl.pallas_call(
+        body,
+        grid=(steps,),
+        in_specs=[
+            tall, line, tall,
+            pl.BlockSpec((tile, width), lambda i: (i, 0)),
+            pl.BlockSpec((tile, width), lambda i: (i + steps, 0)),
+            across, across, line,
+        ],
+        out_specs=[tall, tall, rows_of_128, rows_of_128],
         out_shape=[
             jax.ShapeDtypeStruct((tokens, width), BF16),
             jax.ShapeDtypeStruct((tokens, width), F32),
             jax.ShapeDtypeStruct((width // 128, 128), F32),
-            jax.ShapeDtypeStruct((steps, tile // 128, 128), F32),
             jax.ShapeDtypeStruct((width // 128, 128), F32),
-            jax.ShapeDtypeStruct((2, steps, tile, width), BF16),
-        ],
-        scratch_shapes=[
-            pltpu.VMEM((tokens, width), BF16),
-            pltpu.VMEM((tokens, width), F32),
-            pltpu.VMEM((tokens, width), F32),
-        ],
-        cost_estimate=pl.CostEstimate(flops=12 * tokens * width * units, transcendentals=0, bytes_accessed=40_000_000),
+        ],
+        scratch_shapes=[pltpu.VMEM((tokens, width), F32), pltpu.VMEM((tokens, width), F32)],
+        cost_estimate=pl.CostEstimate(flops=4 * tokens * width * steps * tile, transcendentals=0, bytes_accessed=25_000_000),
         compiler_params=pltpu.CompilerParams(vmem_limit_bytes=50_000_000),
-        name="feed_forward",
+        name="feed_forward_sums",
     )(
-        second_sum, gain.reshape(1, width), grad_out_low, weights, weights,
-        bias_input.reshape(steps, 1, tile), bias_output.reshape(1, width),
-    )
-
-
-def span_projection(near, key_matrix, value_matrix):
+        second_sum, gain.reshape(1, width), grad_out_low, weights, weights, activated, grad_pre_low,
+        bias_output.reshape(1, width),
+    )
+
+
+def self_projection(place, hidden_all, gain, matrices, tokens):
+    total, width = hidden_all.shape
+    rows = 256
+    own = tokens // rows
+
+    def body(place_ref, hid_ref, gain_ref, m0_ref, m1_ref, m2_ref, q_ref, k_ref, v_ref, every_ref, one_ref):
+        held = hid_ref[...].astype(F32)
+        normed = (held * inverse_rms(held) * gain_ref[...]).astype(BF16)
+        every_ref[...] = normed
+        k_ref[...] = product(normed, m1_ref[0]).astype(BF16)
+        v_ref[...] = product(normed, m2_ref[0]).astype(BF16)
+
+        @pl.when(pl.program_id(0) // own == place_ref[0])
+        def _():
+            one_ref[...] = normed
+            q_ref[...] = product(normed, m0_ref[0]).astype(BF16)
+
+    block = pl.BlockSpec((rows, width), lambda i, _: (i, 0))
+    mine = pl.BlockSpec((rows, width), lambda i, place_ref: (jnp.clip(i - place_ref[0] * own, 0, own - 1), 0))
+    matrix = lambda m: pl.BlockSpec((1, width, width), lambda i, _: (m, 0, 0))
+    return pl.pallas_call(
+        body,
+        grid_spec=pltpu.PrefetchScalarGridSpec(
+            num_scalar_prefetch=1,
+            grid=(total // rows,),
+            in_specs=[block, pl.BlockSpec((1, width), lambda i, _: (0, 0)), matrix(0), matrix(1), matrix(2)],
+            out_specs=[mine, block, block, block, mine],
+        ),
+        out_shape=[
+            jax.ShapeDtypeStruct((tokens, width), BF16),
+            jax.ShapeDtypeStruct((total, width), BF16),
+            jax.ShapeDtypeStruct((total, width), BF16),
+            jax.ShapeDtypeStruct((total, width), BF16),
+            jax.ShapeDtypeStruct((tokens, width), BF16),
+        ],
+        cost_estimate=pl.CostEstimate(flops=5 * total * width * width, transcendentals=0, bytes_accessed=25_000_000),
+        name="self_projection",
+    )(place, hidden_all, gain.reshape(1, width), matrices, matrices, matrices)
+
+
+def span_projection(near, matrices):
     blocks, rows, width = near.shape
 
     def body(near_ref, mk_ref, mv_ref, k_ref, v_ref):
-        k_ref[0] = product(near_ref[0], mk_ref[...]).astype(BF16)
-        v_ref[0] = product(near_ref[0], mv_ref[...]).astype(BF16)
+        k_ref[0] = product(near_ref[0], mk_ref[0]).astype(BF16)
+        v_ref[0] = product(near_ref[0], mv_ref[0]).astype(BF16)
 
     block = pl.BlockSpec((1, rows, width), lambda i: (i, 0, 0))
     return pl.pallas_call(
         body,
         grid=(blocks,),
-        in_specs=[block, whole((width, width)), whole((width, width))],
+        in_specs=[block] + [pl.BlockSpec((1, width, width), lambda i, m=m: (m, 0, 0)) for m in (5, 6)],
         out_specs=[block, block],
         out_shape=[jax.ShapeDtypeStruct(near.shape, BF16)] * 2,
         cost_estimate=pl.CostEstimate(flops=4 * blocks * rows * width * width, transcendentals=0, bytes_accessed=15_000_000),
         name="span_projection",
-    )(near, key_matrix, value_matrix)
+    )(near, matrices, matrices)
 
 
 def both_heads(values, head_size):
@@ -1025,7 +1103,7 @@
     )(query, keys, values)
 
 
-def span_attention_back(query, keys, values, grad, near, key_matrix, value_matrix, head_size):
+def span_attention_back(query, keys, values, grad, near, matrices, head_size):
     blocks, rows, width = query.shape
     span_keys = keys.shape[1]
 
@@ -1046,7 +1124,7 @@
         turned = flipped(k)
         wide = [(product(turned[g], ds_low[:, g]) * 0.125).T for g in groups]
         dq_ref[0] = side_by_side([picked(w, rows, head_size) for w in wide]).astype(BF16)
-        dn_ref[0] = dot_t(dk, mk_ref[...]) + dot_t(dv, mv_ref[...])
+        dn_ref[0] = dot_t(dk, mk_ref[0]) + dot_t(dv, mv_ref[0])
         near_t = flipped(near_ref[0])
 
         @pl.when(step == 0)
@@ -1070,7 +1148,8 @@
     return pl.pallas_call(
         body,
         grid=(blocks,),
-        in_specs=[q_spec, k_spec, k_spec, q_spec, k_spec, square, square],
+        in_specs=[q_spec, k_spec, k_spec, q_spec, k_spec]
+        + [pl.BlockSpec((1, width, width), lambda i, m=m: (m, 0, 0)) for m in (5, 6)],
         out_specs=[q_spec, k_spec, square, square],
         out_shape=[
             jax.ShapeDtypeStruct(query.shape, BF16),
@@ -1082,7 +1161,7 @@
         cost_estimate=pl.CostEstimate(flops=20 * blocks * span_keys * width * width, transcendentals=0, bytes_accessed=40_000_000),
         compiler_params=pltpu.CompilerParams(vmem_limit_bytes=50_000_000),
         name="span_attention_back",
-    )(query, keys, values, grad, near, key_matrix, value_matrix)
+    )(query, keys, values, grad, near, matrices, matrices)
 
 
 def per_device(hidden, neighbours, piece_starts, out_grad, attn_weights, ffw_weights, vectors, rel_table):
@@ -1109,7 +1188,7 @@
     (attn_full, vector_full), tiles = gather_with_tiles(
         layout, [attn_weights, vector_block], bias_lines(rel_table, rows, reach), rows
     )
-    ffw_full = gather(lax.optimization_barrier((ffw_weights, vector_full))[0], AXES)
+    ffw_full = gather(ffw_weights, AXES)
     matrices = attn_full.reshape(8, width, width)
     vector_full = vector_full.reshape(-1, vector_rows * 128)[:, : vectors.shape[0]].reshape(-1).astype(F32)
     bias_input = vector_full[:FF]
@@ -1127,15 +1206,14 @@
     place_arg = place.reshape(1)
 
     residual = hidden.reshape(tokens, width).astype(F32)
-    every = hidden_all.reshape(group * tokens, width).astype(F32)
-    normed_every = (every * inverse_rms(every) * gains[0]).astype(BF16)
-    scale_one = inverse_rms(residual)
-    normed_one = (residual * scale_one * gains[0]).astype(BF16)
-    queries = product(normed_one, matrices[0]).astype(BF16).reshape(count, rows, width)
-    keys = product(normed_every, matrices[1]).astype(BF16).reshape(group, count, rows, width)
-    values = product(normed_every, matrices[2]).astype(BF16).reshape(group, count, rows, width)
+    queries, keys, values, normed_every, normed_one = self_projection(
+        place_arg, hidden_all.reshape(group * tokens, width), gains[0], matrices, tokens
+    )
+    queries = queries.reshape(count, rows, width)
+    keys = keys.reshape(group, count, rows, width)
+    values = values.reshape(group, count, rows, width)
     near = neighbours.reshape(count * spans, span_keys, width)
-    cross_keys, cross_values = span_projection(near, matrices[5], matrices[6])
+    cross_keys, cross_values = span_projection(near, matrices)
     context, context_t, lse = self_attention(
         place_arg, queries, keys, values, tiles, mask, head_size, reach
     )
@@ -1157,15 +1235,19 @@
     block_queries = ahead(cross_queries)
     placed = behind(span_attention(block_queries, cross_keys, cross_values, head_size))
     second_sum = first_sum + product(placed, matrices[7])
-    output, grad_second, grad_gain_three, grad_bias_input, grad_bias_output, ffw_step = feed_forward(
-        second_sum, gains[2], out_grad.reshape(tokens, width), ffw_full, bias_input, bias_output
+    out_low = out_grad.reshape(tokens, width)
+    activated, grad_pre_low, grad_bias_input, ffw_step = feed_forward_grads(
+        second_sum, gains[2], out_low, ffw_full, bias_input
+    )
+    output, grad_second, grad_gain_three, grad_bias_output = feed_forward_sums(
+        second_sum, gains[2], out_low, ffw_full, activated, grad_pre_low, bias_output
     )
     blocks_of = lambda array: array.reshape((-1, width) if row_tiles(share) else (-1, share, width))
     ffw_sum = lax.psum_scatter(ffw_step.reshape(2 * FF, width), AXES, scatter_dimension=0, tiled=True)
     grad_second_low = grad_second.astype(BF16)
     grad_placed = times_transposed(grad_second_low, matrices[7]).astype(BF16).reshape(count, rows, width)
     grad_block_queries, near_grad, grad_cross_key_mat, grad_cross_value_mat = span_attention_back(
-        block_queries, cross_keys, cross_values, ahead(grad_placed), near, matrices[5], matrices[6], head_size
+        block_queries, cross_keys, cross_values, ahead(grad_placed), near, matrices, head_size
     )
     grad_cross_queries = behind(grad_block_queries)
     grad_norm_two = times_transposed(grad_cross_queries, matrices[4])
@@ -1208,7 +1290,7 @@
     attn_sum, line_sum, hidden_grad = last_steps(
         layout, (lax.axis_size("dp"), group), blocks_of(matrix_step), share,
         [lines_of(grad_bias_input), None, lines_of(grad_gain_two), grad_gain_three, grad_bias_output, table_line],
-        grad_queries, matrices[0], joined, hidden.reshape(tokens, width), gains[0], grad_first,
+        grad_queries, matrices, joined, hidden.reshape(tokens, width), gains[0], grad_first,
     )
     line_sum = line_sum.reshape(-1)
     own = vectors.shape[0]

time: 495 us -> 478 us (0.966)
  Pallas kernels: 312 us -> 341 us
  matrix products: 56.2 us -> 35.8 us
  waiting for transfers between devices: 25.6 us -> 11.9 us
  local copies, waits for them, and re-layouts: 33 us -> 23.4 us
    pallas_call x2 -> x4, Pallas kernels: 46.7 us -> 71.7 us  [the longest x1 26.5 us: feed_forward_grads(): pl.pallas_call(body, grid=(steps,), in_specs=[tall, line, tall, pl.BlockS...]
    dot_general x6 -> x3, matrix products: 29.8 us -> 9.62 us  [product(): return jnp.dot(left_side, right_side, preferred_element_type=F32)]
    ppermute x2, waiting for transfers between devices: 20.9 us -> 5.88 us  [sum_of_group(): came = lax.ppermute(away, 'fsdp', [(i, i ^ step) for i in range(group)])]
    unnamed x81 -> x65, local copies, waits for them, and re-layouts: 19 us -> 13.6 us
  transfers between devices with their start and end apart: 9 -> 9, of which waited for: 4 -> 3; matrix products, arithmetic and copies ran while one was open for 17% -> 12% of each run, Pallas kernels for 57% -> 67%
where the time goes in v4:
time: 478 us; the launch traced here: 469 us
  Pallas kernels  341 us (71%)
  matrix products  35.8 us (7%)
  starting transfers between devices  30.3 us (6%)
  local copies, waits for them, and re-layouts  23.4 us (5%)
  between operations  14.6 us (3%)
  other arithmetic  12 us (3%)
  waiting for transfers between devices  11.9 us (2%)
    pallas_call x1, Pallas kernels, gather_with_tiles(): pl.pallas_call(body, out_shape=[jax.ShapeDtypeStruct((n,) + block.shape i...  85.2 us
    pallas_call x1, Pallas kernels, last_steps(): pl.pallas_call(body, out_shape=[jax.ShapeDtypeStruct(block, F32), jax.Sha...  64.6 us
    pallas_call x1, Pallas kernels, self_attention_back(): pl.pallas_call(body, grid_spec=grid_spec, out_shape=[jax.ShapeDtypeStruct...  33.3 us
    pallas_call x1, Pallas kernels, span_attention_back(): pl.pallas_call(body, grid=(blocks,), in_specs=[q_spec, k_spec, k_spec, q_...  30.2 us
    pallas_call x1, Pallas kernels, feed_forward_grads(): pl.pallas_call(body, grid=(steps,), in_specs=[tall, line, tall, pl.BlockS...  26.5 us
    dot_general x5, matrix products, times_transposed(): lax.dot_general(left_side, right_side, (((1,), (1,)), ((), ())), preferre...  23.2 us
    pallas_call x1, Pallas kernels, projection_grads(): pl.pallas_call(body, grid_spec=pltpu.PrefetchScalarGridSpec(num_scalar_pr...  22.9 us
    pallas_call x1, Pallas kernels, self_attention(): pl.pallas_call(body, grid_spec=grid_spec, out_shape=[jax.ShapeDtypeStruct...  22.8 us
  transfers between devices with their start and end apart: 9, of which 3 were waited for; matrix products, arithmetic and copies ran while one was open for 12% of the time, Pallas kernels for 67%

profile of v4, /device:TPU:0, one launch (start us, length us, event | category | flops | bytes accessed | tf_op | source)
XLA Modules:
  0.0 468.5 jit_solution(15766666965816016459)
XLA Ops:
  12.0 85.2 %gather_all.1 = (bf16[7168,896]{1,0:T(8,128)(2,1)}, bf16[512,128]{1,0:T(8,128)(2,1)}, f32[14,5,256,256]{3,2,1,0:T(8,128)}) custom-call(bf16[224,896]{1,0:T(8,128)(2,1)} %refs_0_.1, bf16[16,128]{1,0:T(8,128)(2,1)} %pad_bitcast_fusion.refs_1_, f32[14,5,1,512]{3,2,1,0:T(1,128)} %copy.28.refs_2_), custom_call_target="tpu_custom_call" | custom-call | tf_op jit(solution)/shard_map/gather_all/pallas_call | solution.py:255
  101.2 16.6 %self_projection.1 = (bf16[512,896]{1,0:T(8,128)(2,1)}, bf16[2048,896]{1,0:T(8,128)(2,1)}, bf16[2048,896]{1,0:T(8,128)(2,1)}, bf16[2048,896]{1,0:T(8,128)(2,1)}, bf16[512,896]{1,0:T(8,128)(2,1)}) custom-call(s32[1]{0:T(128)} %bitcast.1.place_ref, bf16[2048,896]{1,0:T(8,128)(2,1)} %bitcast.101, f32[1,896]{1,0:T(1,128)} %slice.98.gain_ref.refs_6_, ...), custom_call_target="tpu_custom_call" | custom-call | flops 8220835840 | bytes 25000000 | tf_op jit(solution)/shard_map/self_projection/pallas_call | solution.py:1017
  117.8 22.8 %self_attention.1 = (bf16[2,256,896]{2,1,0:T(8,128)(2,1)}, f32[7,2,128,256]{3,2,1,0:T(8,128)}, f32[7,4,256]{2,1,0:T(4,128)}) custom-call(s32[1]{0:T(128)} %bitcast.1.place_ref, bf16[2,256,896]{2,1,0:T(8,128)(2,1)} %bitcast.106, bf16[4,2,256,896]{3,2,1,0:T(8,128)(2,1)} %bitcast.97, bf16[4,2,256,896]{3,2,1,0:T(8,128)(2,1)} %bitcast.99, ...), custom_call_target="tpu_custom_call" | custom-call | flops 7516192768 | bytes 30000000 | tf_op jit(solution)/shard_map/self_attention/pallas_call | solution.py:753
  140.5 3.0 multiply_reduce_fusion.2
  143.8 3.4 convolution_convert_fusion.2
  148.5 12.9 %span_projection.1 = (bf16[8,256,896]{2,1,0:T(8,128)(2,1)}, bf16[8,256,896]{2,1,0:T(8,128)(2,1)}) custom-call(bf16[8,256,896]{2,1,0:T(8,128)(2,1)} %bitcast.93, bf16[8,896,896]{2,1,0:T(8,128)(2,1)} %bitcast.84, bf16[8,896,896]{2,1,0:T(8,128)(2,1)} %bitcast.85), custom_call_target="tpu_custom_call" | custom-call | flops 6576668672 | bytes 15000000 | tf_op jit(solution)/shard_map/span_projection/pallas_call | solution.py:1045
  162.7 9.9 %span_attention.1 = bf16[8,64,896]{2,1,0:T(8,128)(2,1)} custom-call(bf16[8,64,896]{2,1,0:T(8,128)(2,1)} %bitcast.60, bf16[8,256,896]{2,1,0:T(8,128)(2,1)} %get-tuple-element.46.k_ref, bf16[8,256,896]{2,1,0:T(8,128)(2,1)} %get-tuple-element.47.v_ref), custom_call_target="tpu_custom_call" | custom-call | flops 1879048192 | bytes 12000000 | tf_op jit(solution)/shard_map/span_attention/pallas_call | solution.py:1095
  173.6 2.7 collective-permute-start.1
  177.9 3.2 convolution_add_fusion.sum_ref
  183.0 26.5 %feed_forward_grads.1 = (bf16[512,3584]{1,0:T(8,128)(2,1)S(1)}, bf16[512,3584]{1,0:T(8,128)(2,1)}, f32[7,4,128]{2,1,0:T(4,128)S(1)}, bf16[2,7,512,896]{3,2,1,0:T(8,128)(2,1)}) custom-call(f32[512,896]{1,0:T(8,128)S(1)} %convolution_add_fusion.sum_ref, f32[1,896]{1,0:T(1,128)S(1)} %slice.109.gain_ref, bf16[512,896]{1,0:T(8,128)(2,1)S(1)} %bitcast.72, ...), custom_call_target="tpu_custom_call" | custom-call | flops 13153337344 | bytes 40000000 | tf_op jit(solution)/shard_map/feed_forward_grads/pallas_call | solution.py:906
  214.1 15.8 %feed_forward_sums.1 = (bf16[512,896]{1,0:T(8,128)(2,1)}, f32[512,896]{1,0:T(8,128)S(1)}, f32[7,128]{1,0:T(8,128)S(1)}, f32[7,128]{1,0:T(8,128)S(1)}) custom-call(f32[512,896]{1,0:T(8,128)S(1)} %copy-done.3, f32[1,896]{1,0:T(1,128)S(1)} %slice.109.gain_ref, bf16[512,896]{1,0:T(8,128)(2,1)S(1)} %bitcast.73, ...), custom_call_target="tpu_custom_call" | custom-call | flops 6576668672 | bytes 25000000 | tf_op jit(solution)/shard_map/feed_forward_sums/pallas_call | solution.py:971
  230.0 3.0 convolution_convert_fusion.1
  234.6 4.6 collective-permute-done.2
  239.3 30.2 %span_attention_back.1 = (bf16[8,64,896]{2,1,0:T(8,128)(2,1)S(1)}, f32[8,256,896]{2,1,0:T(8,128)}, bf16[896,896]{1,0:T(8,128)(2,1)S(1)}, bf16[896,896]{1,0:T(8,128)(2,1)S(1)}) custom-call(bf16[8,64,896]{2,1,0:T(8,128)(2,1)S(1)} %bitcast.61, bf16[8,256,896]{2,1,0:T(8,128)(2,1)} %get-tuple-element.46.k_ref, bf16[8,256,896]{2,1,0:T(8,128)(2,1)} %get-tuple-element.47.v_ref, ...), custom_call_target="tpu_custom_call" | custom-call | flops 32883343360 | bytes 40000000 | tf_op jit(solution)/shard_map/span_attention_back/pallas_call | solution.py:1148
  272.9 14.6 %collective-permute-start.3 = (bf16[2,63,896]{2,1,0:T(8,128)(2,1)S(1)}, bf16[2,63,896]{2,1,0:T(8,128)(2,1)S(1)}, u32[]{:S(2)}, u32[]{:S(2)}) collective-permute-start(bf16[2,63,896]{2,1,0:T(8,128)(2,1)S(1)} %slice.134), channel_id=1, source_target_pairs={{0,1},{1,2},{2,3},{4,5},{5,6},{6,7},{8,9},{9,10},{10,11},{12,13},{... | collective-permute-start | bytes 677384 | tf_op jit(solution)/shard_map/ppermute | solution.py:604
  289.2 3.0 multiply_reduce_fusion
  294.2 3.9 convolution_convert_fusion
  298.1 33.3 %self_attention_back.1 = (bf16[2,256,896]{2,1,0:T(8,128)(2,1)}, bf16[4,2,256,896]{3,2,1,0:T(8,128)(2,1)}, bf16[4,2,256,896]{3,2,1,0:T(8,128)(2,1)}, f32[14,4,8,512]{3,2,1,0:T(8,128)}) custom-call(s32[1]{0:T(128)} %bitcast.1.place_ref, bf16[2,256,896]{2,1,0:T(8,128)(2,1)} %bitcast.107, bf16[4,2,256,896]{3,2,1,0:T(8,128)(2,1)} %bitcast.98, ...), custom_call_target="tpu_custom_call" | custom-call | flops 18790481920 | bytes 40000000 | tf_op jit(solution)/shard_map/self_attention_back/pallas_call | solution.py:852
  331.4 7.2 %fusion.3 = f32[2048,896]{1,0:T(8,128)S(1)} fusion(bf16[2048,896]{1,0:T(8,128)(2,1)} %bitcast.110, bf16[7168,896]{1,0:T(8,128)(2,1)} %get-tuple-element.40), kind=kOutput, calls=%fused_computation.15 | convolution fusion | flops 3288334336 | bytes 12615680 | tf_op jit(solution)/shard_map/dot_general | solution.py:630
  338.6 6.1 %add_convert_fusion = bf16[2048,896]{1,0:T(8,128)(2,1)S(1)} fusion(f32[2048,896]{1,0:T(8,128)S(1)} %fusion.3, bf16[2048,896]{1,0:T(8,128)(2,1)S(1)} %bitcast.113, bf16[7168,896]{1,0:T(8,128)(2,1)} %get-tuple-element.40), kind=kOutput, calls=%fused_computation | convolution fusion | flops 3292004352 | bytes 16285696 | tf_op jit(solution)/shard_map/dot_general | solution.py:630
  347.2 7.4 %collective-permute-start.4 = (bf16[2,512,896]{2,1,0:T(8,128)(2,1)}, bf16[2,512,896]{2,1,0:T(8,128)(2,1)S(1)}, u32[]{:S(2)}, u32[]{:S(2)}) collective-permute-start(bf16[2,512,896]{2,1,0:T(8,128)(2,1)} %dynamic-slice_bitcast_fusion), channel_id=1, source_target_pairs={{0,1},{1,0},{2,3},{3,2},{4,5},{5,4},{6,7},{7,6},{8,9},{9,8},{10,11... | collective-permute-start | bytes 5505032 | tf_op jit(solution)/shard_map/ppermute | solution.py:617
  363.3 22.9 %projection_grads.1 = bf16[8,896,896]{2,1,0:T(8,128)(2,1)} custom-call(s32[10]{0:T(128)S(1)} %copy-done.21, bf16[2048,896]{1,0:T(8,128)(2,1)} %get-tuple-element.51.every_ref, bf16[2048,896]{1,0:T(8,128)(2,1)} %bitcast.111, bf16[2048,896]{1,0:T(8,128)(2,1)} %bitcast.112, bf16[512,896]{1,0:T(8,128)(2,1)S(1)} %copy-done.19, bf16[512,896]{1,0:T(8,128)(2,1)S(1)} %bitcast.74, ...), custom_call_target="tpu_custom_call" | custom-call | flops 9865003008 | bytes 40000000 | tf_op jit(solution)/shard_map/projection_grads/pallas_call | solution.py:476
  386.3 5.2 %collective-permute-done.5 = bf16[1,512,896]{2,1,0:T(8,128)(2,1)S(1)} collective-permute-done((bf16[1,512,896]{2,1,0:T(8,128)(2,1)S(1)}, bf16[1,512,896]{2,1,0:T(8,128)(2,1)S(1)}, u32[]{:S(2)}, u32[]{:S(2)}) %collective-permute-start.5) | collective-permute-done | bytes 917536 | tf_op jit(solution)/shard_map/ppermute | solution.py:617
  391.7 64.6 %last_steps.1 = (f32[224,896]{1,0:T(8,128)S(1)}, f32[64,128]{1,0:T(8,128)S(1)}, f32[512,896]{1,0:T(8,128)S(1)}) custom-call(bf16[7168,896]{1,0:T(8,128)(2,1)} %bitcast.90, bf16[512,896]{1,0:T(8,128)(2,1)S(1)} %bitcast.75, bf16[8,896,896]{2,1,0:T(8,128)(2,1)} %bitcast.88, f32[512,896]{1,0:T(8,128)S(1)} %add_bitcast_fusion.refs_3_, ...), custom_call_target="tpu_custom_call" | custom-call | tf_op jit(solution)/shard_map/last_steps/pallas_call | solution.py:586
  (139 shorter events, 45.9 us)
Async XLA Ops:
  7.2 91.8 %copy-start.28 = (s32[2,2]{1,0:T(2,128)S(1)}, s32[2,2]{1,0:T(2,128)}, u32[]{:S(2)}) copy-start(s32[2,2]{1,0:T(2,128)} %param.11) | copy-start | bytes 52
  7.2 4.2 copy-start.29
  7.2 94.0 %all-gather.6.cloned.1.call-start = ((), (), s32[]{:S(2)}) async-start(), calls=%async_computation.3 | async-start | bytes 4587520 | tf_op jit(solution)/shard_map/all_gather | solution.py:1183
  7.9 173.2 %all-gather.4.cloned.1.call-start = ((), (), s32[]{:S(2)}) async-start(), calls=%async_computation.1 | async-start | bytes 13246464 | tf_op jit(solution)/shard_map/all_gather | solution.py:1183
  8.7 449.0 %reduce-scatter.2.cloned.1.call-start = ((), (), s32[]{:S(2)}) async-start(), calls=%async_computation.2 | async-start | bytes 13246464 | tf_op jit(solution)/shard_map/reduce_scatter | solution.py:1246
  117.8 22.8 %copy-start.5 = (bf16[2,256,896]{2,1,0:T(8,128)(2,1)S(1)}, bf16[2,256,896]{2,1,0:T(8,128)(2,1)}, u32[]{:S(2)}) copy-start(bf16[2,256,896]{2,1,0:T(8,128)(2,1)} %param.9) | copy-start | bytes 2752516
  143.6 3.6 copy-start.24
  143.8 3.4 copy-start.13
  147.2 14.4 %collective-permute-start = (bf16[2,63,896]{2,1,0:T(8,128)(2,1)S(1)}, bf16[2,63,896]{2,1,0:T(8,128)(2,1)S(1)}, u32[]{:S(2)}, u32[]{:S(2)}) collective-permute-start(bf16[2,63,896]{2,1,0:T(8,128)(2,1)S(1)} %slice.126), channel_id=1, source_target_pairs={{1,0},{2,1},{3,2},{5,4},{6,5},{7,6},{9,8},{10,9},{11,10},{13,12},{... | collective-permute-start | bytes 677384 | tf_op jit(solution)/shard_map/ppermute | solution.py:604
  173.6 4.1 collective-permute-start.1
  181.1 28.4 %copy-start.2 = (f32[512,896]{1,0:T(8,128)}, f32[512,896]{1,0:T(8,128)S(1)}, u32[]{:S(2)}) copy-start(f32[512,896]{1,0:T(8,128)S(1)} %convolution_add_fusion.sum_ref) | copy-start | bytes 5505028
  233.0 6.3 %copy-start.4 = (bf16[2,256,896]{2,1,0:T(8,128)(2,1)S(1)}, bf16[2,256,896]{2,1,0:T(8,128)(2,1)}, u32[]{:S(2)}) copy-start(bf16[2,256,896]{2,1,0:T(8,128)(2,1)} %pad_maximum_fusion) | copy-start | bytes 2752516
  233.0 6.2 %collective-permute-start.2 = (bf16[2,63,896]{2,1,0:T(8,128)(2,1)S(1)}, bf16[2,63,896]{2,1,0:T(8,128)(2,1)S(1)}, u32[]{:S(2)}, u32[]{:S(2)}) collective-permute-start(bf16[2,63,896]{2,1,0:T(8,128)(2,1)S(1)} %slice.133), channel_id=1, source_target_pairs={{1,0},{2,1},{3,2},{5,4},{6,5},{7,6},{9,8},{10,9},{11,10},{13,12},{... | collective-permute-start | bytes 677384 | tf_op jit(solution)/shard_map/ppermute | solution.py:604
  272.9 15.9 %collective-permute-start.3 = (bf16[2,63,896]{2,1,0:T(8,128)(2,1)S(1)}, bf16[2,63,896]{2,1,0:T(8,128)(2,1)S(1)}, u32[]{:S(2)}, u32[]{:S(2)}) collective-permute-start(bf16[2,63,896]{2,1,0:T(8,128)(2,1)S(1)} %slice.134), channel_id=1, source_target_pairs={{0,1},{1,2},{2,3},{4,5},{5,6},{6,7},{8,9},{9,10},{10,11},{12,13},{... | collective-permute-start | bytes 677384 | tf_op jit(solution)/shard_map/ppermute | solution.py:604
  294.2 3.9 copy-start.9
  331.4 7.2 %copy-start.30 = (bf16[4,2,256,896]{3,2,1,0:T(8,128)(2,1)S(1)}, bf16[4,2,256,896]{3,2,1,0:T(8,128)(2,1)}, u32[]{:S(2)}) copy-start(bf16[4,2,256,896]{3,2,1,0:T(8,128)(2,1)} %get-tuple-element.57) | copy-start | bytes 11010052
  347.2 11.1 %collective-permute-start.4 = (bf16[2,512,896]{2,1,0:T(8,128)(2,1)}, bf16[2,512,896]{2,1,0:T(8,128)(2,1)S(1)}, u32[]{:S(2)}, u32[]{:S(2)}) collective-permute-start(bf16[2,512,896]{2,1,0:T(8,128)(2,1)} %dynamic-slice_bitcast_fusion), channel_id=1, source_target_pairs={{0,1},{1,0},{2,3},{3,2},{4,5},{5,4},{6,7},{7,6},{8,9},{9,8},{10,11... | collective-permute-start | bytes 5505032 | tf_op jit(solution)/shard_map/ppermute | solution.py:617
  358.3 5.0 %copy-start.14 = (bf16[512,896]{1,0:T(8,128)(2,1)S(1)}, bf16[512,896]{1,0:T(8,128)(2,1)}, u32[]{:S(2)}) copy-start(bf16[512,896]{1,0:T(8,128)(2,1)} %copy-done.13) | copy-start | bytes 2752516
  358.3 5.0 %copy-start.17 = (bf16[2,256,896]{2,1,0:T(8,128)(2,1)S(1)}, bf16[2,256,896]{2,1,0:T(8,128)(2,1)}, u32[]{:S(2)}) copy-start(bf16[2,256,896]{2,1,0:T(8,128)(2,1)} %get-tuple-element.59) | copy-start | bytes 2752516
  358.3 5.0 %copy-start.19 = (bf16[512,896]{1,0:T(8,128)(2,1)S(1)}, bf16[512,896]{1,0:T(8,128)(2,1)}, u32[]{:S(2)}) copy-start(bf16[512,896]{1,0:T(8,128)(2,1)} %get-tuple-element.58.l0) | copy-start | bytes 2752516
  358.3 5.0 %copy-start.20 = (bf16[2,256,896]{2,1,0:T(8,128)(2,1)S(1)}, bf16[2,256,896]{2,1,0:T(8,128)(2,1)}, u32[]{:S(2)}) copy-start(bf16[2,256,896]{2,1,0:T(8,128)(2,1)} %get-tuple-element.45) | copy-start | bytes 2752516
  360.6 30.9 %collective-permute-start.5 = (bf16[1,512,896]{2,1,0:T(8,128)(2,1)S(1)}, bf16[1,512,896]{2,1,0:T(8,128)(2,1)S(1)}, u32[]{:S(2)}, u32[]{:S(2)}) collective-permute-start(bf16[1,512,896]{2,1,0:T(8,128)(2,1)S(1)} %constant_dynamic-slice_fusion), channel_id=1, source_target_pairs={{0,2},{1,3},{2,0},{3,1},{4,6},{5,7},{6,4},{7,5},{8,10},{9,11},{10,... | collective-permute-start | bytes 2752520 | tf_op jit(solution)/shard_map/ppermute | solution.py:617
  386.2 5.4 %copy-start.6 = (bf16[2,256,896]{2,1,0:T(8,128)(2,1)S(1)}, bf16[2,256,896]{2,1,0:T(8,128)(2,1)}, u32[]{:S(2)}) copy-start(bf16[2,256,896]{2,1,0:T(8,128)(2,1)} %param.9) | copy-start | bytes 2752516
  386.3 5.4 %copy-start.18 = (f32[1,896]{1,0:T(1,128)S(1)}, f32[1,896]{1,0:T(1,128)}, u32[]{:S(2)}) copy-start(f32[1,896]{1,0:T(1,128)} %slice.98.gain_ref.refs_6_) | copy-start | bytes 10756
  (16 other events, 34.0 us)
Sparse Core Ops, SparseCore 0:
  9.6 53.9 all-gather.5
  66.5 98.1 all-gather.3
  211.4 164.4 reduce-scatter.1

commit v5 on v4

--- a/solution.py
+++ b/solution.py
@@ -493,6 +493,8 @@
 
 def last_steps(layout, sizes, matrix_grads, share, lines, grad_queries, query_matrix, joined, hidden, gain, grad_first):
     tokens, width = grad_queries.shape
+    cut = width // 256 * 128
+    windows = ((0, cut), (cut, width - cut))
     bits = lambda count: [1 << i for i in range(count.bit_length() - 1)]
     rounds = [("fsdp", step) for step in bits(sizes[1])] + [("dp", step) for step in bits(sizes[0])]
     given = [line for line in lines if line is not None]
@@ -516,13 +518,18 @@
                 ((dq_ref, q_buf), (m0_ref.at[0], m0), (in_ref, in_buf), (hid_ref, hid_buf), (gf_ref, first_buf))
             )
         ]
-        big = Reduction(place, mats_ref, row_tiles(share), (0, width), buffers)
+        pieces = [
+            Reduction(place, mats_ref, row_tiles(share), window, buffers[BUFFERS * i : BUFFERS * (i + 1)])
+            for i, window in enumerate(windows)
+        ]
         for i in range(place.nz):
-            big.open(i)
+            for piece_of in pieces:
+                piece_of.open(i)
             if i == 0:
                 for load in loads:
                     load.start()
-        actions = big.actions()
+        actions = [action for both in zip(*[piece_of.actions() for piece_of in pieces], strict=True) for action in both]
+        actions.pop(0)()
         actions.pop(0)()
         for load in loads:
             load.wait()
@@ -559,18 +566,22 @@
 
         for i in range(len(rounds)):
             line_out[i] = sum_ref[...]
+            if actions:
+                actions.pop(0)()
             round_copy(i).start()
-            for _ in range(2):
+            for _ in range(3):
                 if actions:
                     actions.pop(0)()
             round_copy(i).wait_recv()
             sum_ref[...] += line_in[i]
         for action in actions:
             action()
-        big.last(attn_ref)
+        for piece_of, window in zip(pieces, windows, strict=True):
+            piece_of.last(attn_ref.at[:, pl.ds(*window)])
         for i in range(len(rounds)):
             round_copy(i).wait_send()
-        big.drain()
+        for piece_of in pieces:
+            piece_of.drain()
 
     anywhere = pl.BlockSpec(memory_space=pl.ANY)
     inside = pl.BlockSpec(memory_space=pltpu.VMEM)
@@ -582,7 +593,8 @@
         pltpu.VMEM((len(rounds), held_rows, 128), F32), pltpu.VMEM((len(rounds), held_rows, 128), F32),
         dma((len(rounds),)), dma((len(rounds),)),
     ]
-    scratch += reduction_scratch(layout, block, BF16)
+    for window in windows:
+        scratch += reduction_scratch(layout, (share, window[1]), BF16)
     return pl.pallas_call(
         body,
         out_shape=[

time: 478 us -> 480 us (level)
  Pallas kernels: 341 us -> 346 us
    pallas_call x1, Pallas kernels: 64.6 us -> 69.6 us  [last_steps(): pl.pallas_call(body, out_shape=[jax.ShapeDtypeStruct(block, F32), jax.Sha...]
where the time goes in v5:
time: 480 us; the launch traced here: 474 us
  Pallas kernels  346 us (72%)
  matrix products  35.8 us (7%)
  starting transfers between devices  30.3 us (6%)
  local copies, waits for them, and re-layouts  23.4 us (5%)
  between operations  14.6 us (3%)
  other arithmetic  12 us (2%)
  waiting for transfers between devices  11.9 us (2%)
    pallas_call x1, Pallas kernels, gather_with_tiles(): pl.pallas_call(body, out_shape=[jax.ShapeDtypeStruct((n,) + block.shape i...  85.2 us
    pallas_call x1, Pallas kernels, last_steps(): pl.pallas_call(body, out_shape=[jax.ShapeDtypeStruct(block, F32), jax.Sha...  69.6 us
    pallas_call x1, Pallas kernels, self_attention_back(): pl.pallas_call(body, grid_spec=grid_spec, out_shape=[jax.ShapeDtypeStruct...  33.3 us
    pallas_call x1, Pallas kernels, span_attention_back(): pl.pallas_call(body, grid=(blocks,), in_specs=[q_spec, k_spec, k_spec, q_...  30.2 us
    pallas_call x1, Pallas kernels, feed_forward_grads(): pl.pallas_call(body, grid=(steps,), in_specs=[tall, line, tall, pl.BlockS...  26.5 us
    dot_general x5, matrix products, times_transposed(): lax.dot_general(left_side, right_side, (((1,), (1,)), ((), ())), preferre...  23.2 us
    pallas_call x1, Pallas kernels, projection_grads(): pl.pallas_call(body, grid_spec=pltpu.PrefetchScalarGridSpec(num_scalar_pr...  22.9 us
    pallas_call x1, Pallas kernels, self_attention(): pl.pallas_call(body, grid_spec=grid_spec, out_shape=[jax.ShapeDtypeStruct...  22.8 us
  transfers between devices with their start and end apart: 9, of which 3 were waited for; matrix products, arithmetic and copies ran while one was open for 12% of the time, Pallas kernels for 67%

profile of v5, /device:TPU:0, one launch (start us, length us, event | category | flops | bytes accessed | tf_op | source)
XLA Modules:
  0.0 473.5 jit_solution(13049070929157403391)
XLA Ops:
  12.0 85.2 %gather_all.1 = (bf16[7168,896]{1,0:T(8,128)(2,1)}, bf16[512,128]{1,0:T(8,128)(2,1)}, f32[14,5,256,256]{3,2,1,0:T(8,128)}) custom-call(bf16[224,896]{1,0:T(8,128)(2,1)} %refs_0_.1, bf16[16,128]{1,0:T(8,128)(2,1)} %pad_bitcast_fusion.refs_1_, f32[14,5,1,512]{3,2,1,0:T(1,128)} %copy.28.refs_2_), custom_call_target="tpu_custom_call" | custom-call | tf_op jit(solution)/shard_map/gather_all/pallas_call | solution.py:255
  101.2 16.6 %self_projection.1 = (bf16[512,896]{1,0:T(8,128)(2,1)}, bf16[2048,896]{1,0:T(8,128)(2,1)}, bf16[2048,896]{1,0:T(8,128)(2,1)}, bf16[2048,896]{1,0:T(8,128)(2,1)}, bf16[512,896]{1,0:T(8,128)(2,1)}) custom-call(s32[1]{0:T(128)} %bitcast.1.place_ref, bf16[2048,896]{1,0:T(8,128)(2,1)} %bitcast.101, f32[1,896]{1,0:T(1,128)} %slice.98.gain_ref.refs_6_, ...), custom_call_target="tpu_custom_call" | custom-call | flops 8220835840 | bytes 25000000 | tf_op jit(solution)/shard_map/self_projection/pallas_call | solution.py:1029
  117.8 22.8 %self_attention.1 = (bf16[2,256,896]{2,1,0:T(8,128)(2,1)}, f32[7,2,128,256]{3,2,1,0:T(8,128)}, f32[7,4,256]{2,1,0:T(4,128)}) custom-call(s32[1]{0:T(128)} %bitcast.1.place_ref, bf16[2,256,896]{2,1,0:T(8,128)(2,1)} %bitcast.106, bf16[4,2,256,896]{3,2,1,0:T(8,128)(2,1)} %bitcast.97, bf16[4,2,256,896]{3,2,1,0:T(8,128)(2,1)} %bitcast.99, ...), custom_call_target="tpu_custom_call" | custom-call | flops 7516192768 | bytes 30000000 | tf_op jit(solution)/shard_map/self_attention/pallas_call | solution.py:765
  140.5 3.0 multiply_reduce_fusion.2
  143.8 3.4 convolution_convert_fusion.2
  148.5 12.9 %span_projection.1 = (bf16[8,256,896]{2,1,0:T(8,128)(2,1)}, bf16[8,256,896]{2,1,0:T(8,128)(2,1)}) custom-call(bf16[8,256,896]{2,1,0:T(8,128)(2,1)} %bitcast.93, bf16[8,896,896]{2,1,0:T(8,128)(2,1)} %bitcast.84, bf16[8,896,896]{2,1,0:T(8,128)(2,1)} %bitcast.85), custom_call_target="tpu_custom_call" | custom-call | flops 6576668672 | bytes 15000000 | tf_op jit(solution)/shard_map/span_projection/pallas_call | solution.py:1057
  162.7 9.9 %span_attention.1 = bf16[8,64,896]{2,1,0:T(8,128)(2,1)} custom-call(bf16[8,64,896]{2,1,0:T(8,128)(2,1)} %bitcast.60, bf16[8,256,896]{2,1,0:T(8,128)(2,1)} %get-tuple-element.46.k_ref, bf16[8,256,896]{2,1,0:T(8,128)(2,1)} %get-tuple-element.47.v_ref), custom_call_target="tpu_custom_call" | custom-call | flops 1879048192 | bytes 12000000 | tf_op jit(solution)/shard_map/span_attention/pallas_call | solution.py:1107
  173.6 2.7 collective-permute-start.1
  177.9 3.2 convolution_add_fusion.sum_ref
  183.0 26.5 %feed_forward_grads.1 = (bf16[512,3584]{1,0:T(8,128)(2,1)S(1)}, bf16[512,3584]{1,0:T(8,128)(2,1)}, f32[7,4,128]{2,1,0:T(4,128)S(1)}, bf16[2,7,512,896]{3,2,1,0:T(8,128)(2,1)}) custom-call(f32[512,896]{1,0:T(8,128)S(1)} %convolution_add_fusion.sum_ref, f32[1,896]{1,0:T(1,128)S(1)} %slice.109.gain_ref, bf16[512,896]{1,0:T(8,128)(2,1)S(1)} %bitcast.72, ...), custom_call_target="tpu_custom_call" | custom-call | flops 13153337344 | bytes 40000000 | tf_op jit(solution)/shard_map/feed_forward_grads/pallas_call | solution.py:918
  214.1 15.8 %feed_forward_sums.1 = (bf16[512,896]{1,0:T(8,128)(2,1)}, f32[512,896]{1,0:T(8,128)S(1)}, f32[7,128]{1,0:T(8,128)S(1)}, f32[7,128]{1,0:T(8,128)S(1)}) custom-call(f32[512,896]{1,0:T(8,128)S(1)} %copy-done.3, f32[1,896]{1,0:T(1,128)S(1)} %slice.109.gain_ref, bf16[512,896]{1,0:T(8,128)(2,1)S(1)} %bitcast.73, ...), custom_call_target="tpu_custom_call" | custom-call | flops 6576668672 | bytes 25000000 | tf_op jit(solution)/shard_map/feed_forward_sums/pallas_call | solution.py:983
  230.0 3.0 convolution_convert_fusion.1
  234.6 4.6 collective-permute-done.2
  239.3 30.2 %span_attention_back.1 = (bf16[8,64,896]{2,1,0:T(8,128)(2,1)S(1)}, f32[8,256,896]{2,1,0:T(8,128)}, bf16[896,896]{1,0:T(8,128)(2,1)S(1)}, bf16[896,896]{1,0:T(8,128)(2,1)S(1)}) custom-call(bf16[8,64,896]{2,1,0:T(8,128)(2,1)S(1)} %bitcast.61, bf16[8,256,896]{2,1,0:T(8,128)(2,1)} %get-tuple-element.46.k_ref, bf16[8,256,896]{2,1,0:T(8,128)(2,1)} %get-tuple-element.47.v_ref, ...), custom_call_target="tpu_custom_call" | custom-call | flops 32883343360 | bytes 40000000 | tf_op jit(solution)/shard_map/span_attention_back/pallas_call | solution.py:1160
  272.9 14.6 %collective-permute-start.3 = (bf16[2,63,896]{2,1,0:T(8,128)(2,1)S(1)}, bf16[2,63,896]{2,1,0:T(8,128)(2,1)S(1)}, u32[]{:S(2)}, u32[]{:S(2)}) collective-permute-start(bf16[2,63,896]{2,1,0:T(8,128)(2,1)S(1)} %slice.134), channel_id=1, source_target_pairs={{0,1},{1,2},{2,3},{4,5},{5,6},{6,7},{8,9},{9,10},{10,11},{12,13},{... | collective-permute-start | bytes 677384 | tf_op jit(solution)/shard_map/ppermute | solution.py:616
  289.2 3.0 multiply_reduce_fusion
  294.2 3.9 convolution_convert_fusion
  298.1 33.3 %self_attention_back.1 = (bf16[2,256,896]{2,1,0:T(8,128)(2,1)}, bf16[4,2,256,896]{3,2,1,0:T(8,128)(2,1)}, bf16[4,2,256,896]{3,2,1,0:T(8,128)(2,1)}, f32[14,4,8,512]{3,2,1,0:T(8,128)}) custom-call(s32[1]{0:T(128)} %bitcast.1.place_ref, bf16[2,256,896]{2,1,0:T(8,128)(2,1)} %bitcast.107, bf16[4,2,256,896]{3,2,1,0:T(8,128)(2,1)} %bitcast.98, ...), custom_call_target="tpu_custom_call" | custom-call | flops 18790481920 | bytes 40000000 | tf_op jit(solution)/shard_map/self_attention_back/pallas_call | solution.py:864
  331.4 7.2 %fusion.3 = f32[2048,896]{1,0:T(8,128)S(1)} fusion(bf16[2048,896]{1,0:T(8,128)(2,1)} %bitcast.110, bf16[7168,896]{1,0:T(8,128)(2,1)} %get-tuple-element.40), kind=kOutput, calls=%fused_computation.15 | convolution fusion | flops 3288334336 | bytes 12615680 | tf_op jit(solution)/shard_map/dot_general | solution.py:642
  338.6 6.1 %add_convert_fusion = bf16[2048,896]{1,0:T(8,128)(2,1)S(1)} fusion(f32[2048,896]{1,0:T(8,128)S(1)} %fusion.3, bf16[2048,896]{1,0:T(8,128)(2,1)S(1)} %bitcast.113, bf16[7168,896]{1,0:T(8,128)(2,1)} %get-tuple-element.40), kind=kOutput, calls=%fused_computation | convolution fusion | flops 3292004352 | bytes 16285696 | tf_op jit(solution)/shard_map/dot_general | solution.py:642
  347.2 7.4 %collective-permute-start.4 = (bf16[2,512,896]{2,1,0:T(8,128)(2,1)}, bf16[2,512,896]{2,1,0:T(8,128)(2,1)S(1)}, u32[]{:S(2)}, u32[]{:S(2)}) collective-permute-start(bf16[2,512,896]{2,1,0:T(8,128)(2,1)} %dynamic-slice_bitcast_fusion), channel_id=1, source_target_pairs={{0,1},{1,0},{2,3},{3,2},{4,5},{5,4},{6,7},{7,6},{8,9},{9,8},{10,11... | collective-permute-start | bytes 5505032 | tf_op jit(solution)/shard_map/ppermute | solution.py:629
  363.3 22.9 %projection_grads.1 = bf16[8,896,896]{2,1,0:T(8,128)(2,1)} custom-call(s32[10]{0:T(128)S(1)} %copy-done.21, bf16[2048,896]{1,0:T(8,128)(2,1)} %get-tuple-element.51.every_ref, bf16[2048,896]{1,0:T(8,128)(2,1)} %bitcast.111, bf16[2048,896]{1,0:T(8,128)(2,1)} %bitcast.112, bf16[512,896]{1,0:T(8,128)(2,1)S(1)} %copy-done.19, bf16[512,896]{1,0:T(8,128)(2,1)S(1)} %bitcast.74, ...), custom_call_target="tpu_custom_call" | custom-call | flops 9865003008 | bytes 40000000 | tf_op jit(solution)/shard_map/projection_grads/pallas_call | solution.py:476
  386.3 5.2 %collective-permute-done.5 = bf16[1,512,896]{2,1,0:T(8,128)(2,1)S(1)} collective-permute-done((bf16[1,512,896]{2,1,0:T(8,128)(2,1)S(1)}, bf16[1,512,896]{2,1,0:T(8,128)(2,1)S(1)}, u32[]{:S(2)}, u32[]{:S(2)}) %collective-permute-start.5) | collective-permute-done | bytes 917536 | tf_op jit(solution)/shard_map/ppermute | solution.py:629
  391.7 69.6 %last_steps.1 = (f32[224,896]{1,0:T(8,128)S(1)}, f32[64,128]{1,0:T(8,128)S(1)}, f32[512,896]{1,0:T(8,128)S(1)}) custom-call(bf16[7168,896]{1,0:T(8,128)(2,1)} %bitcast.90, bf16[512,896]{1,0:T(8,128)(2,1)S(1)} %bitcast.75, bf16[8,896,896]{2,1,0:T(8,128)(2,1)} %bitcast.88, f32[512,896]{1,0:T(8,128)S(1)} %add_bitcast_fusion.refs_3_, ...), custom_call_target="tpu_custom_call" | custom-call | tf_op jit(solution)/shard_map/last_steps/pallas_call | solution.py:598
  (139 shorter events, 45.9 us)
Async XLA Ops:
  7.2 91.8 %copy-start.28 = (s32[2,2]{1,0:T(2,128)S(1)}, s32[2,2]{1,0:T(2,128)}, u32[]{:S(2)}) copy-start(s32[2,2]{1,0:T(2,128)} %param.11) | copy-start | bytes 52
  7.2 4.2 copy-start.29
  7.2 94.0 %all-gather.6.cloned.1.call-start = ((), (), s32[]{:S(2)}) async-start(), calls=%async_computation.3 | async-start | bytes 4587520 | tf_op jit(solution)/shard_map/all_gather | solution.py:1195
  7.9 173.2 %all-gather.4.cloned.1.call-start = ((), (), s32[]{:S(2)}) async-start(), calls=%async_computation.1 | async-start | bytes 13246464 | tf_op jit(solution)/shard_map/all_gather | solution.py:1195
  8.7 454.0 %reduce-scatter.2.cloned.1.call-start = ((), (), s32[]{:S(2)}) async-start(), calls=%async_computation.2 | async-start | bytes 13246464 | tf_op jit(solution)/shard_map/reduce_scatter | solution.py:1258
  117.8 22.8 %copy-start.5 = (bf16[2,256,896]{2,1,0:T(8,128)(2,1)S(1)}, bf16[2,256,896]{2,1,0:T(8,128)(2,1)}, u32[]{:S(2)}) copy-start(bf16[2,256,896]{2,1,0:T(8,128)(2,1)} %param.9) | copy-start | bytes 2752516
  143.6 3.6 copy-start.24
  143.8 3.4 copy-start.13
  147.2 14.4 %collective-permute-start = (bf16[2,63,896]{2,1,0:T(8,128)(2,1)S(1)}, bf16[2,63,896]{2,1,0:T(8,128)(2,1)S(1)}, u32[]{:S(2)}, u32[]{:S(2)}) collective-permute-start(bf16[2,63,896]{2,1,0:T(8,128)(2,1)S(1)} %slice.126), channel_id=1, source_target_pairs={{1,0},{2,1},{3,2},{5,4},{6,5},{7,6},{9,8},{10,9},{11,10},{13,12},{... | collective-permute-start | bytes 677384 | tf_op jit(solution)/shard_map/ppermute | solution.py:616
  173.6 4.1 collective-permute-start.1
  181.1 28.4 %copy-start.2 = (f32[512,896]{1,0:T(8,128)}, f32[512,896]{1,0:T(8,128)S(1)}, u32[]{:S(2)}) copy-start(f32[512,896]{1,0:T(8,128)S(1)} %convolution_add_fusion.sum_ref) | copy-start | bytes 5505028
  233.0 6.3 %copy-start.4 = (bf16[2,256,896]{2,1,0:T(8,128)(2,1)S(1)}, bf16[2,256,896]{2,1,0:T(8,128)(2,1)}, u32[]{:S(2)}) copy-start(bf16[2,256,896]{2,1,0:T(8,128)(2,1)} %pad_maximum_fusion) | copy-start | bytes 2752516
  233.0 6.2 %collective-permute-start.2 = (bf16[2,63,896]{2,1,0:T(8,128)(2,1)S(1)}, bf16[2,63,896]{2,1,0:T(8,128)(2,1)S(1)}, u32[]{:S(2)}, u32[]{:S(2)}) collective-permute-start(bf16[2,63,896]{2,1,0:T(8,128)(2,1)S(1)} %slice.133), channel_id=1, source_target_pairs={{1,0},{2,1},{3,2},{5,4},{6,5},{7,6},{9,8},{10,9},{11,10},{13,12},{... | collective-permute-start | bytes 677384 | tf_op jit(solution)/shard_map/ppermute | solution.py:616
  272.9 15.9 %collective-permute-start.3 = (bf16[2,63,896]{2,1,0:T(8,128)(2,1)S(1)}, bf16[2,63,896]{2,1,0:T(8,128)(2,1)S(1)}, u32[]{:S(2)}, u32[]{:S(2)}) collective-permute-start(bf16[2,63,896]{2,1,0:T(8,128)(2,1)S(1)} %slice.134), channel_id=1, source_target_pairs={{0,1},{1,2},{2,3},{4,5},{5,6},{6,7},{8,9},{9,10},{10,11},{12,13},{... | collective-permute-start | bytes 677384 | tf_op jit(solution)/shard_map/ppermute | solution.py:616
  294.2 3.9 copy-start.9
  331.4 7.2 %copy-start.30 = (bf16[4,2,256,896]{3,2,1,0:T(8,128)(2,1)S(1)}, bf16[4,2,256,896]{3,2,1,0:T(8,128)(2,1)}, u32[]{:S(2)}) copy-start(bf16[4,2,256,896]{3,2,1,0:T(8,128)(2,1)} %get-tuple-element.57) | copy-start | bytes 11010052
  347.2 11.1 %collective-permute-start.4 = (bf16[2,512,896]{2,1,0:T(8,128)(2,1)}, bf16[2,512,896]{2,1,0:T(8,128)(2,1)S(1)}, u32[]{:S(2)}, u32[]{:S(2)}) collective-permute-start(bf16[2,512,896]{2,1,0:T(8,128)(2,1)} %dynamic-slice_bitcast_fusion), channel_id=1, source_target_pairs={{0,1},{1,0},{2,3},{3,2},{4,5},{5,4},{6,7},{7,6},{8,9},{9,8},{10,11... | collective-permute-start | bytes 5505032 | tf_op jit(solution)/shard_map/ppermute | solution.py:629
  358.3 5.0 %copy-start.14 = (bf16[512,896]{1,0:T(8,128)(2,1)S(1)}, bf16[512,896]{1,0:T(8,128)(2,1)}, u32[]{:S(2)}) copy-start(bf16[512,896]{1,0:T(8,128)(2,1)} %copy-done.13) | copy-start | bytes 2752516
  358.3 5.0 %copy-start.17 = (bf16[2,256,896]{2,1,0:T(8,128)(2,1)S(1)}, bf16[2,256,896]{2,1,0:T(8,128)(2,1)}, u32[]{:S(2)}) copy-start(bf16[2,256,896]{2,1,0:T(8,128)(2,1)} %get-tuple-element.59) | copy-start | bytes 2752516
  358.3 5.0 %copy-start.19 = (bf16[512,896]{1,0:T(8,128)(2,1)S(1)}, bf16[512,896]{1,0:T(8,128)(2,1)}, u32[]{:S(2)}) copy-start(bf16[512,896]{1,0:T(8,128)(2,1)} %get-tuple-element.58.l0) | copy-start | bytes 2752516
  358.3 5.0 %copy-start.20 = (bf16[2,256,896]{2,1,0:T(8,128)(2,1)S(1)}, bf16[2,256,896]{2,1,0:T(8,128)(2,1)}, u32[]{:S(2)}) copy-start(bf16[2,256,896]{2,1,0:T(8,128)(2,1)} %get-tuple-element.45) | copy-start | bytes 2752516
  360.6 30.9 %collective-permute-start.5 = (bf16[1,512,896]{2,1,0:T(8,128)(2,1)S(1)}, bf16[1,512,896]{2,1,0:T(8,128)(2,1)S(1)}, u32[]{:S(2)}, u32[]{:S(2)}) collective-permute-start(bf16[1,512,896]{2,1,0:T(8,128)(2,1)S(1)} %constant_dynamic-slice_fusion), channel_id=1, source_target_pairs={{0,2},{1,3},{2,0},{3,1},{4,6},{5,7},{6,4},{7,5},{8,10},{9,11},{10,... | collective-permute-start | bytes 2752520 | tf_op jit(solution)/shard_map/ppermute | solution.py:629
  386.2 5.4 %copy-start.6 = (bf16[2,256,896]{2,1,0:T(8,128)(2,1)S(1)}, bf16[2,256,896]{2,1,0:T(8,128)(2,1)}, u32[]{:S(2)}) copy-start(bf16[2,256,896]{2,1,0:T(8,128)(2,1)} %param.9) | copy-start | bytes 2752516
  386.3 5.4 %copy-start.18 = (f32[1,896]{1,0:T(1,128)S(1)}, f32[1,896]{1,0:T(1,128)}, u32[]{:S(2)}) copy-start(f32[1,896]{1,0:T(1,128)} %slice.98.gain_ref.refs_6_) | copy-start | bytes 10756
  (16 other events, 34.0 us)
Sparse Core Ops, SparseCore 0:
  9.6 53.9 all-gather.5
  66.5 98.1 all-gather.3
  211.4 164.4 reduce-scatter.1
